TPU v7x, 256 devices: a whole 4x4x8 slice. The times are simulated.
256 devices in a mesh: dp: 64 (over z, x, core), tensor: 4 (over y).
Axes of the slice: x: 4, y: 4, z: 8, core: 2. Of those that a mesh axis runs over, the one named last changes fastest.
Arguments:
- attn_out: bfloat16 [65536, 8192], P('dp', 'tensor'), may hold values from -8 to 8, as said below
- grad_out: bfloat16 [65536, 2048], P('dp'), may hold values from -0.35327148 to 0.35327148, as said below
- grad_acc: float32 [2048, 8192], P('dp', 'tensor'), may hold values from -1060 to 1060, as said below
- master_weight: float32 [2048, 8192], P('dp', 'tensor'), may hold values from -60 to 60, as said below
- moment_m: float32 [2048, 8192], P('dp', 'tensor'), may hold values from -4 to 4
- moment_v: float32 [2048, 8192], P('dp', 'tensor'), may hold values from 0.001 to 0.01
Outputs:
- moment_new: float32 [2048, 8192], P('dp', 'tensor')
- second_new: float32 [2048, 8192], P('dp', 'tensor')
- scaled_step: float32 [2048, 8192], P('dp', 'tensor')
Inputs may be any that keep to these rules, and one draw needn't show every extreme that they name: `attn_out`: finite values. `grad_out`: finite values. `grad_acc`: finite values. `master_weight`: finite values.
All inputs are finite; a program needn't handle non-finite values.
Results may differ from a plain program's by a relative error of at most 0.0003.
Values sent between devices are 32-bit elements; how exact they have to be, the bound alone decides.
No kernel may reach another device: no remote copies, remote signals or barrier semaphores. Data moves between devices by JAX's collectives and lax.ppermute only.
A program may use at most 128 MiB of HBM per device.

v0:
```python
import jax
import jax.numpy as jnp
from jax import lax
from jax.sharding import PartitionSpec as P

beta_first = 0.9
beta_second = 0.999
weight_decay = 0.01
epsilon = 1e-06


def lamb_moments(gradient, divisor, weight, moment, second):
    clipped = gradient / divisor
    moment_new = beta_first * moment + (1.0 - beta_first) * clipped
    second_new = beta_second * second + (1.0 - beta_second) * clipped * clipped
    update = moment_new / (jnp.sqrt(second_new) + epsilon) + weight_decay * weight
    return (moment_new, second_new, update)


def shards(attn_out, grad_out, grad_acc, master_weight, moment_m, moment_v):
    entry_count = grad_out.shape[1] * attn_out.shape[1] * lax.axis_size("tensor")
    batch_grad = lax.psum_scatter(
        lax.dot_general(
            grad_out, attn_out, (((0,), (0,)), ((), ())), preferred_element_type=jnp.float32
        ),
        "dp",
        scatter_dimension=0,
        tiled=True,
    )
    gradient = grad_acc + batch_grad
    grad_whole, weight_whole, moment_whole, second_whole = (
        lax.all_to_all(gradient, "tensor", split_axis=0, concat_axis=1, tiled=True),
        lax.all_to_all(master_weight, "tensor", split_axis=0, concat_axis=1, tiled=True),
        lax.all_to_all(moment_m, "tensor", split_axis=0, concat_axis=1, tiled=True),
        lax.all_to_all(moment_v, "tensor", split_axis=0, concat_axis=1, tiled=True),
    )
    grad_energy = lax.psum(jnp.sum(grad_whole * grad_whole), ("dp", "tensor"))
    divisor = jnp.sqrt(grad_energy / entry_count + epsilon)
    moment_rows, second_rows, update = lamb_moments(
        grad_whole, divisor, weight_whole, moment_whole, second_whole
    )
    weight_norm = jnp.sqrt(jnp.sum(weight_whole * weight_whole, axis=1, keepdims=True))
    update_norm = jnp.sqrt(jnp.sum(update * update, axis=1, keepdims=True))
    step_rows = weight_norm / (update_norm + epsilon) * update
    moment_new, second_new, scaled_step = (
        lax.all_to_all(moment_rows, "tensor", split_axis=1, concat_axis=0, tiled=True),
        lax.all_to_all(second_rows, "tensor", split_axis=1, concat_axis=0, tiled=True),
        lax.all_to_all(step_rows, "tensor", split_axis=1, concat_axis=0, tiled=True),
    )
    return (moment_new, second_new, scaled_step)


def solution(mesh):
    in_specs = (
        P("dp", "tensor"),
        P("dp", None),
        P("dp", "tensor"),
        P("dp", "tensor"),
        P("dp", "tensor"),
        P("dp", "tensor"),
    )
    out_specs = (P("dp", "tensor"), P("dp", "tensor"), P("dp", "tensor"))
    return jax.shard_map(shards, mesh=mesh, in_specs=in_specs, out_specs=out_specs, check_vma=False)
```

profile of v0, /device:TPU:8, one launch (start us, length us, event | category | flops | bytes accessed | tf_op | source)
XLA Modules:
  0.0 344.2 jit_solution(4638704765077835054)
XLA Ops:
  7.2 0.0 reduce-scatter.2.cloned.1.call-start
  7.2 15.2 %fusion.4 = f32[2048,2048]{1,0:T(8,128)} fusion(bf16[1024,2048]{1,0:T(8,128)(2,1)} %param.7, bf16[1024,2048]{1,0:T(8,128)(2,1)} %param.6), kind=kOutput, calls=%fused_computation.12 | convolution fusion | flops 8589934592 | bytes 25165824 | tf_op jit(solution)/shard_map/dot_general | solution.py:23
  22.4 0.0 reduce-scatter.2.cloned.1.call-update
  22.4 0.9 copy-done.1
  23.3 9.9 %all_to_all.100 = f32[4,8,2048]{2,1,0:T(8,128)S(1)} all-to-all(f32[4,8,2048]{2,1,0:T(8,128)S(1)} %bitcast.35), channel_id=1, replica_groups=mesh['dp'=64,'tensor'=4] {'tensor'}, dimensions={0} | all-to-all | bytes 524288 | tf_op jit(solution)/shard_map/all_to_all | solution.py:33
  33.3 4.8 %all-to-all-start = ((f32[4,8,2048]{2,1,0:T(8,128)}), f32[4,8,2048]{2,1,0:T(8,128)S(1)}, u32[]{:S(2)}, u32[]{:S(2)}) async-start(f32[4,8,2048]{2,1,0:T(8,128)} %bitcast), calls=%async_computation | async-start | bytes 524288 | tf_op jit(solution)/shard_map/all_to_all | solution.py:34
  38.1 176.5 %reduce-scatter.2.cloned.1.call-done = f32[32,2048]{1,0:T(8,128)} async-done(((f32[2048,2048]{1,0:T(8,128)}), f32[32,2048]{1,0:T(8,128)}) %reduce-scatter.2.cloned.1.call-update) | async-done | bytes 262160 | tf_op jit(solution)/shard_map/reduce_scatter | solution.py:22
  214.6 1.0 add_bitcast_fusion
  215.6 0.0 all-to-all-done
  215.6 9.7 %all_to_all.101 = f32[4,8,2048]{2,1,0:T(8,128)S(1)} all-to-all(f32[4,8,2048]{2,1,0:T(8,128)S(1)} %add_bitcast_fusion), channel_id=1, replica_groups=mesh['dp'=64,'tensor'=4] {'tensor'}, dimensions={0} | all-to-all | bytes 524288 | tf_op jit(solution)/shard_map/all_to_all | solution.py:32
  225.3 4.8 %all-to-all-start.3 = ((f32[4,8,2048]{2,1,0:T(8,128)}), f32[4,8,2048]{2,1,0:T(8,128)S(1)}, u32[]{:S(2)}, u32[]{:S(2)}) async-start(f32[4,8,2048]{2,1,0:T(8,128)} %bitcast.6), calls=%async_computation.4 | async-start | bytes 524288 | tf_op jit(solution)/shard_map/all_to_all | solution.py:35
  230.2 0.7 multiply_reduce_fusion.2
  230.8 0.2 multiply_reduce_fusion.1
  231.0 73.7 %psum.7 = f32[]{:T(128)} all-reduce(f32[]{:T(128)} %multiply_reduce_fusion.2), channel_id=1, replica_groups=mesh['dp'=64,'tensor'=4] {'dp','tensor'}, use_global_device_ids=true, to_apply=%region_2.0 | all-reduce | flops 1 | bytes 8 | tf_op jit(solution)/shard_map/psum | solution.py:37
  305.5 0.0 all-to-all-done.3
  305.5 1.0 multiply_reduce_fusion
  306.5 0.1 broadcast_multiply_fusion
  306.6 9.5 %all_to_all.102 = f32[8,4,2048]{2,0,1:T(8,128)S(1)} all-to-all(f32[8,4,2048]{2,0,1:T(8,128)S(1)} %broadcast_multiply_fusion), channel_id=1, replica_groups=mesh['dp'=64,'tensor'=4] {'tensor'}, dimensions={1} | all-to-all | bytes 524288 | tf_op jit(solution)/shard_map/all_to_all | solution.py:48
  316.1 9.1 %all_to_all.103 = f32[8,4,2048]{2,0,1:T(8,128)S(1)} all-to-all(f32[8,4,2048]{2,0,1:T(8,128)S(1)} %get-tuple-element.5), channel_id=1, replica_groups=mesh['dp'=64,'tensor'=4] {'tensor'}, dimensions={1} | all-to-all | bytes 524288 | tf_op jit(solution)/shard_map/all_to_all | solution.py:47
  325.2 4.8 %all-to-all-start.2 = ((f32[8,4,2048]{2,0,1:T(8,128)}), f32[8,4,2048]{2,0,1:T(8,128)S(1)}, u32[]{:S(2)}, u32[]{:S(2)}) async-start(f32[8,4,2048]{2,0,1:T(8,128)} %get-tuple-element.6), calls=%async_computation.3 | async-start | bytes 524288 | tf_op jit(solution)/shard_map/all_to_all | solution.py:46
  330.0 5.2 %all-to-all-done.2 = f32[8,4,2048]{2,0,1:T(8,128)S(1)} async-done(((f32[8,4,2048]{2,0,1:T(8,128)}), f32[8,4,2048]{2,0,1:T(8,128)S(1)}, u32[]{:S(2)}, u32[]{:S(2)}) %all-to-all-start.2) | async-done | bytes 262176 | tf_op jit(solution)/shard_map/all_to_all | solution.py:46
  335.2 0.7 copy.12
  335.9 0.7 copy.13
  336.6 0.7 copy.14
  (4 shorter events, 0.0 us)
Async XLA Ops:
  7.2 207.5 %reduce-scatter.2.cloned.1.call-start = ((), (), s32[]{:S(2)}) async-start(), calls=%async_computation.8 | async-start | bytes 17039360 | tf_op jit(solution)/shard_map/reduce_scatter | solution.py:22
  22.4 0.9 copy-start.1
  22.4 192.2 %copy-start = (f32[32,2048]{1,0:T(8,128)S(1)}, f32[32,2048]{1,0:T(8,128)}, u32[]{:S(2)}) copy-start(f32[32,2048]{1,0:T(8,128)} %param.8) | copy-start | bytes 786436
  33.3 182.4 %all-to-all-start = ((f32[4,8,2048]{2,1,0:T(8,128)}), f32[4,8,2048]{2,1,0:T(8,128)S(1)}, u32[]{:S(2)}, u32[]{:S(2)}) async-start(f32[4,8,2048]{2,1,0:T(8,128)} %bitcast), calls=%async_computation | async-start | bytes 524288 | tf_op jit(solution)/shard_map/all_to_all | solution.py:34
  225.3 80.1 %all-to-all-start.3 = ((f32[4,8,2048]{2,1,0:T(8,128)}), f32[4,8,2048]{2,1,0:T(8,128)S(1)}, u32[]{:S(2)}, u32[]{:S(2)}) async-start(f32[4,8,2048]{2,1,0:T(8,128)} %bitcast.6), calls=%async_computation.4 | async-start | bytes 524288 | tf_op jit(solution)/shard_map/all_to_all | solution.py:35
  325.2 10.1 %all-to-all-start.2 = ((f32[8,4,2048]{2,0,1:T(8,128)}), f32[8,4,2048]{2,0,1:T(8,128)S(1)}, u32[]{:S(2)}, u32[]{:S(2)}) async-start(f32[8,4,2048]{2,0,1:T(8,128)} %get-tuple-element.6), calls=%async_computation.3 | async-start | bytes 524288 | tf_op jit(solution)/shard_map/all_to_all | solution.py:46
Sparse Core Ops, SparseCore 0:
  22.5 192.0 reduce-scatter.1
where the time goes:
time: 345 us; the launch traced here: 344 us
  waiting for transfers between devices  182 us (53%)
  blocking collectives  112 us (32%)
  matrix products  15.2 us (4%)
  between operations  14.8 us (4%)
  starting transfers between devices  14.5 us (4%)
    reduce_scatter x1, waiting for transfers between devices, shards(): lax.psum_scatter(lax.dot_general(grad_out, attn_out, (((0,), (0,)), ((),...  177 us
    psum x1, blocking collectives, shards(): grad_energy = lax.psum(jnp.sum(grad_whole * grad_whole), ('dp', 'tensor'))  73.7 us
    dot_general x1, matrix products, shards(): lax.dot_general(grad_out, attn_out, (((0,), (0,)), ((), ())), preferred_e...  15.2 us
    all_to_all x1, blocking collectives, shards(): lax.all_to_all(master_weight, 'tensor', split_axis=0, concat_axis=1, tile...  9.92 us
    all_to_all x1, blocking collectives, shards(): lax.all_to_all(gradient, 'tensor', split_axis=0, concat_axis=1, tiled=True)  9.71 us
    all_to_all x1, blocking collectives, shards(): lax.all_to_all(step_rows, 'tensor', split_axis=1, concat_axis=0, tiled=True)  9.55 us
    all_to_all x1, blocking collectives, shards(): lax.all_to_all(second_rows, 'tensor', split_axis=1, concat_axis=0, tiled=...  9.06 us
  transfers between devices with their start and end apart: 4, of which 2 were waited for; matrix products, arithmetic and copies ran while one was open for 1% of the time, Pallas kernels for 0%

commit v1 on v0

v1 whole, which is shorter than its diff:
```python
import functools

import jax
import jax.numpy as jnp
from jax import lax
from jax.experimental import pallas as pl
from jax.experimental.pallas import tpu as pltpu
from jax.sharding import Mesh, PartitionSpec as P

beta_first = 0.9
beta_second = 0.999
weight_decay = 0.01
epsilon = 1e-06

DP = ("z", "x", "c")
NZ, NX = 8, 4
SIZE = {"z": NZ, "x": NX}
COLS_Z = 1152


def dot(lhs_ref, rhs_ref, z, start, cols):
    lhs = lhs_ref[:, pl.ds(pl.multiple_of(z * 256, 256), 256)]
    rhs = rhs_ref[:, start : start + cols]
    return lax.dot_general(lhs, rhs, (((0,), (0,)), ((), ())), preferred_element_type=jnp.float32)


def near_x(x, c):
    s = 1 - 2 * c
    ahead = lax.rem(x + s + NX, NX)
    return [(ahead, c), (ahead, 1 - c), (lax.rem(x + 2, NX), c), (x, c)]


def product_z_kernel(hops, cols, where_ref, lhs_ref, rhs_ref, keep_ref, send_ref, acc):
    z, x, c = where_ref[0], where_ref[1], where_ref[2]
    s = 1 - 2 * c
    near, far = near_x(x, c), near_x(x, 1 - c)

    def put(ref, at, groups):
        for i, (gx, gc) in enumerate(groups):
            row = pl.multiple_of(gx * 64 + gc * 32, 32)
            ref[at + i] = acc[pl.ds(row, 32), :]

    at = 0
    for hop in hops:
        acc[...] = dot(lhs_ref, rhs_ref, lax.rem(z + s * hop + NZ, NZ), 0, cols)
        if hop in (0, NZ // 2):
            put(keep_ref, at, near)
            put(send_ref, at, far)
            at += 4
        else:
            put(keep_ref, at, near + far)
            acc[...] = dot(lhs_ref, rhs_ref, lax.rem(z - s * hop + NZ, NZ), 0, cols)
            put(send_ref, at, far + near)
            at += 8


def product_x_kernel(start, cols, where_ref, lhs_ref, rhs_ref, keep2_ref, send2_ref, keep_ref, send_ref, acc):
    z, x, c = where_ref[0], where_ref[1], where_ref[2]
    s = 1 - 2 * c
    ahead, behind, across = lax.rem(x + s + NX, NX), lax.rem(x - s + NX, NX), lax.rem(x + 2, NX)

    def rows(gx, gc):
        return acc[pl.ds(pl.multiple_of(gx * 64 + gc * 32, 32), 32), :]

    def put(slot, group, near):
        if near:
            keep_ref[slot] = rows(ahead, group)
            send_ref[8 + slot] = rows(behind, group)
            keep2_ref[slot] = rows(across, group)
            keep_ref[16 + slot] = rows(x, group)
        else:
            keep_ref[8 + slot] = rows(ahead, group)
            send_ref[slot] = rows(behind, group)
            send2_ref[slot] = rows(across, group)
            send_ref[16 + slot] = rows(x, group)

    @pl.loop(0, NZ)
    def _(t):
        acc[...] = dot(lhs_ref, rhs_ref, lax.rem(z + s * t + NZ, NZ), start, cols)

        @pl.when(jnp.logical_and(t > 0, t < 4))
        def _():
            put(2 * t - 2, c, True)
            put(2 * t - 1, 1 - c, True)

        @pl.when(t > 4)
        def _():
            put(14 - 2 * t, 1 - c, False)
            put(15 - 2 * t, c, False)

        @pl.when(jnp.logical_or(t == 0, t == 4))
        def _():
            slot = jnp.where(t == 4, 6, 7)
            put(slot, c, True)
            put(slot, 1 - c, False)


VMEM = pl.BlockSpec(memory_space=pltpu.VMEM)


def product(kernel, groups, cols, rows, where, grad_out, attn_out):
    return pl.pallas_call(
        kernel,
        in_specs=[pl.BlockSpec(memory_space=pltpu.SMEM), VMEM, VMEM],
        out_specs=[VMEM] * len(groups),
        out_shape=[jax.ShapeDtypeStruct((g, 32, cols), jnp.float32) for g in groups],
        scratch_shapes=[pltpu.VMEM((256, cols), jnp.float32)],
        compiler_params=pltpu.CompilerParams(vmem_limit_bytes=VLIM),
        cost_estimate=pl.CostEstimate(flops=COST * rows * cols, bytes_accessed=COST * rows, transcendentals=0),
    )(where, grad_out, attn_out)


VLIM = 24 << 20
COST = 1


def other_core(value):
    return lax.ppermute(value, "c", [(0, 1), (1, 0)])


def onward(value, axis):
    n = SIZE[axis]
    return lax.ppermute(value, (axis, "c"), [(2 * i + c, 2 * ((i + 1 - 2 * c) % n) + c) for i in range(n) for c in range(2)])


def at_front(part, whole):
    return lax.pad(part, jnp.float32(0), [(0, whole - part.shape[0], 0), (0, 0, 0), (0, 0, 0)])


def ring_sum(blocks, own, axis):
    moving = onward(blocks[0](), axis)
    for block in blocks[1:]:
        here = block()
        if moving.shape != here.shape:
            moving = at_front(moving, here.shape[0])
        moving = onward(here + moving, axis)
    half = moving.shape[0] // 2
    return moving[:half] + other_core(moving[half:]) + own()


def sum_over(tile, axes, n):
    copies = jnp.broadcast_to(tile[None], (n,) + tile.shape)
    return jnp.sum(lax.all_to_all(copies, axes, 0, 0, tiled=True), axis=0)


def after(value, *others):
    return lax.optimization_barrier((value,) + others)[0]


def shards(attn_out, grad_out, grad_acc, master_weight, moment_m, moment_v):
    entry_count = 2048 * 8192
    cols_x = attn_out.shape[1] - COLS_Z
    where = jnp.stack([lax.axis_index(a) for a in DP]).astype(jnp.int32)

    def product_z(where, hops):
        groups = sum(4 if hop in (0, NZ // 2) else 8 for hop in hops)
        return product(
            functools.partial(product_z_kernel, hops, COLS_Z), [groups] * 2, COLS_Z, groups * 64, where, grad_out, attn_out
        )

    def both(keep, send):
        got = other_core(send)
        return lambda lo=0, hi=None: keep[lo:hi] + got[lo:hi]

    pair4 = product_z(where, (4,))
    z4 = both(*pair4)
    pair3 = product_z(after(where, pair4[0]), (3,))
    z3 = both(*pair3)
    z4_there = lax.optimization_barrier(z4())
    keep2, send2, keep, send = product(
        functools.partial(product_x_kernel, COLS_Z, cols_x),
        [8, 8, 24, 24], cols_x, 2048, after(where, pair3[0], z4_there), grad_out, attn_out,
    )
    x2, x10 = both(keep2, send2), both(keep, send)
    pair2 = product_z(after(where, keep2), (2,))
    z2 = both(*pair2)
    x2_there = lax.optimization_barrier(x2())
    pair10 = product_z(after(where, pair2[0], x2_there), (1, 0))
    z10 = both(*pair10)

    sum_z = ring_sum([lambda: z4_there, z3, z2, lambda: z10(0, 8)], lambda: z10(8, 12), "z")
    sum_x = ring_sum([lambda: x2_there, lambda: x10(0, 16)], lambda: x10(16, 24), "x")
    batch_z = ring_sum([lambda: sum_z[2:3], lambda: sum_z[0:2]], lambda: sum_z[3:4], "x")
    batch_x = ring_sum(
        [lambda: sum_x[6:7], lambda: sum_x[4:6], lambda: sum_x[2:4], lambda: sum_x[0:2]], lambda: sum_x[7:8], "z"
    )
    gradient = grad_acc + jnp.concatenate([batch_z[0], batch_x[0]], axis=1)

    energy = jnp.sum((gradient * gradient).reshape(4, 8, 16, 128), axis=(0, 2))
    energy = sum_over(sum_over(energy, ("z", "x"), NZ * NX), ("c", "y"), 8)
    divisor = jnp.sqrt(jnp.sum(energy) / entry_count + epsilon)
    clipped = gradient / divisor
    moment_new = beta_first * moment_m + (1.0 - beta_first) * clipped
    second_new = beta_second * moment_v + (1.0 - beta_second) * clipped * clipped
    update = moment_new / (jnp.sqrt(second_new) + epsilon) + weight_decay * master_weight
    squares = jnp.stack([jnp.sum(master_weight * master_weight, axis=1), jnp.sum(update * update, axis=1)])
    norms = jnp.sqrt(lax.psum(squares, "y"))
    trust = norms[0] / (norms[1] + epsilon)
    return moment_new, second_new, trust[:, None] * update


def solution(mesh):
    fine = Mesh(mesh.devices.reshape(NZ, NX, 2, 4), DP + ("y",))
    split = P(DP, "y")
    return jax.shard_map(
        shards, mesh=fine, in_specs=(split, P(DP, None)) + (split,) * 4, out_specs=(split,) * 3, check_vma=False
    )
```

time: 345 us -> 148 us (0.43)
  waiting for transfers between devices: 182 us -> 69.1 us
  blocking collectives: 112 us -> 35.6 us
  Pallas kernels: 0 us -> 16.5 us
  matrix products: 15.2 us -> 0 us
  between operations: 14.8 us -> 1.68 us
    reduce_scatter x1 -> x0, waiting for transfers between devices: 177 us -> none  [shards(): lax.psum_scatter(lax.dot_general(grad_out, attn_out, (((0,), (0,)), ((),...]
    ppermute x0 -> x22, waiting for transfers between devices: none -> 69.1 us  [the longest x12 64.1 us: onward(): lax.ppermute(value, (axis, 'c'), [(2 * i + c, 2 * ((i + 1 - 2 * c) % n) +...]
    psum x1, blocking collectives: 73.7 us -> 9.1 us  [shards(): norms = jnp.sqrt(lax.psum(squares, 'y'))]
    pallas_call x0 -> x5, Pallas kernels: none -> 16.5 us  [product(): pl.pallas_call(kernel, in_specs=[pl.BlockSpec(memory_space=pltpu.SMEM), V...]
    ppermute x0 -> x22, starting transfers between devices: none -> 15.4 us  [the longest x12 7.87 us: onward(): lax.ppermute(value, (axis, 'c'), [(2 * i + c, 2 * ((i + 1 - 2 * c) % n) +...]
    dot_general x1 -> x0, matrix products: 15.2 us -> none  [shards(): lax.dot_general(grad_out, attn_out, (((0,), (0,)), ((), ())), preferred_e...]
    all_to_all x3 -> x0, starting transfers between devices: 14.5 us -> none  [the longest x1 4.84 us: shards(): lax.all_to_all(moment_m, 'tensor', split_axis=0, concat_axis=1, tiled=True)]
    all_to_all x4 -> x2, blocking collectives: 38.2 us -> 26.5 us  [sum_over(): return jnp.sum(lax.all_to_all(copies, axes, 0, 0, tiled=True), axis=0)]
  transfers between devices with their start and end apart: 4 -> 22, of which waited for: 2 -> 12; matrix products, arithmetic and copies ran while one was open for 1% -> 1% of each run, Pallas kernels for 0% -> 10%
where the time goes in v1:
time: 148 us; the launch traced here: 147 us
  waiting for transfers between devices  69.1 us (47%)
  blocking collectives  35.6 us (24%)
  Pallas kernels  16.5 us (11%)
  starting transfers between devices  15.4 us (10%)
  local copies, waits for them, and re-layouts  4.57 us (3%)
  other arithmetic  4.43 us (3%)
  between operations  1.68 us (1%)
    ppermute x12, waiting for transfers between devices, onward(): lax.ppermute(value, (axis, 'c'), [(2 * i + c, 2 * ((i + 1 - 2 * c) % n) +...  64.1 us
    all_to_all x2, blocking collectives, sum_over(): return jnp.sum(lax.all_to_all(copies, axes, 0, 0, tiled=True), axis=0)  26.5 us
    pallas_call x5, Pallas kernels, product(): pl.pallas_call(kernel, in_specs=[pl.BlockSpec(memory_space=pltpu.SMEM), V...  16.5 us
    psum x1, blocking collectives, shards(): norms = jnp.sqrt(lax.psum(squares, 'y'))  9.1 us
    ppermute x12, starting transfers between devices, onward(): lax.ppermute(value, (axis, 'c'), [(2 * i + c, 2 * ((i + 1 - 2 * c) % n) +...  7.87 us
    ppermute x10, starting transfers between devices, other_core(): return lax.ppermute(value, 'c', [(0, 1), (1, 0)])  7.57 us
    ppermute x10, waiting for transfers between devices, other_core(): return lax.ppermute(value, 'c', [(0, 1), (1, 0)])  5.05 us
    unnamed x12, local copies, waits for them, and re-layouts  4.4 us
  transfers between devices with their start and end apart: 22, of which 12 were waited for; matrix products, arithmetic and copies ran while one was open for 1% of the time, Pallas kernels for 10%

profile of v1, /device:TPU:8, one launch (start us, length us, event | category | flops | bytes accessed | tf_op | source)
XLA Modules:
  0.0 147.3 jit_solution(5341003891866437721)
XLA Ops:
  0.7 2.2 %copy-done = bf16[1024,2048]{1,0:T(8,128)(2,1)S(1)} copy-done((bf16[1024,2048]{1,0:T(8,128)(2,1)S(1)}, bf16[1024,2048]{1,0:T(8,128)(2,1)}, u32[]{:S(2)}) %copy-start) | copy-done | bytes 4194328
  2.9 2.2 %copy-done.1 = bf16[1024,2048]{1,0:T(8,128)(2,1)S(1)} copy-done((bf16[1024,2048]{1,0:T(8,128)(2,1)S(1)}, bf16[1024,2048]{1,0:T(8,128)(2,1)}, u32[]{:S(2)}) %copy-start.1) | copy-done | bytes 4194328
  6.7 2.3 %shard_map.86 = (f32[8,32,1152]{2,1,0:T(8,128)S(1)}, f32[8,32,1152]{2,1,0:T(8,128)S(1)}) custom-call(s32[3]{0:T(128)S(1)} %pad_add_fusion.1.where_ref, bf16[1024,2048]{1,0:T(8,128)(2,1)S(1)} %copy-done, bf16[1024,2048]{1,0:T(8,128)(2,1)S(1)} %copy-done.1), custom_call_target="tpu_custom_call" | custom-call | flops 589824 | bytes 512 | tf_op jit(solution)/shard_map/pallas_call | solution.py:102
  9.7 2.0 %collective-permute-start.5 = (f32[4,32,1152]{2,1,0:T(8,128)S(1)}, f32[4,32,1152]{2,1,0:T(8,128)S(1)}, u32[]{:S(2)}, u32[]{:S(2)}) collective-permute-start(f32[4,32,1152]{2,1,0:T(8,128)S(1)} %add.114), channel_id=1, source_target_pairs={{0,32},{4,228},{32,64},{36,4},{64,96},{68,36},{96,128},{100,68},{1... | collective-permute-start | bytes 1769480 | tf_op jit(solution)/shard_map/ppermute | solution.py:123
  11.7 7.3 %shard_map.87 = (f32[8,32,896]{2,1,0:T(8,128)S(1)}, f32[8,32,896]{2,1,0:T(8,128)S(1)}, f32[24,32,896]{2,1,0:T(8,128)S(1)}, f32[24,32,896]{2,1,0:T(8,128)S(1)}) custom-call(s32[3]{0:T(128)S(1)} %pad_add_fusion.1.where_ref, bf16[1024,2048]{1,0:T(8,128)(2,1)S(1)} %copy-done, bf16[1024,2048]{1,0:T(8,128)(2,1)S(1)} %copy-done.1), custom_call_target="tpu_custom_call" | custom-call | flops 1835008 | bytes 2048 | tf_op jit(solution)/shard_map/pallas_call | solution.py:102
  19.0 3.7 %collective-permute-start.13 = (f32[24,32,896]{2,1,0:T(8,128)S(1)}, f32[24,32,896]{2,1,0:T(8,128)S(1)}, u32[]{:S(2)}, u32[]{:S(2)}) collective-permute-start(f32[24,32,896]{2,1,0:T(8,128)S(1)} %get-tuple-element.34), channel_id=1, source_target_pairs={{0,4},{4,0},{1,5},{5,1},{2,6},{6,2},{3,7},{7,3},{8,12},{12,8},{9,1... | collective-permute-start | bytes 8257544 | tf_op jit(solution)/shard_map/ppermute | solution.py:118
  22.8 2.3 %shard_map.88 = (f32[8,32,1152]{2,1,0:T(8,128)S(1)}, f32[8,32,1152]{2,1,0:T(8,128)S(1)}) custom-call(s32[3]{0:T(128)S(1)} %pad_add_fusion.1.where_ref, bf16[1024,2048]{1,0:T(8,128)(2,1)S(1)} %copy-done, bf16[1024,2048]{1,0:T(8,128)(2,1)S(1)} %copy-done.1), custom_call_target="tpu_custom_call" | custom-call | flops 589824 | bytes 512 | tf_op jit(solution)/shard_map/pallas_call | solution.py:102
  26.7 3.8 %collective-permute-done.1 = f32[8,32,896]{2,1,0:T(8,128)S(1)} collective-permute-done((f32[8,32,896]{2,1,0:T(8,128)S(1)}, f32[8,32,896]{2,1,0:T(8,128)S(1)}, u32[]{:S(2)}, u32[]{:S(2)}) %collective-permute-start.1) | collective-permute-done | bytes 917536 | tf_op jit(solution)/shard_map/ppermute | solution.py:118
  30.6 1.8 %collective-permute-start.14 = (f32[8,32,896]{2,1,0:T(8,128)S(1)}, f32[8,32,896]{2,1,0:T(8,128)S(1)}, u32[]{:S(2)}, u32[]{:S(2)}) collective-permute-start(f32[8,32,896]{2,1,0:T(8,128)S(1)} %add.115), channel_id=1, source_target_pairs={{0,8},{4,28},{8,16},{12,4},{16,24},{20,12},{24,0},{28,20},{1,9},{5... | collective-permute-start | bytes 2752520 | tf_op jit(solution)/shard_map/ppermute | solution.py:123
  32.4 3.0 %shard_map.89 = (f32[12,32,1152]{2,1,0:T(8,128)S(1)}, f32[12,32,1152]{2,1,0:T(8,128)S(1)}) custom-call(s32[3]{0:T(128)S(1)} %pad_add_fusion.1.where_ref, bf16[1024,2048]{1,0:T(8,128)(2,1)S(1)} %copy-done, bf16[1024,2048]{1,0:T(8,128)(2,1)S(1)} %copy-done.1), custom_call_target="tpu_custom_call" | custom-call | flops 884736 | bytes 768 | tf_op jit(solution)/shard_map/pallas_call | solution.py:102
  36.9 6.0 %collective-permute-done.6 = f32[8,32,1152]{2,1,0:T(8,128)S(1)} collective-permute-done((f32[8,32,1152]{2,1,0:T(8,128)S(1)}, f32[8,32,1152]{2,1,0:T(8,128)S(1)}, u32[]{:S(2)}, u32[]{:S(2)}) %collective-permute-start.6) | collective-permute-done | bytes 1179680 | tf_op jit(solution)/shard_map/ppermute | solution.py:123
  43.2 2.3 %collective-permute-done.14 = f32[8,32,896]{2,1,0:T(8,128)S(1)} collective-permute-done((f32[8,32,896]{2,1,0:T(8,128)S(1)}, f32[8,32,896]{2,1,0:T(8,128)S(1)}, u32[]{:S(2)}, u32[]{:S(2)}) %collective-permute-start.14) | collective-permute-done | bytes 917536 | tf_op jit(solution)/shard_map/ppermute | solution.py:123
  46.2 14.4 %collective-permute-done.7 = f32[8,32,1152]{2,1,0:T(8,128)S(1)} collective-permute-done((f32[8,32,1152]{2,1,0:T(8,128)S(1)}, f32[8,32,1152]{2,1,0:T(8,128)S(1)}, u32[]{:S(2)}, u32[]{:S(2)}) %collective-permute-start.7) | collective-permute-done | bytes 1179680 | tf_op jit(solution)/shard_map/ppermute | solution.py:123
  60.9 9.5 %collective-permute-done.15 = f32[16,32,896]{2,1,0:T(8,128)S(1)} collective-permute-done((f32[16,32,896]{2,1,0:T(8,128)S(1)}, f32[16,32,896]{2,1,0:T(8,128)S(1)}, u32[]{:S(2)}, u32[]{:S(2)}) %collective-permute-start.15) | collective-permute-done | bytes 1835040 | tf_op jit(solution)/shard_map/ppermute | solution.py:123
  70.5 7.8 %collective-permute-done.8 = f32[8,32,1152]{2,1,0:T(8,128)S(1)} collective-permute-done((f32[8,32,1152]{2,1,0:T(8,128)S(1)}, f32[8,32,1152]{2,1,0:T(8,128)S(1)}, u32[]{:S(2)}, u32[]{:S(2)}) %collective-permute-start.8) | collective-permute-done | bytes 1179680 | tf_op jit(solution)/shard_map/ppermute | solution.py:123
  78.8 6.0 %collective-permute-done.17 = f32[1,32,896]{2,1,0:T(8,128)S(1)} collective-permute-done((f32[1,32,896]{2,1,0:T(8,128)S(1)}, f32[1,32,896]{2,1,0:T(8,128)S(1)}, u32[]{:S(2)}, u32[]{:S(2)}) %collective-permute-start.17) | collective-permute-done | bytes 114720 | tf_op jit(solution)/shard_map/ppermute | solution.py:123
  85.1 1.6 %collective-permute-start.10 = (f32[1,32,1152]{2,1,0:T(8,128)S(1)}, f32[1,32,1152]{2,1,0:T(8,128)S(1)}, u32[]{:S(2)}, u32[]{:S(2)}) collective-permute-start(f32[1,32,1152]{2,1,0:T(8,128)S(1)} %slice.109), channel_id=1, source_target_pairs={{0,8},{4,28},{8,16},{12,4},{16,24},{20,12},{24,0},{28,20},{1,9},{5... | collective-permute-start | bytes 442376 | tf_op jit(solution)/shard_map/ppermute | solution.py:123
  86.7 5.5 %collective-permute-done.18 = f32[2,32,896]{2,1,0:T(8,128)S(1)} collective-permute-done((f32[2,32,896]{2,1,0:T(8,128)S(1)}, f32[2,32,896]{2,1,0:T(8,128)S(1)}, u32[]{:S(2)}, u32[]{:S(2)}) %collective-permute-start.18) | collective-permute-done | bytes 229408 | tf_op jit(solution)/shard_map/ppermute | solution.py:123
  92.3 1.6 %collective-permute-start.11 = (f32[2,32,1152]{2,1,0:T(8,128)S(1)}, f32[2,32,1152]{2,1,0:T(8,128)S(1)}, u32[]{:S(2)}, u32[]{:S(2)}) collective-permute-start(f32[2,32,1152]{2,1,0:T(8,128)S(1)} %slice_add_fusion.6), channel_id=1, source_target_pairs={{0,8},{4,28},{8,16},{12,4},{16,24},{20,12},{24,0},{28,20},{1,9},{5... | collective-permute-start | bytes 884744 | tf_op jit(solution)/shard_map/ppermute | solution.py:123
  93.9 5.6 %collective-permute-done.19 = f32[2,32,896]{2,1,0:T(8,128)S(1)} collective-permute-done((f32[2,32,896]{2,1,0:T(8,128)S(1)}, f32[2,32,896]{2,1,0:T(8,128)S(1)}, u32[]{:S(2)}, u32[]{:S(2)}) %collective-permute-start.19) | collective-permute-done | bytes 229408 | tf_op jit(solution)/shard_map/ppermute | solution.py:123
  100.5 6.4 %collective-permute-done.20 = f32[2,32,896]{2,1,0:T(8,128)S(1)} collective-permute-done((f32[2,32,896]{2,1,0:T(8,128)S(1)}, f32[2,32,896]{2,1,0:T(8,128)S(1)}, u32[]{:S(2)}, u32[]{:S(2)}) %collective-permute-start.20) | collective-permute-done | bytes 229408 | tf_op jit(solution)/shard_map/ppermute | solution.py:123
  108.4 17.8 %all_to_all.10 = f32[32,8,128]{2,1,0:T(8,128)S(1)} all-to-all(f32[32,8,128]{2,1,0:T(8,128)S(1)} %broadcast_in_dim.4), channel_id=1, replica_groups=mesh['z'=8,'x'=4,'c'=2,'y'=4] {'z','x'}, dimensions={0} | all-to-all | bytes 262144 | tf_op jit(solution)/shard_map/all_to_all | solution.py:143
  126.3 8.7 %all_to_all.11 = f32[8,8,128]{2,1,0:T(8,128)S(1)} all-to-all(f32[8,8,128]{2,1,0:T(8,128)S(1)} %broadcast_in_dim.5), channel_id=1, replica_groups=mesh['z'=8,'x'=4,'c'=2,'y'=4] {'c','y'}, dimensions={0} | all-to-all | bytes 65536 | tf_op jit(solution)/shard_map/all_to_all | solution.py:143
  137.4 9.1 %psum.7 = f32[2,32]{1,0:T(2,128)S(1)} all-reduce(f32[2,32]{1,0:T(2,128)S(1)} %pad_maximum_fusion), channel_id=1, replica_groups=mesh['z'=8,'x'=4,'c'=2,'y'=4] {'y'}, use_global_device_ids=true, to_apply=%region_5.0 | all-reduce | flops 64 | bytes 512 | tf_op jit(solution)/shard_map/psum | solution.py:197
  (71 shorter events, 13.0 us)
Async XLA Ops:
  6.6 3.0 %collective-permute-start = (f32[4,32,1152]{2,1,0:T(8,128)S(1)}, f32[4,32,1152]{2,1,0:T(8,128)S(1)}, u32[]{:S(2)}, u32[]{:S(2)}) collective-permute-start(f32[4,32,1152]{2,1,0:T(8,128)S(1)} %get-tuple-element.22), channel_id=1, source_target_pairs={{0,4},{4,0},{1,5},{5,1},{2,6},{6,2},{3,7},{7,3},{8,12},{12,8},{9,1... | collective-permute-start | bytes 1769480 | tf_op jit(solution)/shard_map/ppermute | solution.py:118
  9.0 16.1 %collective-permute-start.4 = (f32[8,32,1152]{2,1,0:T(8,128)S(1)}, f32[8,32,1152]{2,1,0:T(8,128)S(1)}, u32[]{:S(2)}, u32[]{:S(2)}) collective-permute-start(f32[8,32,1152]{2,1,0:T(8,128)S(1)} %get-tuple-element.32), channel_id=1, source_target_pairs={{0,4},{4,0},{1,5},{5,1},{2,6},{6,2},{3,7},{7,3},{8,12},{12,8},{9,1... | collective-permute-start | bytes 3538952 | tf_op jit(solution)/shard_map/ppermute | solution.py:118
  9.7 15.5 %collective-permute-start.5 = (f32[4,32,1152]{2,1,0:T(8,128)S(1)}, f32[4,32,1152]{2,1,0:T(8,128)S(1)}, u32[]{:S(2)}, u32[]{:S(2)}) collective-permute-start(f32[4,32,1152]{2,1,0:T(8,128)S(1)} %add.114), channel_id=1, source_target_pairs={{0,32},{4,228},{32,64},{36,4},{64,96},{68,36},{96,128},{100,68},{1... | collective-permute-start | bytes 1769480 | tf_op jit(solution)/shard_map/ppermute | solution.py:123
  19.0 26.5 %collective-permute-start.13 = (f32[24,32,896]{2,1,0:T(8,128)S(1)}, f32[24,32,896]{2,1,0:T(8,128)S(1)}, u32[]{:S(2)}, u32[]{:S(2)}) collective-permute-start(f32[24,32,896]{2,1,0:T(8,128)S(1)} %get-tuple-element.34), channel_id=1, source_target_pairs={{0,4},{4,0},{1,5},{5,1},{2,6},{6,2},{3,7},{7,3},{8,12},{12,8},{9,1... | collective-permute-start | bytes 8257544 | tf_op jit(solution)/shard_map/ppermute | solution.py:118
  25.1 11.8 %collective-permute-start.3 = (f32[8,32,1152]{2,1,0:T(8,128)S(1)}, f32[8,32,1152]{2,1,0:T(8,128)S(1)}, u32[]{:S(2)}, u32[]{:S(2)}) collective-permute-start(f32[8,32,1152]{2,1,0:T(8,128)S(1)} %get-tuple-element.31), channel_id=1, source_target_pairs={{0,4},{4,0},{1,5},{5,1},{2,6},{6,2},{3,7},{7,3},{8,12},{12,8},{9,1... | collective-permute-start | bytes 3538952 | tf_op jit(solution)/shard_map/ppermute | solution.py:118
  25.4 17.5 %collective-permute-start.6 = (f32[8,32,1152]{2,1,0:T(8,128)S(1)}, f32[8,32,1152]{2,1,0:T(8,128)S(1)}, u32[]{:S(2)}, u32[]{:S(2)}) collective-permute-start(f32[8,32,1152]{2,1,0:T(8,128)S(1)} %pad_add_fusion), channel_id=1, source_target_pairs={{0,32},{4,228},{32,64},{36,4},{64,96},{68,36},{96,128},{100,68},{1... | collective-permute-start | bytes 3538952 | tf_op jit(solution)/shard_map/ppermute | solution.py:123
  25.5 5.0 %collective-permute-start.1 = (f32[8,32,896]{2,1,0:T(8,128)S(1)}, f32[8,32,896]{2,1,0:T(8,128)S(1)}, u32[]{:S(2)}, u32[]{:S(2)}) collective-permute-start(f32[8,32,896]{2,1,0:T(8,128)S(1)} %get-tuple-element.27), channel_id=1, source_target_pairs={{0,4},{4,0},{1,5},{5,1},{2,6},{6,2},{3,7},{7,3},{8,12},{12,8},{9,1... | collective-permute-start | bytes 2752520 | tf_op jit(solution)/shard_map/ppermute | solution.py:118
  30.6 14.9 %collective-permute-start.14 = (f32[8,32,896]{2,1,0:T(8,128)S(1)}, f32[8,32,896]{2,1,0:T(8,128)S(1)}, u32[]{:S(2)}, u32[]{:S(2)}) collective-permute-start(f32[8,32,896]{2,1,0:T(8,128)S(1)} %add.115), channel_id=1, source_target_pairs={{0,8},{4,28},{8,16},{12,4},{16,24},{20,12},{24,0},{28,20},{1,9},{5... | collective-permute-start | bytes 2752520 | tf_op jit(solution)/shard_map/ppermute | solution.py:123
  35.4 10.8 %collective-permute-start.2 = (f32[12,32,1152]{2,1,0:T(8,128)S(1)}, f32[12,32,1152]{2,1,0:T(8,128)S(1)}, u32[]{:S(2)}, u32[]{:S(2)}) collective-permute-start(f32[12,32,1152]{2,1,0:T(8,128)S(1)} %get-tuple-element.30), channel_id=1, source_target_pairs={{0,4},{4,0},{1,5},{5,1},{2,6},{6,2},{3,7},{7,3},{8,12},{12,8},{9,1... | collective-permute-start | bytes 5308424 | tf_op jit(solution)/shard_map/ppermute | solution.py:118
  43.1 17.5 %collective-permute-start.7 = (f32[8,32,1152]{2,1,0:T(8,128)S(1)}, f32[8,32,1152]{2,1,0:T(8,128)S(1)}, u32[]{:S(2)}, u32[]{:S(2)}) collective-permute-start(f32[8,32,1152]{2,1,0:T(8,128)S(1)} %add_add_fusion), channel_id=1, source_target_pairs={{0,32},{4,228},{32,64},{36,4},{64,96},{68,36},{96,128},{100,68},{1... | collective-permute-start | bytes 3538952 | tf_op jit(solution)/shard_map/ppermute | solution.py:123
  45.9 24.5 %collective-permute-start.15 = (f32[16,32,896]{2,1,0:T(8,128)S(1)}, f32[16,32,896]{2,1,0:T(8,128)S(1)}, u32[]{:S(2)}, u32[]{:S(2)}) collective-permute-start(f32[16,32,896]{2,1,0:T(8,128)S(1)} %fusion), channel_id=1, source_target_pairs={{0,8},{4,28},{8,16},{12,4},{16,24},{20,12},{24,0},{28,20},{1,9},{5... | collective-permute-start | bytes 5505032 | tf_op jit(solution)/shard_map/ppermute | solution.py:123
  60.8 17.5 %collective-permute-start.8 = (f32[8,32,1152]{2,1,0:T(8,128)S(1)}, f32[8,32,1152]{2,1,0:T(8,128)S(1)}, u32[]{:S(2)}, u32[]{:S(2)}) collective-permute-start(f32[8,32,1152]{2,1,0:T(8,128)S(1)} %fusion.1), channel_id=1, source_target_pairs={{0,32},{4,228},{32,64},{36,4},{64,96},{68,36},{96,128},{100,68},{1... | collective-permute-start | bytes 3538952 | tf_op jit(solution)/shard_map/ppermute | solution.py:123
  70.4 8.0 %collective-permute-start.16 = (f32[8,32,896]{2,1,0:T(8,128)S(1)}, f32[8,32,896]{2,1,0:T(8,128)S(1)}, u32[]{:S(2)}, u32[]{:S(2)}) collective-permute-start(f32[8,32,896]{2,1,0:T(8,128)S(1)} %slice.115), channel_id=1, source_target_pairs={{0,4},{4,0},{1,5},{5,1},{2,6},{6,2},{3,7},{7,3},{8,12},{12,8},{9,1... | collective-permute-start | bytes 2752520 | tf_op jit(solution)/shard_map/ppermute | solution.py:118
  78.3 6.6 %collective-permute-start.9 = (f32[4,32,1152]{2,1,0:T(8,128)S(1)}, f32[4,32,1152]{2,1,0:T(8,128)S(1)}, u32[]{:S(2)}, u32[]{:S(2)}) collective-permute-start(f32[4,32,1152]{2,1,0:T(8,128)S(1)} %slice.106), channel_id=1, source_target_pairs={{0,4},{4,0},{1,5},{5,1},{2,6},{6,2},{3,7},{7,3},{8,12},{12,8},{9,1... | collective-permute-start | bytes 1769480 | tf_op jit(solution)/shard_map/ppermute | solution.py:118
  78.7 6.1 %collective-permute-start.17 = (f32[1,32,896]{2,1,0:T(8,128)S(1)}, f32[1,32,896]{2,1,0:T(8,128)S(1)}, u32[]{:S(2)}, u32[]{:S(2)}) collective-permute-start(f32[1,32,896]{2,1,0:T(8,128)S(1)} %slice.120), channel_id=1, source_target_pairs={{0,32},{4,228},{32,64},{36,4},{64,96},{68,36},{96,128},{100,68},{1... | collective-permute-start | bytes 344072 | tf_op jit(solution)/shard_map/ppermute | solution.py:123
  84.8 7.3 %collective-permute-start.18 = (f32[2,32,896]{2,1,0:T(8,128)S(1)}, f32[2,32,896]{2,1,0:T(8,128)S(1)}, u32[]{:S(2)}, u32[]{:S(2)}) collective-permute-start(f32[2,32,896]{2,1,0:T(8,128)S(1)} %slice_add_fusion.7), channel_id=1, source_target_pairs={{0,32},{4,228},{32,64},{36,4},{64,96},{68,36},{96,128},{100,68},{1... | collective-permute-start | bytes 688136 | tf_op jit(solution)/shard_map/ppermute | solution.py:123
  85.1 7.2 %collective-permute-start.10 = (f32[1,32,1152]{2,1,0:T(8,128)S(1)}, f32[1,32,1152]{2,1,0:T(8,128)S(1)}, u32[]{:S(2)}, u32[]{:S(2)}) collective-permute-start(f32[1,32,1152]{2,1,0:T(8,128)S(1)} %slice.109), channel_id=1, source_target_pairs={{0,8},{4,28},{8,16},{12,4},{16,24},{20,12},{24,0},{28,20},{1,9},{5... | collective-permute-start | bytes 442376 | tf_op jit(solution)/shard_map/ppermute | solution.py:123
  92.2 7.3 %collective-permute-start.19 = (f32[2,32,896]{2,1,0:T(8,128)S(1)}, f32[2,32,896]{2,1,0:T(8,128)S(1)}, u32[]{:S(2)}, u32[]{:S(2)}) collective-permute-start(f32[2,32,896]{2,1,0:T(8,128)S(1)} %slice_add_fusion.8), channel_id=1, source_target_pairs={{0,32},{4,228},{32,64},{36,4},{64,96},{68,36},{96,128},{100,68},{1... | collective-permute-start | bytes 688136 | tf_op jit(solution)/shard_map/ppermute | solution.py:123
  92.3 8.0 %collective-permute-start.11 = (f32[2,32,1152]{2,1,0:T(8,128)S(1)}, f32[2,32,1152]{2,1,0:T(8,128)S(1)}, u32[]{:S(2)}, u32[]{:S(2)}) collective-permute-start(f32[2,32,1152]{2,1,0:T(8,128)S(1)} %slice_add_fusion.6), channel_id=1, source_target_pairs={{0,8},{4,28},{8,16},{12,4},{16,24},{20,12},{24,0},{28,20},{1,9},{5... | collective-permute-start | bytes 884744 | tf_op jit(solution)/shard_map/ppermute | solution.py:123
  99.5 7.3 %collective-permute-start.20 = (f32[2,32,896]{2,1,0:T(8,128)S(1)}, f32[2,32,896]{2,1,0:T(8,128)S(1)}, u32[]{:S(2)}, u32[]{:S(2)}) collective-permute-start(f32[2,32,896]{2,1,0:T(8,128)S(1)} %slice_add_fusion.9), channel_id=1, source_target_pairs={{0,32},{4,228},{32,64},{36,4},{64,96},{68,36},{96,128},{100,68},{1... | collective-permute-start | bytes 688136 | tf_op jit(solution)/shard_map/ppermute | solution.py:123
  100.4 6.6 %collective-permute-start.12 = (f32[1,32,1152]{2,1,0:T(8,128)S(1)}, f32[1,32,1152]{2,1,0:T(8,128)S(1)}, u32[]{:S(2)}, u32[]{:S(2)}) collective-permute-start(f32[1,32,1152]{2,1,0:T(8,128)S(1)} %slice.111), channel_id=1, source_target_pairs={{0,4},{4,0},{1,5},{5,1},{2,6},{6,2},{3,7},{7,3},{8,12},{12,8},{9,1... | collective-permute-start | bytes 442376 | tf_op jit(solution)/shard_map/ppermute | solution.py:118
  106.8 29.4 %copy-start.3 = (f32[32,2048]{1,0:T(8,128)S(1)}, f32[32,2048]{1,0:T(8,128)}, u32[]{:S(2)}) copy-start(f32[32,2048]{1,0:T(8,128)} %param.9) | copy-start | bytes 786436
  106.9 29.4 %copy-start.4 = (f32[32,2048]{1,0:T(8,128)S(1)}, f32[32,2048]{1,0:T(8,128)}, u32[]{:S(2)}) copy-start(f32[32,2048]{1,0:T(8,128)} %param.11) | copy-start | bytes 786436
  106.9 1.4 collective-permute-start.21
  (4 other events, 49.8 us)

commit v2 on v1

--- a/solution.py
+++ b/solution.py
@@ -15,7 +15,8 @@
 DP = ("z", "x", "c")
 NZ, NX = 8, 4
 SIZE = {"z": NZ, "x": NX}
-COLS_Z = 1152
+COLS_Z = 1280
+COLS_X = (512, 256)
 
 
 def dot(lhs_ref, rhs_ref, z, start, cols):
@@ -25,9 +26,7 @@
 
 
 def near_x(x, c):
-    s = 1 - 2 * c
-    ahead = lax.rem(x + s + NX, NX)
-    return [(ahead, c), (ahead, 1 - c), (lax.rem(x + 2, NX), c), (x, c)]
+    return [(lax.rem(x + k, NX), c) for k in range(NX)]
 
 
 def product_z_kernel(hops, cols, where_ref, lhs_ref, rhs_ref, keep_ref, send_ref, acc):
@@ -54,6 +53,23 @@
             at += 8
 
 
+def product_far_kernel(cols, where_ref, lhs_hbm, rhs_hbm, keep_ref, send_ref, acc, lhs, rhs, sems):
+    z, x, c = where_ref[0], where_ref[1], where_ref[2]
+    block = pl.multiple_of(lax.rem(z + NZ // 2, NZ) * 256, 256)
+    copies = [
+        pltpu.make_async_copy(lhs_hbm.at[:, pl.ds(block, 256)], lhs, sems.at[0]),
+        pltpu.make_async_copy(rhs_hbm.at[:, pl.ds(0, cols)], rhs, sems.at[1]),
+    ]
+    for copy in copies:
+        copy.start()
+    for copy in copies:
+        copy.wait()
+    acc[...] = lax.dot_general(lhs[...], rhs[...], (((0,), (0,)), ((), ())), preferred_element_type=jnp.float32)
+    for ref, core in ((keep_ref, c), (send_ref, 1 - c)):
+        for i, (gx, gc) in enumerate(near_x(x, core)):
+            ref[i] = acc[pl.ds(pl.multiple_of(gx * 64 + gc * 32, 32), 32), :]
+
+
 def product_x_kernel(start, cols, where_ref, lhs_ref, rhs_ref, keep2_ref, send2_ref, keep_ref, send_ref, acc):
     z, x, c = where_ref[0], where_ref[1], where_ref[2]
     s = 1 - 2 * c
@@ -110,6 +126,24 @@
     )(where, grad_out, attn_out)
 
 
+def product_far(where, grad_out, attn_out):
+    tokens, hbm = attn_out.shape[0], pl.BlockSpec(memory_space=pltpu.HBM)
+    return pl.pallas_call(
+        functools.partial(product_far_kernel, COLS_Z),
+        in_specs=[pl.BlockSpec(memory_space=pltpu.SMEM), hbm, hbm],
+        out_specs=[VMEM] * 2,
+        out_shape=[jax.ShapeDtypeStruct((4, 32, COLS_Z), jnp.float32)] * 2,
+        scratch_shapes=[
+            pltpu.VMEM((256, COLS_Z), jnp.float32),
+            pltpu.VMEM((tokens, 256), jnp.bfloat16),
+            pltpu.VMEM((tokens, COLS_Z), jnp.bfloat16),
+            pltpu.SemaphoreType.DMA((2,)),
+        ],
+        compiler_params=pltpu.CompilerParams(vmem_limit_bytes=VLIM),
+        cost_estimate=pl.CostEstimate(flops=COST * 256 * COLS_Z, bytes_accessed=COST * 256, transcendentals=0),
+    )(where, grad_out, attn_out)
+
+
 VLIM = 24 << 20
 COST = 1
 
@@ -123,19 +157,13 @@
     return lax.ppermute(value, (axis, "c"), [(2 * i + c, 2 * ((i + 1 - 2 * c) % n) + c) for i in range(n) for c in range(2)])
 
 
+def shift(value, axis, by):
+    n = SIZE[axis]
+    return lax.ppermute(value, axis, [(i, (i + by) % n) for i in range(n)])
+
+
 def at_front(part, whole):
     return lax.pad(part, jnp.float32(0), [(0, whole - part.shape[0], 0), (0, 0, 0), (0, 0, 0)])
-
-
-def ring_sum(blocks, own, axis):
-    moving = onward(blocks[0](), axis)
-    for block in blocks[1:]:
-        here = block()
-        if moving.shape != here.shape:
-            moving = at_front(moving, here.shape[0])
-        moving = onward(here + moving, axis)
-    half = moving.shape[0] // 2
-    return moving[:half] + other_core(moving[half:]) + own()
 
 
 def sum_over(tile, axes, n):
@@ -144,12 +172,16 @@
 
 
 def after(value, *others):
-    return lax.optimization_barrier((value,) + others)[0]
+    return lax.optimization_barrier((value, others))[0]
+
+
+def halves(cols):
+    middle = cols // 256 * 128
+    return slice(0, middle), slice(middle, cols)
 
 
 def shards(attn_out, grad_out, grad_acc, master_weight, moment_m, moment_v):
     entry_count = 2048 * 8192
-    cols_x = attn_out.shape[1] - COLS_Z
     where = jnp.stack([lax.axis_index(a) for a in DP]).astype(jnp.int32)
 
     def product_z(where, hops):
@@ -158,33 +190,69 @@
             functools.partial(product_z_kernel, hops, COLS_Z), [groups] * 2, COLS_Z, groups * 64, where, grad_out, attn_out
         )
 
-    def both(keep, send):
-        got = other_core(send)
-        return lambda lo=0, hi=None: keep[lo:hi] + got[lo:hi]
-
-    pair4 = product_z(where, (4,))
-    z4 = both(*pair4)
-    pair3 = product_z(after(where, pair4[0]), (3,))
-    z3 = both(*pair3)
-    z4_there = lax.optimization_barrier(z4())
-    keep2, send2, keep, send = product(
-        functools.partial(product_x_kernel, COLS_Z, cols_x),
-        [8, 8, 24, 24], cols_x, 2048, after(where, pair3[0], z4_there), grad_out, attn_out,
+    def both(pair):
+        return pair[0] + pair[1]
+
+    cuts_z = halves(COLS_Z)
+    starts_x = (COLS_Z, COLS_Z + COLS_X[0])
+
+    def product_x(where, i):
+        return product(
+            functools.partial(product_x_kernel, starts_x[i], COLS_X[i]),
+            [8, 8, 24, 24], COLS_X[i], 2048, where, grad_out, attn_out,
+        )
+
+    def add(here, moving):
+        return here + (moving if moving.shape == here.shape else at_front(moving, here.shape[0]))
+
+    far_z = product_far(where, grad_out, attn_out)
+    far_z = (far_z[0], other_core(far_z[1]))
+    pair3 = product_z(after(where, far_z[0]), (3,))
+    pair3 = (pair3[0], other_core(pair3[1]))
+    first_z = lax.optimization_barrier(both(far_z))
+    z = onward(first_z, "z")
+    keep_far, send_far, keep_xa, send_xa = product_x(after(where, pair3[0], first_z), 0)
+    far_xa = (keep_far, other_core(send_far))
+    z = [z[..., cut] for cut in cuts_z]
+    keep_far, send_far, keep_xb, send_xb = product_x(after(where, z, far_xa[1]), 1)
+    far_xb = (keep_far, other_core(send_far))
+
+    def hop_z(z, pair, rows):
+        a = add(both(pair)[:rows, :, cuts_z[0]], z[0])
+        b = add(both(pair)[:rows, :, cuts_z[1]], after(z[1], a))
+        return (a, b), [onward(a, "z"), onward(b, "z")]
+
+    step, z = hop_z(z, pair3, 8)
+    pair2 = product_z(after(where, step, keep_xb), (2,))
+    pair2 = (pair2[0], other_core(pair2[1]))
+    first_xa = lax.optimization_barrier(both(far_xa))
+    first_xb = after(both(far_xb), first_xa)
+    x = [onward(first_xa, "x"), onward(first_xb, "x")]
+    pair_xa = (keep_xa, other_core(after(send_xa, first_xa)))
+    pair_xb = (keep_xb, other_core(after(send_xb, first_xb, pair_xa[1])))
+    pair1 = product_z(after(where, z, first_xb), (1, 0))
+    pair1 = (pair1[0], other_core(pair1[1]))
+    step, z = hop_z(z, pair2, 8)
+    a = add(both(pair_xa)[:16], x[0])
+    b = add(both(pair_xb)[:16], after(x[1], a))
+    x = [onward(a, "x"), onward(b, "x")]
+    step, z = hop_z(z, pair1, 8)
+
+    def swapped(parts, rows):
+        return [part[:rows] + other_core(part[rows:]) for part in parts]
+
+    sum_z = jnp.concatenate(swapped(z, 4), axis=2) + both(pair1)[8:12]
+    sum_x = jnp.concatenate(
+        [part + both(pair)[16:24] for part, pair in zip(swapped(x, 8), (pair_xa, pair_xb))], axis=2
     )
-    x2, x10 = both(keep2, send2), both(keep, send)
-    pair2 = product_z(after(where, keep2), (2,))
-    z2 = both(*pair2)
-    x2_there = lax.optimization_barrier(x2())
-    pair10 = product_z(after(where, pair2[0], x2_there), (1, 0))
-    z10 = both(*pair10)
-
-    sum_z = ring_sum([lambda: z4_there, z3, z2, lambda: z10(0, 8)], lambda: z10(8, 12), "z")
-    sum_x = ring_sum([lambda: x2_there, lambda: x10(0, 16)], lambda: x10(16, 24), "x")
-    batch_z = ring_sum([lambda: sum_z[2:3], lambda: sum_z[0:2]], lambda: sum_z[3:4], "x")
-    batch_x = ring_sum(
-        [lambda: sum_x[6:7], lambda: sum_x[4:6], lambda: sum_x[2:4], lambda: sum_x[0:2]], lambda: sum_x[7:8], "z"
-    )
-    gradient = grad_acc + jnp.concatenate([batch_z[0], batch_x[0]], axis=1)
+
+    batch_z = sum_z[0] + sum(shift(sum_z[k], "x", k) for k in (1, 2, 3))
+    moving = onward(sum_x[6:7], "z")
+    moving = onward(sum_x[4:6] + at_front(moving, 2), "z")
+    moving = onward(sum_x[2:4] + moving, "z")
+    moving = onward(sum_x[0:2] + moving, "z")
+    batch_x = moving[0] + other_core(moving[1]) + sum_x[7]
+    gradient = grad_acc + jnp.concatenate([batch_z, batch_x], axis=1)
 
     energy = jnp.sum((gradient * gradient).reshape(4, 8, 16, 128), axis=(0, 2))
     energy = sum_over(sum_over(energy, ("z", "x"), NZ * NX), ("c", "y"), 8)

time: 148 us -> 158 us (1.068)
  starting transfers between devices: 15.4 us -> 28.4 us
  waiting for transfers between devices: 69.1 us -> 65.4 us
  Pallas kernels: 16.5 us -> 18.5 us
    ppermute x12 -> x15, waiting for transfers between devices: 64.1 us -> 58.4 us  [onward(): lax.ppermute(value, (axis, 'c'), [(2 * i + c, 2 * ((i + 1 - 2 * c) % n) +...]
    ppermute x12 -> x15, starting transfers between devices: 7.87 us -> 12.9 us  [onward(): lax.ppermute(value, (axis, 'c'), [(2 * i + c, 2 * ((i + 1 - 2 * c) % n) +...]
    ppermute x0 -> x3, waiting for transfers between devices: none -> 4.1 us  [shift(): return lax.ppermute(value, axis, [(i, (i + by) % n) for i in range(n)])]
    ppermute x10 -> x13, starting transfers between devices: 7.57 us -> 11.6 us  [other_core(): return lax.ppermute(value, 'c', [(0, 1), (1, 0)])]
    ppermute x0 -> x3, starting transfers between devices: none -> 3.94 us  [shift(): return lax.ppermute(value, axis, [(i, (i + by) % n) for i in range(n)])]
    ppermute x10 -> x13, waiting for transfers between devices: 5.05 us -> 2.91 us  [other_core(): return lax.ppermute(value, 'c', [(0, 1), (1, 0)])]
    pallas_call x0 -> x1, Pallas kernels: none -> 1.99 us  [product_far(): pl.pallas_call(functools.partial(product_far_kernel, COLS_Z), in_specs=[p...]
  transfers between devices with their start and end apart: 22 -> 31, of which waited for: 12 -> 13; matrix products, arithmetic and copies ran while one was open for 1% -> 2% of each run, Pallas kernels for 10% -> 10%
where the time goes in v2:
time: 158 us
  waiting for transfers between devices  65.4 us (41%)
  blocking collectives  34.4 us (22%)
  starting transfers between devices  28.4 us (18%)
  Pallas kernels  18.5 us (12%)
  other arithmetic  5.2 us (3%)
  local copies, waits for them, and re-layouts  4.61 us (3%)
  between operations  1.76 us (1%)
    ppermute x15, waiting for transfers between devices, onward(): lax.ppermute(value, (axis, 'c'), [(2 * i + c, 2 * ((i + 1 - 2 * c) % n) +...  58.4 us
    all_to_all x2, blocking collectives, sum_over(): return jnp.sum(lax.all_to_all(copies, axes, 0, 0, tiled=True), axis=0)  25.3 us
    pallas_call x5, Pallas kernels, product(): pl.pallas_call(kernel, in_specs=[pl.BlockSpec(memory_space=pltpu.SMEM), V...  16.5 us
    ppermute x15, starting transfers between devices, onward(): lax.ppermute(value, (axis, 'c'), [(2 * i + c, 2 * ((i + 1 - 2 * c) % n) +...  12.9 us
    ppermute x13, starting transfers between devices, other_core(): return lax.ppermute(value, 'c', [(0, 1), (1, 0)])  11.6 us
    psum x1, blocking collectives, shards(): norms = jnp.sqrt(lax.psum(squares, 'y'))  9.1 us
    unnamed x12, local copies, waits for them, and re-layouts  4.4 us
    ppermute x3, waiting for transfers between devices, shift(): return lax.ppermute(value, axis, [(i, (i + by) % n) for i in range(n)])  4.1 us
  transfers between devices with their start and end apart: 31, of which 13 were waited for; matrix products, arithmetic and copies ran while one was open for 2% of the time, Pallas kernels for 10%

profile of v2, /device:TPU:8, one launch (start us, length us, event | category | flops | bytes accessed | tf_op | source)
XLA Modules:
  0.0 158.2 jit_solution(9259799641647720232)
XLA Ops:
  0.7 2.2 %copy-done = bf16[1024,2048]{1,0:T(8,128)(2,1)S(1)} copy-done((bf16[1024,2048]{1,0:T(8,128)(2,1)S(1)}, bf16[1024,2048]{1,0:T(8,128)(2,1)}, u32[]{:S(2)}) %copy-start) | copy-done | bytes 4194328
  2.9 2.2 %copy-done.1 = bf16[1024,2048]{1,0:T(8,128)(2,1)S(1)} copy-done((bf16[1024,2048]{1,0:T(8,128)(2,1)S(1)}, bf16[1024,2048]{1,0:T(8,128)(2,1)}, u32[]{:S(2)}) %copy-start.1) | copy-done | bytes 4194328
  5.1 2.0 %shard_map.85 = (f32[4,32,1280]{2,1,0:T(8,128)S(1)}, f32[4,32,1280]{2,1,0:T(8,128)S(1)}) custom-call(s32[3]{0:T(128)S(1)} %pad_add_fusion.where_ref, bf16[1024,2048]{1,0:T(8,128)(2,1)S(1)} %copy-done, bf16[1024,2048]{1,0:T(8,128)(2,1)S(1)} %copy-done.1), custom_call_target="tpu_custom_call" | custom-call | flops 327680 | bytes 256 | tf_op jit(solution)/shard_map/pallas_call | solution.py:131
  7.2 2.3 %shard_map.86 = (f32[8,32,1280]{2,1,0:T(8,128)S(1)}, f32[8,32,1280]{2,1,0:T(8,128)S(1)}) custom-call(s32[3]{0:T(128)S(1)} %pad_add_fusion.where_ref, bf16[1024,2048]{1,0:T(8,128)(2,1)S(1)} %copy-done, bf16[1024,2048]{1,0:T(8,128)(2,1)S(1)} %copy-done.1), custom_call_target="tpu_custom_call" | custom-call | flops 655360 | bytes 512 | tf_op jit(solution)/shard_map/pallas_call | solution.py:118
  10.2 2.0 %collective-permute-start.2 = (f32[4,32,1280]{2,1,0:T(8,128)S(1)}, f32[4,32,1280]{2,1,0:T(8,128)S(1)}, u32[]{:S(2)}, u32[]{:S(2)}) collective-permute-start(f32[4,32,1280]{2,1,0:T(8,128)S(1)} %add.144), channel_id=1, source_target_pairs={{0,32},{4,228},{32,64},{36,4},{64,96},{68,36},{96,128},{100,68},{1... | collective-permute-start | bytes 1966088 | tf_op jit(solution)/shard_map/ppermute | solution.py:157
  12.1 4.9 %shard_map.87 = (f32[8,32,512]{2,1,0:T(8,128)S(1)}, f32[8,32,512]{2,1,0:T(8,128)S(1)}, f32[24,32,512]{2,1,0:T(8,128)S(1)}, f32[24,32,512]{2,1,0:T(8,128)S(1)}) custom-call(s32[3]{0:T(128)S(1)} %pad_add_fusion.where_ref, bf16[1024,2048]{1,0:T(8,128)(2,1)S(1)} %copy-done, bf16[1024,2048]{1,0:T(8,128)(2,1)S(1)} %copy-done.1), custom_call_target="tpu_custom_call" | custom-call | flops 1048576 | bytes 2048 | tf_op jit(solution)/shard_map/pallas_call | solution.py:118
  17.0 3.8 %collective-permute-start.5 = (f32[8,32,512]{2,1,0:T(8,128)S(1)}, f32[8,32,512]{2,1,0:T(8,128)S(1)}, u32[]{:S(2)}, u32[]{:S(2)}) collective-permute-start(f32[8,32,512]{2,1,0:T(8,128)S(1)} %get-tuple-element.38), channel_id=1, source_target_pairs={{0,4},{4,0},{1,5},{5,1},{2,6},{6,2},{3,7},{7,3},{8,12},{12,8},{9,1... | collective-permute-start | bytes 1572872 | tf_op jit(solution)/shard_map/ppermute | solution.py:152
  25.2 3.9 %shard_map.88 = (f32[8,32,256]{2,1,0:T(8,128)S(1)}, f32[8,32,256]{2,1,0:T(8,128)S(1)}, f32[24,32,256]{2,1,0:T(8,128)S(1)}, f32[24,32,256]{2,1,0:T(8,128)S(1)}) custom-call(s32[3]{0:T(128)S(1)} %pad_add_fusion.where_ref, bf16[1024,2048]{1,0:T(8,128)(2,1)S(1)} %copy-done, bf16[1024,2048]{1,0:T(8,128)(2,1)S(1)} %copy-done.1), custom_call_target="tpu_custom_call" | custom-call | flops 524288 | bytes 2048 | tf_op jit(solution)/shard_map/pallas_call | solution.py:118
  31.0 2.3 %shard_map.90 = (f32[8,32,1280]{2,1,0:T(8,128)S(1)}, f32[8,32,1280]{2,1,0:T(8,128)S(1)}) custom-call(s32[3]{0:T(128)S(1)} %pad_add_fusion.where_ref, bf16[1024,2048]{1,0:T(8,128)(2,1)S(1)} %copy-done, bf16[1024,2048]{1,0:T(8,128)(2,1)S(1)} %copy-done.1), custom_call_target="tpu_custom_call" | custom-call | flops 655360 | bytes 512 | tf_op jit(solution)/shard_map/pallas_call | solution.py:118
  36.9 7.0 %collective-permute-done.3 = f32[8,32,640]{2,1,0:T(8,128)S(1)} collective-permute-done((f32[8,32,640]{2,1,0:T(8,128)S(1)}, f32[8,32,640]{2,1,0:T(8,128)S(1)}, u32[]{:S(2)}, u32[]{:S(2)}) %collective-permute-start.3) | collective-permute-done | bytes 655392 | tf_op jit(solution)/shard_map/ppermute | solution.py:157
  43.9 3.1 %shard_map.89 = (f32[12,32,1280]{2,1,0:T(8,128)S(1)}, f32[12,32,1280]{2,1,0:T(8,128)S(1)}) custom-call(s32[3]{0:T(128)S(1)} %pad_add_fusion.where_ref, bf16[1024,2048]{1,0:T(8,128)(2,1)S(1)} %copy-done, bf16[1024,2048]{1,0:T(8,128)(2,1)S(1)} %copy-done.1), custom_call_target="tpu_custom_call" | custom-call | flops 983040 | bytes 768 | tf_op jit(solution)/shard_map/pallas_call | solution.py:118
  51.2 15.3 %collective-permute-done.23 = f32[8,32,256]{2,1,0:T(8,128)S(1)} collective-permute-done((f32[8,32,256]{2,1,0:T(8,128)S(1)}, f32[8,32,256]{2,1,0:T(8,128)S(1)}, u32[]{:S(2)}, u32[]{:S(2)}) %collective-permute-start.23) | collective-permute-done | bytes 262176 | tf_op jit(solution)/shard_map/ppermute | solution.py:157
  67.2 2.2 %collective-permute-start.21 = (f32[8,32,512]{2,1,0:T(8,128)S(1)}, f32[8,32,512]{2,1,0:T(8,128)S(1)}, u32[]{:S(2)}, u32[]{:S(2)}) collective-permute-start(f32[8,32,512]{2,1,0:T(8,128)S(1)} %slice.155), channel_id=1, source_target_pairs={{0,4},{4,0},{1,5},{5,1},{2,6},{6,2},{3,7},{7,3},{8,12},{12,8},{9,1... | collective-permute-start | bytes 1572872 | tf_op jit(solution)/shard_map/ppermute | solution.py:152
  69.7 8.7 %collective-permute-done.12 = f32[8,32,640]{2,1,0:T(8,128)S(1)} collective-permute-done((f32[8,32,640]{2,1,0:T(8,128)S(1)}, f32[8,32,640]{2,1,0:T(8,128)S(1)}, u32[]{:S(2)}, u32[]{:S(2)}) %collective-permute-start.12) | collective-permute-done | bytes 655392 | tf_op jit(solution)/shard_map/ppermute | solution.py:157
  81.8 3.7 %collective-permute-start.10 = (f32[8,32,640]{2,1,0:T(8,128)S(1)}, f32[8,32,640]{2,1,0:T(8,128)S(1)}, u32[]{:S(2)}, u32[]{:S(2)}) collective-permute-start(f32[8,32,640]{2,1,0:T(8,128)S(1)} %slice_add_fusion.5), channel_id=1, source_target_pairs={{0,32},{4,228},{32,64},{36,4},{64,96},{68,36},{96,128},{100,68},{1... | collective-permute-start | bytes 1966088 | tf_op jit(solution)/shard_map/ppermute | solution.py:157
  86.9 15.2 %collective-permute-done.27 = f32[2,32,768]{2,1,0:T(8,128)S(1)} collective-permute-done((f32[2,32,768]{2,1,0:T(8,128)S(1)}, f32[2,32,768]{2,1,0:T(8,128)S(1)}, u32[]{:S(2)}, u32[]{:S(2)}) %collective-permute-start.27) | collective-permute-done | bytes 196640 | tf_op jit(solution)/shard_map/ppermute | solution.py:157
  103.5 5.6 %collective-permute-done.28 = f32[2,32,768]{2,1,0:T(8,128)S(1)} collective-permute-done((f32[2,32,768]{2,1,0:T(8,128)S(1)}, f32[2,32,768]{2,1,0:T(8,128)S(1)}, u32[]{:S(2)}, u32[]{:S(2)}) %collective-permute-start.28) | collective-permute-done | bytes 196640 | tf_op jit(solution)/shard_map/ppermute | solution.py:157
  109.5 1.9 %collective-permute-start.16 = (f32[32,1280]{1,0:T(8,128)S(1)}, f32[32,1280]{1,0:T(8,128)S(1)}, u32[]{:S(2)}, u32[]{:S(2)}) collective-permute-start(f32[32,1280]{1,0:T(8,128)S(1)} %get-tuple-element.63), channel_id=1, source_target_pairs={{0,16},{8,24},{16,0},{24,8},{1,17},{9,25},{17,1},{25,9},{2,18},{10... | collective-permute-start | bytes 491528 | tf_op jit(solution)/shard_map/ppermute | solution.py:162
  113.4 2.7 %collective-permute-done.29 = f32[2,32,768]{2,1,0:T(8,128)S(1)} collective-permute-done((f32[2,32,768]{2,1,0:T(8,128)S(1)}, f32[2,32,768]{2,1,0:T(8,128)S(1)}, u32[]{:S(2)}, u32[]{:S(2)}) %collective-permute-start.29) | collective-permute-done | bytes 196640 | tf_op jit(solution)/shard_map/ppermute | solution.py:157
  116.2 2.0 %collective-permute-done.16 = f32[32,1280]{1,0:T(8,128)S(1)} collective-permute-done((f32[32,1280]{1,0:T(8,128)S(1)}, f32[32,1280]{1,0:T(8,128)S(1)}, u32[]{:S(2)}, u32[]{:S(2)}) %collective-permute-start.16) | collective-permute-done | bytes 163872 | tf_op jit(solution)/shard_map/ppermute | solution.py:162
  118.2 2.1 %collective-permute-done.15 = f32[32,1280]{1,0:T(8,128)S(1)} collective-permute-done((f32[32,1280]{1,0:T(8,128)S(1)}, f32[32,1280]{1,0:T(8,128)S(1)}, u32[]{:S(2)}, u32[]{:S(2)}) %collective-permute-start.15) | collective-permute-done | bytes 163872 | tf_op jit(solution)/shard_map/ppermute | solution.py:162
  120.5 16.6 %all_to_all.10 = f32[32,8,128]{2,1,0:T(8,128)S(1)} all-to-all(f32[32,8,128]{2,1,0:T(8,128)S(1)} %broadcast_in_dim.4), channel_id=1, replica_groups=mesh['z'=8,'x'=4,'c'=2,'y'=4] {'z','x'}, dimensions={0} | all-to-all | bytes 262144 | tf_op jit(solution)/shard_map/all_to_all | solution.py:171
  137.2 8.7 %all_to_all.11 = f32[8,8,128]{2,1,0:T(8,128)S(1)} all-to-all(f32[8,8,128]{2,1,0:T(8,128)S(1)} %broadcast_in_dim.5), channel_id=1, replica_groups=mesh['z'=8,'x'=4,'c'=2,'y'=4] {'c','y'}, dimensions={0} | all-to-all | bytes 65536 | tf_op jit(solution)/shard_map/all_to_all | solution.py:171
  148.3 9.1 %psum.7 = f32[2,32]{1,0:T(2,128)S(1)} all-reduce(f32[2,32]{1,0:T(2,128)S(1)} %pad_maximum_fusion.1), channel_id=1, replica_groups=mesh['z'=8,'x'=4,'c'=2,'y'=4] {'y'}, use_global_device_ids=true, to_apply=%region_5.0 | all-reduce | flops 64 | bytes 512 | tf_op jit(solution)/shard_map/psum | solution.py:265
  (104 shorter events, 27.1 us)
Async XLA Ops:
  9.5 15.2 %collective-permute-start = (f32[8,32,1280]{2,1,0:T(8,128)S(1)}, f32[8,32,1280]{2,1,0:T(8,128)S(1)}, u32[]{:S(2)}, u32[]{:S(2)}) collective-permute-start(f32[8,32,1280]{2,1,0:T(8,128)S(1)} %get-tuple-element.34), channel_id=1, source_target_pairs={{0,4},{4,0},{1,5},{5,1},{2,6},{6,2},{3,7},{7,3},{8,12},{12,8},{9,1... | collective-permute-start | bytes 3932168 | tf_op jit(solution)/shard_map/ppermute | solution.py:152
  10.2 14.5 %collective-permute-start.2 = (f32[4,32,1280]{2,1,0:T(8,128)S(1)}, f32[4,32,1280]{2,1,0:T(8,128)S(1)}, u32[]{:S(2)}, u32[]{:S(2)}) collective-permute-start(f32[4,32,1280]{2,1,0:T(8,128)S(1)} %add.144), channel_id=1, source_target_pairs={{0,32},{4,228},{32,64},{36,4},{64,96},{68,36},{96,128},{100,68},{1... | collective-permute-start | bytes 1966088 | tf_op jit(solution)/shard_map/ppermute | solution.py:157
  22.5 24.7 %collective-permute-start.18 = (f32[24,32,512]{2,1,0:T(8,128)S(1)}, f32[24,32,512]{2,1,0:T(8,128)S(1)}, u32[]{:S(2)}, u32[]{:S(2)}) collective-permute-start(f32[24,32,512]{2,1,0:T(8,128)S(1)} %get-tuple-element.55), channel_id=1, source_target_pairs={{0,4},{4,0},{1,5},{5,1},{2,6},{6,2},{3,7},{7,3},{8,12},{12,8},{9,1... | collective-permute-start | bytes 4718600 | tf_op jit(solution)/shard_map/ppermute | solution.py:152
  25.0 11.9 %collective-permute-start.4 = (f32[8,32,640]{2,1,0:T(8,128)S(1)}, f32[8,32,640]{2,1,0:T(8,128)S(1)}, u32[]{:S(2)}, u32[]{:S(2)}) collective-permute-start(f32[8,32,640]{2,1,0:T(8,128)S(1)} %slice_add_fusion.6), channel_id=1, source_target_pairs={{0,32},{4,228},{32,64},{36,4},{64,96},{68,36},{96,128},{100,68},{1... | collective-permute-start | bytes 1966088 | tf_op jit(solution)/shard_map/ppermute | solution.py:157
  25.1 18.8 %collective-permute-start.3 = (f32[8,32,640]{2,1,0:T(8,128)S(1)}, f32[8,32,640]{2,1,0:T(8,128)S(1)}, u32[]{:S(2)}, u32[]{:S(2)}) collective-permute-start(f32[8,32,640]{2,1,0:T(8,128)S(1)} %slice_add_fusion.7), channel_id=1, source_target_pairs={{0,32},{4,228},{32,64},{36,4},{64,96},{68,36},{96,128},{100,68},{1... | collective-permute-start | bytes 1966088 | tf_op jit(solution)/shard_map/ppermute | solution.py:157
  33.3 17.4 %collective-permute-start.8 = (f32[8,32,1280]{2,1,0:T(8,128)S(1)}, f32[8,32,1280]{2,1,0:T(8,128)S(1)}, u32[]{:S(2)}, u32[]{:S(2)}) collective-permute-start(f32[8,32,1280]{2,1,0:T(8,128)S(1)} %get-tuple-element.50), channel_id=1, source_target_pairs={{0,4},{4,0},{1,5},{5,1},{2,6},{6,2},{3,7},{7,3},{8,12},{12,8},{9,1... | collective-permute-start | bytes 3932168 | tf_op jit(solution)/shard_map/ppermute | solution.py:152
  33.4 14.1 %collective-permute-start.19 = (f32[8,32,512]{2,1,0:T(8,128)S(1)}, f32[8,32,512]{2,1,0:T(8,128)S(1)}, u32[]{:S(2)}, u32[]{:S(2)}) collective-permute-start(f32[8,32,512]{2,1,0:T(8,128)S(1)} %add.148), channel_id=1, source_target_pairs={{0,8},{4,28},{8,16},{12,4},{16,24},{20,12},{24,0},{28,20},{1,9},{5... | collective-permute-start | bytes 1572872 | tf_op jit(solution)/shard_map/ppermute | solution.py:157
  47.0 22.3 %collective-permute-start.7 = (f32[12,32,1280]{2,1,0:T(8,128)S(1)}, f32[12,32,1280]{2,1,0:T(8,128)S(1)}, u32[]{:S(2)}, u32[]{:S(2)}) collective-permute-start(f32[12,32,1280]{2,1,0:T(8,128)S(1)} %get-tuple-element.46), channel_id=1, source_target_pairs={{0,4},{4,0},{1,5},{5,1},{2,6},{6,2},{3,7},{7,3},{8,12},{12,8},{9,1... | collective-permute-start | bytes 5898248 | tf_op jit(solution)/shard_map/ppermute | solution.py:152
  47.6 19.5 %collective-permute-start.20 = (f32[16,32,512]{2,1,0:T(8,128)S(1)}, f32[16,32,512]{2,1,0:T(8,128)S(1)}, u32[]{:S(2)}, u32[]{:S(2)}) collective-permute-start(f32[16,32,512]{2,1,0:T(8,128)S(1)} %slice_add_fusion), channel_id=1, source_target_pairs={{0,8},{4,28},{8,16},{12,4},{16,24},{20,12},{24,0},{28,20},{1,9},{5... | collective-permute-start | bytes 3145736 | tf_op jit(solution)/shard_map/ppermute | solution.py:157
  49.2 17.3 %collective-permute-start.22 = (f32[24,32,256]{2,1,0:T(8,128)S(1)}, f32[24,32,256]{2,1,0:T(8,128)S(1)}, u32[]{:S(2)}, u32[]{:S(2)}) collective-permute-start(f32[24,32,256]{2,1,0:T(8,128)S(1)} %get-tuple-element.57), channel_id=1, source_target_pairs={{0,4},{4,0},{1,5},{5,1},{2,6},{6,2},{3,7},{7,3},{8,12},{12,8},{9,1... | collective-permute-start | bytes 2359304 | tf_op jit(solution)/shard_map/ppermute | solution.py:152
  50.7 15.8 %collective-permute-start.23 = (f32[8,32,256]{2,1,0:T(8,128)S(1)}, f32[8,32,256]{2,1,0:T(8,128)S(1)}, u32[]{:S(2)}, u32[]{:S(2)}) collective-permute-start(f32[8,32,256]{2,1,0:T(8,128)S(1)} %add.147), channel_id=1, source_target_pairs={{0,8},{4,28},{8,16},{12,4},{16,24},{20,12},{24,0},{28,20},{1,9},{5... | collective-permute-start | bytes 786440 | tf_op jit(solution)/shard_map/ppermute | solution.py:157
  51.0 18.6 %collective-permute-start.9 = (f32[8,32,640]{2,1,0:T(8,128)S(1)}, f32[8,32,640]{2,1,0:T(8,128)S(1)}, u32[]{:S(2)}, u32[]{:S(2)}) collective-permute-start(f32[8,32,640]{2,1,0:T(8,128)S(1)} %slice_add_fusion.4), channel_id=1, source_target_pairs={{0,32},{4,228},{32,64},{36,4},{64,96},{68,36},{96,128},{100,68},{1... | collective-permute-start | bytes 1966088 | tf_op jit(solution)/shard_map/ppermute | solution.py:157
  66.5 11.8 %collective-permute-start.12 = (f32[8,32,640]{2,1,0:T(8,128)S(1)}, f32[8,32,640]{2,1,0:T(8,128)S(1)}, u32[]{:S(2)}, u32[]{:S(2)}) collective-permute-start(f32[8,32,640]{2,1,0:T(8,128)S(1)} %slice_add_fusion.2), channel_id=1, source_target_pairs={{0,32},{4,228},{32,64},{36,4},{64,96},{68,36},{96,128},{100,68},{1... | collective-permute-start | bytes 1966088 | tf_op jit(solution)/shard_map/ppermute | solution.py:157
  66.7 11.6 %collective-permute-start.24 = (f32[16,32,256]{2,1,0:T(8,128)S(1)}, f32[16,32,256]{2,1,0:T(8,128)S(1)}, u32[]{:S(2)}, u32[]{:S(2)}) collective-permute-start(f32[16,32,256]{2,1,0:T(8,128)S(1)} %slice_add_fusion.8), channel_id=1, source_target_pairs={{0,8},{4,28},{8,16},{12,4},{16,24},{20,12},{24,0},{28,20},{1,9},{5... | collective-permute-start | bytes 1572872 | tf_op jit(solution)/shard_map/ppermute | solution.py:157
  67.2 11.3 %collective-permute-start.21 = (f32[8,32,512]{2,1,0:T(8,128)S(1)}, f32[8,32,512]{2,1,0:T(8,128)S(1)}, u32[]{:S(2)}, u32[]{:S(2)}) collective-permute-start(f32[8,32,512]{2,1,0:T(8,128)S(1)} %slice.155), channel_id=1, source_target_pairs={{0,4},{4,0},{1,5},{5,1},{2,6},{6,2},{3,7},{7,3},{8,12},{12,8},{9,1... | collective-permute-start | bytes 1572872 | tf_op jit(solution)/shard_map/ppermute | solution.py:152
  80.3 22.5 %collective-permute-start.13 = (f32[8,32,640]{2,1,0:T(8,128)S(1)}, f32[8,32,640]{2,1,0:T(8,128)S(1)}, u32[]{:S(2)}, u32[]{:S(2)}) collective-permute-start(f32[8,32,640]{2,1,0:T(8,128)S(1)} %slice_add_fusion.3), channel_id=1, source_target_pairs={{0,32},{4,228},{32,64},{36,4},{64,96},{68,36},{96,128},{100,68},{1... | collective-permute-start | bytes 1966088 | tf_op jit(solution)/shard_map/ppermute | solution.py:157
  81.8 21.4 %collective-permute-start.10 = (f32[8,32,640]{2,1,0:T(8,128)S(1)}, f32[8,32,640]{2,1,0:T(8,128)S(1)}, u32[]{:S(2)}, u32[]{:S(2)}) collective-permute-start(f32[8,32,640]{2,1,0:T(8,128)S(1)} %slice_add_fusion.5), channel_id=1, source_target_pairs={{0,32},{4,228},{32,64},{36,4},{64,96},{68,36},{96,128},{100,68},{1... | collective-permute-start | bytes 1966088 | tf_op jit(solution)/shard_map/ppermute | solution.py:157
  86.0 16.1 %collective-permute-start.27 = (f32[2,32,768]{2,1,0:T(8,128)S(1)}, f32[2,32,768]{2,1,0:T(8,128)S(1)}, u32[]{:S(2)}, u32[]{:S(2)}) collective-permute-start(f32[2,32,768]{2,1,0:T(8,128)S(1)} %fusion.6), channel_id=1, source_target_pairs={{0,32},{4,228},{32,64},{36,4},{64,96},{68,36},{96,128},{100,68},{1... | collective-permute-start | bytes 589832 | tf_op jit(solution)/shard_map/ppermute | solution.py:157
  102.1 7.0 %collective-permute-start.28 = (f32[2,32,768]{2,1,0:T(8,128)S(1)}, f32[2,32,768]{2,1,0:T(8,128)S(1)}, u32[]{:S(2)}, u32[]{:S(2)}) collective-permute-start(f32[2,32,768]{2,1,0:T(8,128)S(1)} %fusion.4), channel_id=1, source_target_pairs={{0,32},{4,228},{32,64},{36,4},{64,96},{68,36},{96,128},{100,68},{1... | collective-permute-start | bytes 589832 | tf_op jit(solution)/shard_map/ppermute | solution.py:157
  102.8 6.4 %collective-permute-start.14 = (f32[4,32,640]{2,1,0:T(8,128)S(1)}, f32[4,32,640]{2,1,0:T(8,128)S(1)}, u32[]{:S(2)}, u32[]{:S(2)}) collective-permute-start(f32[4,32,640]{2,1,0:T(8,128)S(1)} %slice.147), channel_id=1, source_target_pairs={{0,4},{4,0},{1,5},{5,1},{2,6},{6,2},{3,7},{7,3},{8,12},{12,8},{9,1... | collective-permute-start | bytes 983048 | tf_op jit(solution)/shard_map/ppermute | solution.py:152
  109.1 7.0 %collective-permute-start.29 = (f32[2,32,768]{2,1,0:T(8,128)S(1)}, f32[2,32,768]{2,1,0:T(8,128)S(1)}, u32[]{:S(2)}, u32[]{:S(2)}) collective-permute-start(f32[2,32,768]{2,1,0:T(8,128)S(1)} %fusion.2), channel_id=1, source_target_pairs={{0,32},{4,228},{32,64},{36,4},{64,96},{68,36},{96,128},{100,68},{1... | collective-permute-start | bytes 589832 | tf_op jit(solution)/shard_map/ppermute | solution.py:157
  109.5 8.7 %collective-permute-start.16 = (f32[32,1280]{1,0:T(8,128)S(1)}, f32[32,1280]{1,0:T(8,128)S(1)}, u32[]{:S(2)}, u32[]{:S(2)}) collective-permute-start(f32[32,1280]{1,0:T(8,128)S(1)} %get-tuple-element.63), channel_id=1, source_target_pairs={{0,16},{8,24},{16,0},{24,8},{1,17},{9,25},{17,1},{25,9},{2,18},{10... | collective-permute-start | bytes 491528 | tf_op jit(solution)/shard_map/ppermute | solution.py:162
  111.4 6.8 %collective-permute-start.17 = (f32[32,1280]{1,0:T(8,128)S(1)}, f32[32,1280]{1,0:T(8,128)S(1)}, u32[]{:S(2)}, u32[]{:S(2)}) collective-permute-start(f32[32,1280]{1,0:T(8,128)S(1)} %get-tuple-element.64), channel_id=1, source_target_pairs={{0,24},{8,0},{16,8},{24,16},{1,25},{9,1},{17,9},{25,17},{2,26},{10... | collective-permute-start | bytes 491528 | tf_op jit(solution)/shard_map/ppermute | solution.py:162
  112.5 7.8 %collective-permute-start.15 = (f32[32,1280]{1,0:T(8,128)S(1)}, f32[32,1280]{1,0:T(8,128)S(1)}, u32[]{:S(2)}, u32[]{:S(2)}) collective-permute-start(f32[32,1280]{1,0:T(8,128)S(1)} %get-tuple-element.65), channel_id=1, source_target_pairs={{0,8},{8,16},{16,24},{24,0},{1,9},{9,17},{17,25},{25,1},{2,10},{10... | collective-permute-start | bytes 491528 | tf_op jit(solution)/shard_map/ppermute | solution.py:162
  (13 other events, 139.0 us)

commit v3 on v1

--- a/solution.py
+++ b/solution.py
@@ -15,7 +15,7 @@
 DP = ("z", "x", "c")
 NZ, NX = 8, 4
 SIZE = {"z": NZ, "x": NX}
-COLS_Z = 1152
+COLS_Z = 1280
 
 
 def dot(lhs_ref, rhs_ref, z, start, cols):
@@ -25,9 +25,7 @@
 
 
 def near_x(x, c):
-    s = 1 - 2 * c
-    ahead = lax.rem(x + s + NX, NX)
-    return [(ahead, c), (ahead, 1 - c), (lax.rem(x + 2, NX), c), (x, c)]
+    return [(lax.rem(x + k, NX), c) for k in range(NX)]
 
 
 def product_z_kernel(hops, cols, where_ref, lhs_ref, rhs_ref, keep_ref, send_ref, acc):
@@ -123,19 +121,13 @@
     return lax.ppermute(value, (axis, "c"), [(2 * i + c, 2 * ((i + 1 - 2 * c) % n) + c) for i in range(n) for c in range(2)])
 
 
+def shift(value, axis, by):
+    n = SIZE[axis]
+    return lax.ppermute(value, axis, [(i, (i + by) % n) for i in range(n)])
+
+
 def at_front(part, whole):
     return lax.pad(part, jnp.float32(0), [(0, whole - part.shape[0], 0), (0, 0, 0), (0, 0, 0)])
-
-
-def ring_sum(blocks, own, axis):
-    moving = onward(blocks[0](), axis)
-    for block in blocks[1:]:
-        here = block()
-        if moving.shape != here.shape:
-            moving = at_front(moving, here.shape[0])
-        moving = onward(here + moving, axis)
-    half = moving.shape[0] // 2
-    return moving[:half] + other_core(moving[half:]) + own()
 
 
 def sum_over(tile, axes, n):
@@ -144,12 +136,11 @@
 
 
 def after(value, *others):
-    return lax.optimization_barrier((value,) + others)[0]
+    return lax.optimization_barrier((value, others))[0]
 
 
 def shards(attn_out, grad_out, grad_acc, master_weight, moment_m, moment_v):
     entry_count = 2048 * 8192
-    cols_x = attn_out.shape[1] - COLS_Z
     where = jnp.stack([lax.axis_index(a) for a in DP]).astype(jnp.int32)
 
     def product_z(where, hops):
@@ -158,33 +149,47 @@
             functools.partial(product_z_kernel, hops, COLS_Z), [groups] * 2, COLS_Z, groups * 64, where, grad_out, attn_out
         )
 
-    def both(keep, send):
-        got = other_core(send)
-        return lambda lo=0, hi=None: keep[lo:hi] + got[lo:hi]
+    def both(pair):
+        return pair[0] + pair[1]
+
+    cols_x = attn_out.shape[1] - COLS_Z
+
+    def add(here, moving):
+        return here + (moving if moving.shape == here.shape else at_front(moving, here.shape[0]))
 
     pair4 = product_z(where, (4,))
-    z4 = both(*pair4)
+    pair4 = (pair4[0], other_core(pair4[1]))
     pair3 = product_z(after(where, pair4[0]), (3,))
-    z3 = both(*pair3)
-    z4_there = lax.optimization_barrier(z4())
-    keep2, send2, keep, send = product(
+    pair3 = (pair3[0], other_core(pair3[1]))
+    first_z = lax.optimization_barrier(both(pair4))
+    keep_far, send_far, keep_x, send_x = product(
         functools.partial(product_x_kernel, COLS_Z, cols_x),
-        [8, 8, 24, 24], cols_x, 2048, after(where, pair3[0], z4_there), grad_out, attn_out,
+        [8, 8, 24, 24], cols_x, 2048, after(where, pair3[0], first_z), grad_out, attn_out,
     )
-    x2, x10 = both(keep2, send2), both(keep, send)
-    pair2 = product_z(after(where, keep2), (2,))
-    z2 = both(*pair2)
-    x2_there = lax.optimization_barrier(x2())
-    pair10 = product_z(after(where, pair2[0], x2_there), (1, 0))
-    z10 = both(*pair10)
-
-    sum_z = ring_sum([lambda: z4_there, z3, z2, lambda: z10(0, 8)], lambda: z10(8, 12), "z")
-    sum_x = ring_sum([lambda: x2_there, lambda: x10(0, 16)], lambda: x10(16, 24), "x")
-    batch_z = ring_sum([lambda: sum_z[2:3], lambda: sum_z[0:2]], lambda: sum_z[3:4], "x")
-    batch_x = ring_sum(
-        [lambda: sum_x[6:7], lambda: sum_x[4:6], lambda: sum_x[2:4], lambda: sum_x[0:2]], lambda: sum_x[7:8], "z"
-    )
-    gradient = grad_acc + jnp.concatenate([batch_z[0], batch_x[0]], axis=1)
+    next_z = add(both(pair3)[:8], onward(first_z, "z"))
+    far_x = (keep_far, after(other_core(send_far), next_z))
+    pair2 = product_z(after(where, keep_far, next_z), (2,))
+    pair2 = (pair2[0], other_core(pair2[1]))
+    first_x = lax.optimization_barrier(both(far_x))
+    pair_x = (keep_x, other_core(after(send_x, first_x)))
+    pair1 = product_z(after(where, pair2[0], first_x), (1, 0))
+    pair1 = (pair1[0], other_core(pair1[1]))
+
+    z = onward(next_z, "z")
+    for pair in (pair2, pair1):
+        z = onward(add(both(pair)[:8], z), "z")
+    sum_z = z[:4] + other_core(z[4:]) + both(pair1)[8:12]
+    x = onward(first_x, "x")
+    x = onward(add(both(pair_x)[:16], x), "x")
+    sum_x = x[:8] + other_core(x[8:]) + both(pair_x)[16:24]
+
+    batch_z = sum_z[0] + sum(shift(sum_z[k], "x", k) for k in (1, 2, 3))
+    moving = onward(sum_x[6:7], "z")
+    moving = onward(add(sum_x[4:6], moving), "z")
+    moving = onward(sum_x[2:4] + moving, "z")
+    moving = onward(sum_x[0:2] + moving, "z")
+    batch_x = moving[0] + other_core(moving[1]) + sum_x[7]
+    gradient = grad_acc + jnp.concatenate([batch_z, batch_x], axis=1)
 
     energy = jnp.sum((gradient * gradient).reshape(4, 8, 16, 128), axis=(0, 2))
     energy = sum_over(sum_over(energy, ("z", "x"), NZ * NX), ("c", "y"), 8)

time: 148 us -> 147 us (level)
  starting transfers between devices: 15.4 us -> 19.2 us
  waiting for transfers between devices: 69.1 us -> 65.5 us
    ppermute x0 -> x3, starting transfers between devices: none -> 5.14 us  [shift(): return lax.ppermute(value, axis, [(i, (i + by) % n) for i in range(n)])]
    ppermute x12 -> x10, waiting for transfers between devices: 64.1 us -> 59.4 us  [onward(): lax.ppermute(value, (axis, 'c'), [(2 * i + c, 2 * ((i + 1 - 2 * c) % n) +...]
    ppermute x0 -> x3, waiting for transfers between devices: none -> 3.88 us  [shift(): return lax.ppermute(value, axis, [(i, (i + by) % n) for i in range(n)])]
    ppermute x10 -> x9, waiting for transfers between devices: 5.05 us -> 2.29 us  [other_core(): return lax.ppermute(value, 'c', [(0, 1), (1, 0)])]
    ppermute x12 -> x10, starting transfers between devices: 7.87 us -> 5.61 us  [onward(): lax.ppermute(value, (axis, 'c'), [(2 * i + c, 2 * ((i + 1 - 2 * c) % n) +...]
    ppermute x10 -> x9, starting transfers between devices: 7.57 us -> 8.42 us  [other_core(): return lax.ppermute(value, 'c', [(0, 1), (1, 0)])]
  transfers between devices with their start and end apart: 22 -> 22, of which waited for: 12 -> 13; matrix products, arithmetic and copies ran while one was open for 1% -> 1% of each run, Pallas kernels for 10% -> 10%
where the time goes in v3:
time: 147 us
  waiting for transfers between devices  65.5 us (45%)
  blocking collectives  35.2 us (24%)
  starting transfers between devices  19.2 us (13%)
  Pallas kernels  15.7 us (11%)
  other arithmetic  4.68 us (3%)
  local copies, waits for them, and re-layouts  4.58 us (3%)
  between operations  1.67 us (1%)
    ppermute x10, waiting for transfers between devices, onward(): lax.ppermute(value, (axis, 'c'), [(2 * i + c, 2 * ((i + 1 - 2 * c) % n) +...  59.4 us
    all_to_all x2, blocking collectives, sum_over(): return jnp.sum(lax.all_to_all(copies, axes, 0, 0, tiled=True), axis=0)  26.1 us
    pallas_call x5, Pallas kernels, product(): pl.pallas_call(kernel, in_specs=[pl.BlockSpec(memory_space=pltpu.SMEM), V...  15.7 us
    psum x1, blocking collectives, shards(): norms = jnp.sqrt(lax.psum(squares, 'y'))  9.1 us
    ppermute x9, starting transfers between devices, other_core(): return lax.ppermute(value, 'c', [(0, 1), (1, 0)])  8.42 us
    ppermute x10, starting transfers between devices, onward(): lax.ppermute(value, (axis, 'c'), [(2 * i + c, 2 * ((i + 1 - 2 * c) % n) +...  5.61 us
    ppermute x3, starting transfers between devices, shift(): return lax.ppermute(value, axis, [(i, (i + by) % n) for i in range(n)])  5.14 us
    unnamed x12, local copies, waits for them, and re-layouts  4.4 us
  transfers between devices with their start and end apart: 22, of which 13 were waited for; matrix products, arithmetic and copies ran while one was open for 1% of the time, Pallas kernels for 10%

profile of v3, /device:TPU:8, one launch (start us, length us, event | category | flops | bytes accessed | tf_op | source)
XLA Modules:
  0.0 146.5 jit_solution(18022721732734624649)
XLA Ops:
  0.7 2.2 %copy-done = bf16[1024,2048]{1,0:T(8,128)(2,1)S(1)} copy-done((bf16[1024,2048]{1,0:T(8,128)(2,1)S(1)}, bf16[1024,2048]{1,0:T(8,128)(2,1)}, u32[]{:S(2)}) %copy-start) | copy-done | bytes 4194328
  2.9 2.2 %copy-done.1 = bf16[1024,2048]{1,0:T(8,128)(2,1)S(1)} copy-done((bf16[1024,2048]{1,0:T(8,128)(2,1)S(1)}, bf16[1024,2048]{1,0:T(8,128)(2,1)}, u32[]{:S(2)}) %copy-start.1) | copy-done | bytes 4194328
  6.8 2.3 %shard_map.86 = (f32[8,32,1280]{2,1,0:T(8,128)S(1)}, f32[8,32,1280]{2,1,0:T(8,128)S(1)}) custom-call(s32[3]{0:T(128)S(1)} %pad_add_fusion.1.where_ref, bf16[1024,2048]{1,0:T(8,128)(2,1)S(1)} %copy-done, bf16[1024,2048]{1,0:T(8,128)(2,1)S(1)} %copy-done.1), custom_call_target="tpu_custom_call" | custom-call | flops 655360 | bytes 512 | tf_op jit(solution)/shard_map/pallas_call | solution.py:100
  9.8 2.0 %collective-permute-start.2 = (f32[4,32,1280]{2,1,0:T(8,128)S(1)}, f32[4,32,1280]{2,1,0:T(8,128)S(1)}, u32[]{:S(2)}, u32[]{:S(2)}) collective-permute-start(f32[4,32,1280]{2,1,0:T(8,128)S(1)} %add.108), channel_id=1, source_target_pairs={{0,32},{4,228},{32,64},{36,4},{64,96},{68,36},{96,128},{100,68},{1... | collective-permute-start | bytes 1966088 | tf_op jit(solution)/shard_map/ppermute | solution.py:121
  11.7 6.3 %shard_map.87 = (f32[8,32,768]{2,1,0:T(8,128)S(1)}, f32[8,32,768]{2,1,0:T(8,128)S(1)}, f32[24,32,768]{2,1,0:T(8,128)S(1)}, f32[24,32,768]{2,1,0:T(8,128)S(1)}) custom-call(s32[3]{0:T(128)S(1)} %pad_add_fusion.1.where_ref, bf16[1024,2048]{1,0:T(8,128)(2,1)S(1)} %copy-done, bf16[1024,2048]{1,0:T(8,128)(2,1)S(1)} %copy-done.1), custom_call_target="tpu_custom_call" | custom-call | flops 1572864 | bytes 2048 | tf_op jit(solution)/shard_map/pallas_call | solution.py:100
  18.1 3.8 %collective-permute-start.3 = (f32[8,32,768]{2,1,0:T(8,128)S(1)}, f32[8,32,768]{2,1,0:T(8,128)S(1)}, u32[]{:S(2)}, u32[]{:S(2)}) collective-permute-start(f32[8,32,768]{2,1,0:T(8,128)S(1)} %get-tuple-element.30), channel_id=1, source_target_pairs={{0,4},{4,0},{1,5},{5,1},{2,6},{6,2},{3,7},{7,3},{8,12},{12,8},{9,1... | collective-permute-start | bytes 2359304 | tf_op jit(solution)/shard_map/ppermute | solution.py:116
  21.9 2.4 %collective-permute-done.2 = f32[4,32,1280]{2,1,0:T(8,128)S(1)} collective-permute-done((f32[4,32,1280]{2,1,0:T(8,128)S(1)}, f32[4,32,1280]{2,1,0:T(8,128)S(1)}, u32[]{:S(2)}, u32[]{:S(2)}) %collective-permute-start.2) | collective-permute-done | bytes 655392 | tf_op jit(solution)/shard_map/ppermute | solution.py:121
  24.8 2.3 %shard_map.88 = (f32[8,32,1280]{2,1,0:T(8,128)S(1)}, f32[8,32,1280]{2,1,0:T(8,128)S(1)}) custom-call(s32[3]{0:T(128)S(1)} %pad_add_fusion.1.where_ref, bf16[1024,2048]{1,0:T(8,128)(2,1)S(1)} %copy-done, bf16[1024,2048]{1,0:T(8,128)(2,1)S(1)} %copy-done.1), custom_call_target="tpu_custom_call" | custom-call | flops 655360 | bytes 512 | tf_op jit(solution)/shard_map/pallas_call | solution.py:100
  27.1 2.2 %collective-permute-start.5 = (f32[8,32,1280]{2,1,0:T(8,128)S(1)}, f32[8,32,1280]{2,1,0:T(8,128)S(1)}, u32[]{:S(2)}, u32[]{:S(2)}) collective-permute-start(f32[8,32,1280]{2,1,0:T(8,128)S(1)} %get-tuple-element.35), channel_id=1, source_target_pairs={{0,4},{4,0},{1,5},{5,1},{2,6},{6,2},{3,7},{7,3},{8,12},{12,8},{9,1... | collective-permute-start | bytes 3932168 | tf_op jit(solution)/shard_map/ppermute | solution.py:116
  30.8 3.1 %shard_map.89 = (f32[12,32,1280]{2,1,0:T(8,128)S(1)}, f32[12,32,1280]{2,1,0:T(8,128)S(1)}) custom-call(s32[3]{0:T(128)S(1)} %pad_add_fusion.1.where_ref, bf16[1024,2048]{1,0:T(8,128)(2,1)S(1)} %copy-done, bf16[1024,2048]{1,0:T(8,128)(2,1)S(1)} %copy-done.1), custom_call_target="tpu_custom_call" | custom-call | flops 983040 | bytes 768 | tf_op jit(solution)/shard_map/pallas_call | solution.py:100
  35.3 8.3 %collective-permute-done.6 = f32[8,32,1280]{2,1,0:T(8,128)S(1)} collective-permute-done((f32[8,32,1280]{2,1,0:T(8,128)S(1)}, f32[8,32,1280]{2,1,0:T(8,128)S(1)}, u32[]{:S(2)}, u32[]{:S(2)}) %collective-permute-start.6) | collective-permute-done | bytes 1310752 | tf_op jit(solution)/shard_map/ppermute | solution.py:121
  46.3 16.5 %collective-permute-done.7 = f32[8,32,1280]{2,1,0:T(8,128)S(1)} collective-permute-done((f32[8,32,1280]{2,1,0:T(8,128)S(1)}, f32[8,32,1280]{2,1,0:T(8,128)S(1)}, u32[]{:S(2)}, u32[]{:S(2)}) %collective-permute-start.7) | collective-permute-done | bytes 1310752 | tf_op jit(solution)/shard_map/ppermute | solution.py:121
  63.0 3.2 %collective-permute-done.15 = f32[16,32,768]{2,1,0:T(8,128)S(1)} collective-permute-done((f32[16,32,768]{2,1,0:T(8,128)S(1)}, f32[16,32,768]{2,1,0:T(8,128)S(1)}, u32[]{:S(2)}, u32[]{:S(2)}) %collective-permute-start.15) | collective-permute-done | bytes 1572896 | tf_op jit(solution)/shard_map/ppermute | solution.py:121
  66.3 2.3 %collective-permute-done.16 = f32[8,32,768]{2,1,0:T(8,128)S(1)} collective-permute-done((f32[8,32,768]{2,1,0:T(8,128)S(1)}, f32[8,32,768]{2,1,0:T(8,128)S(1)}, u32[]{:S(2)}, u32[]{:S(2)}) %collective-permute-start.16) | collective-permute-done | bytes 786464 | tf_op jit(solution)/shard_map/ppermute | solution.py:116
  68.9 12.9 %collective-permute-done.8 = f32[8,32,1280]{2,1,0:T(8,128)S(1)} collective-permute-done((f32[8,32,1280]{2,1,0:T(8,128)S(1)}, f32[8,32,1280]{2,1,0:T(8,128)S(1)}, u32[]{:S(2)}, u32[]{:S(2)}) %collective-permute-start.8) | collective-permute-done | bytes 1310752 | tf_op jit(solution)/shard_map/ppermute | solution.py:121
  83.0 6.9 %collective-permute-done.18 = f32[2,32,768]{2,1,0:T(8,128)S(1)} collective-permute-done((f32[2,32,768]{2,1,0:T(8,128)S(1)}, f32[2,32,768]{2,1,0:T(8,128)S(1)}, u32[]{:S(2)}, u32[]{:S(2)}) %collective-permute-start.18) | collective-permute-done | bytes 196640 | tf_op jit(solution)/shard_map/ppermute | solution.py:121
  90.1 6.7 %collective-permute-done.19 = f32[2,32,768]{2,1,0:T(8,128)S(1)} collective-permute-done((f32[2,32,768]{2,1,0:T(8,128)S(1)}, f32[2,32,768]{2,1,0:T(8,128)S(1)}, u32[]{:S(2)}, u32[]{:S(2)}) %collective-permute-start.19) | collective-permute-done | bytes 196640 | tf_op jit(solution)/shard_map/ppermute | solution.py:121
  97.0 3.1 %collective-permute-start.11 = (f32[32,1280]{1,0:T(8,128)S(1)}, f32[32,1280]{1,0:T(8,128)S(1)}, u32[]{:S(2)}, u32[]{:S(2)}) collective-permute-start(f32[32,1280]{1,0:T(8,128)S(1)} %get-tuple-element.43), channel_id=1, source_target_pairs={{0,16},{8,24},{16,0},{24,8},{1,17},{9,25},{17,1},{25,9},{2,18},{10... | collective-permute-start | bytes 491528 | tf_op jit(solution)/shard_map/ppermute | solution.py:126
  102.2 1.6 %collective-permute-done.20 = f32[2,32,768]{2,1,0:T(8,128)S(1)} collective-permute-done((f32[2,32,768]{2,1,0:T(8,128)S(1)}, f32[2,32,768]{2,1,0:T(8,128)S(1)}, u32[]{:S(2)}, u32[]{:S(2)}) %collective-permute-start.20) | collective-permute-done | bytes 196640 | tf_op jit(solution)/shard_map/ppermute | solution.py:121
  104.0 1.7 %collective-permute-done.12 = f32[32,1280]{1,0:T(8,128)S(1)} collective-permute-done((f32[32,1280]{1,0:T(8,128)S(1)}, f32[32,1280]{1,0:T(8,128)S(1)}, u32[]{:S(2)}, u32[]{:S(2)}) %collective-permute-start.12) | collective-permute-done | bytes 163872 | tf_op jit(solution)/shard_map/ppermute | solution.py:126
  105.8 2.0 %collective-permute-done.10 = f32[32,1280]{1,0:T(8,128)S(1)} collective-permute-done((f32[32,1280]{1,0:T(8,128)S(1)}, f32[32,1280]{1,0:T(8,128)S(1)}, u32[]{:S(2)}, u32[]{:S(2)}) %collective-permute-start.10) | collective-permute-done | bytes 163872 | tf_op jit(solution)/shard_map/ppermute | solution.py:126
  108.0 17.5 %all_to_all.10 = f32[32,8,128]{2,1,0:T(8,128)S(1)} all-to-all(f32[32,8,128]{2,1,0:T(8,128)S(1)} %broadcast_in_dim.4), channel_id=1, replica_groups=mesh['z'=8,'x'=4,'c'=2,'y'=4] {'z','x'}, dimensions={0} | all-to-all | bytes 262144 | tf_op jit(solution)/shard_map/all_to_all | solution.py:135
  125.5 8.7 %all_to_all.11 = f32[8,8,128]{2,1,0:T(8,128)S(1)} all-to-all(f32[8,8,128]{2,1,0:T(8,128)S(1)} %broadcast_in_dim.5), channel_id=1, replica_groups=mesh['z'=8,'x'=4,'c'=2,'y'=4] {'c','y'}, dimensions={0} | all-to-all | bytes 65536 | tf_op jit(solution)/shard_map/all_to_all | solution.py:135
  136.6 9.1 %psum.7 = f32[2,32]{1,0:T(2,128)S(1)} all-reduce(f32[2,32]{1,0:T(2,128)S(1)} %pad_maximum_fusion), channel_id=1, replica_groups=mesh['z'=8,'x'=4,'c'=2,'y'=4] {'y'}, use_global_device_ids=true, to_apply=%region_5.0 | all-reduce | flops 64 | bytes 512 | tf_op jit(solution)/shard_map/psum | solution.py:202
  (71 shorter events, 15.6 us)
Async XLA Ops:
  6.7 3.0 %collective-permute-start = (f32[4,32,1280]{2,1,0:T(8,128)S(1)}, f32[4,32,1280]{2,1,0:T(8,128)S(1)}, u32[]{:S(2)}, u32[]{:S(2)}) collective-permute-start(f32[4,32,1280]{2,1,0:T(8,128)S(1)} %get-tuple-element.24), channel_id=1, source_target_pairs={{0,4},{4,0},{1,5},{5,1},{2,6},{6,2},{3,7},{7,3},{8,12},{12,8},{9,1... | collective-permute-start | bytes 1966088 | tf_op jit(solution)/shard_map/ppermute | solution.py:116
  9.1 15.2 %collective-permute-start.1 = (f32[8,32,1280]{2,1,0:T(8,128)S(1)}, f32[8,32,1280]{2,1,0:T(8,128)S(1)}, u32[]{:S(2)}, u32[]{:S(2)}) collective-permute-start(f32[8,32,1280]{2,1,0:T(8,128)S(1)} %get-tuple-element.27), channel_id=1, source_target_pairs={{0,4},{4,0},{1,5},{5,1},{2,6},{6,2},{3,7},{7,3},{8,12},{12,8},{9,1... | collective-permute-start | bytes 3932168 | tf_op jit(solution)/shard_map/ppermute | solution.py:116
  9.8 14.5 %collective-permute-start.2 = (f32[4,32,1280]{2,1,0:T(8,128)S(1)}, f32[4,32,1280]{2,1,0:T(8,128)S(1)}, u32[]{:S(2)}, u32[]{:S(2)}) collective-permute-start(f32[4,32,1280]{2,1,0:T(8,128)S(1)} %add.108), channel_id=1, source_target_pairs={{0,32},{4,228},{32,64},{36,4},{64,96},{68,36},{96,128},{100,68},{1... | collective-permute-start | bytes 1966088 | tf_op jit(solution)/shard_map/ppermute | solution.py:121
  18.1 6.4 %collective-permute-start.3 = (f32[8,32,768]{2,1,0:T(8,128)S(1)}, f32[8,32,768]{2,1,0:T(8,128)S(1)}, u32[]{:S(2)}, u32[]{:S(2)}) collective-permute-start(f32[8,32,768]{2,1,0:T(8,128)S(1)} %get-tuple-element.30), channel_id=1, source_target_pairs={{0,4},{4,0},{1,5},{5,1},{2,6},{6,2},{3,7},{7,3},{8,12},{12,8},{9,1... | collective-permute-start | bytes 2359304 | tf_op jit(solution)/shard_map/ppermute | solution.py:116
  24.6 19.4 %collective-permute-start.13 = (f32[24,32,768]{2,1,0:T(8,128)S(1)}, f32[24,32,768]{2,1,0:T(8,128)S(1)}, u32[]{:S(2)}, u32[]{:S(2)}) collective-permute-start(f32[24,32,768]{2,1,0:T(8,128)S(1)} %get-tuple-element.38), channel_id=1, source_target_pairs={{0,4},{4,0},{1,5},{5,1},{2,6},{6,2},{3,7},{7,3},{8,12},{12,8},{9,1... | collective-permute-start | bytes 7077896 | tf_op jit(solution)/shard_map/ppermute | solution.py:116
  24.7 18.9 %collective-permute-start.6 = (f32[8,32,1280]{2,1,0:T(8,128)S(1)}, f32[8,32,1280]{2,1,0:T(8,128)S(1)}, u32[]{:S(2)}, u32[]{:S(2)}) collective-permute-start(f32[8,32,1280]{2,1,0:T(8,128)S(1)} %pad_add_fusion), channel_id=1, source_target_pairs={{0,32},{4,228},{32,64},{36,4},{64,96},{68,36},{96,128},{100,68},{1... | collective-permute-start | bytes 3932168 | tf_op jit(solution)/shard_map/ppermute | solution.py:121
  27.1 16.5 %collective-permute-start.5 = (f32[8,32,1280]{2,1,0:T(8,128)S(1)}, f32[8,32,1280]{2,1,0:T(8,128)S(1)}, u32[]{:S(2)}, u32[]{:S(2)}) collective-permute-start(f32[8,32,1280]{2,1,0:T(8,128)S(1)} %get-tuple-element.35), channel_id=1, source_target_pairs={{0,4},{4,0},{1,5},{5,1},{2,6},{6,2},{3,7},{7,3},{8,12},{12,8},{9,1... | collective-permute-start | bytes 3932168 | tf_op jit(solution)/shard_map/ppermute | solution.py:116
  29.3 15.0 %collective-permute-start.14 = (f32[8,32,768]{2,1,0:T(8,128)S(1)}, f32[8,32,768]{2,1,0:T(8,128)S(1)}, u32[]{:S(2)}, u32[]{:S(2)}) collective-permute-start(f32[8,32,768]{2,1,0:T(8,128)S(1)} %add.111), channel_id=1, source_target_pairs={{0,8},{4,28},{8,16},{12,4},{16,24},{20,12},{24,0},{28,20},{1,9},{5... | collective-permute-start | bytes 2359304 | tf_op jit(solution)/shard_map/ppermute | solution.py:121
  33.9 12.1 %collective-permute-start.4 = (f32[12,32,1280]{2,1,0:T(8,128)S(1)}, f32[12,32,1280]{2,1,0:T(8,128)S(1)}, u32[]{:S(2)}, u32[]{:S(2)}) collective-permute-start(f32[12,32,1280]{2,1,0:T(8,128)S(1)} %get-tuple-element.34), channel_id=1, source_target_pairs={{0,4},{4,0},{1,5},{5,1},{2,6},{6,2},{3,7},{7,3},{8,12},{12,8},{9,1... | collective-permute-start | bytes 5898248 | tf_op jit(solution)/shard_map/ppermute | solution.py:116
  43.9 18.9 %collective-permute-start.7 = (f32[8,32,1280]{2,1,0:T(8,128)S(1)}, f32[8,32,1280]{2,1,0:T(8,128)S(1)}, u32[]{:S(2)}, u32[]{:S(2)}) collective-permute-start(f32[8,32,1280]{2,1,0:T(8,128)S(1)} %add_add_fusion), channel_id=1, source_target_pairs={{0,32},{4,228},{32,64},{36,4},{64,96},{68,36},{96,128},{100,68},{1... | collective-permute-start | bytes 3932168 | tf_op jit(solution)/shard_map/ppermute | solution.py:121
  44.5 21.7 %collective-permute-start.15 = (f32[16,32,768]{2,1,0:T(8,128)S(1)}, f32[16,32,768]{2,1,0:T(8,128)S(1)}, u32[]{:S(2)}, u32[]{:S(2)}) collective-permute-start(f32[16,32,768]{2,1,0:T(8,128)S(1)} %slice_add_fusion), channel_id=1, source_target_pairs={{0,8},{4,28},{8,16},{12,4},{16,24},{20,12},{24,0},{28,20},{1,9},{5... | collective-permute-start | bytes 4718600 | tf_op jit(solution)/shard_map/ppermute | solution.py:121
  62.9 18.9 %collective-permute-start.8 = (f32[8,32,1280]{2,1,0:T(8,128)S(1)}, f32[8,32,1280]{2,1,0:T(8,128)S(1)}, u32[]{:S(2)}, u32[]{:S(2)}) collective-permute-start(f32[8,32,1280]{2,1,0:T(8,128)S(1)} %slice_add_fusion.1), channel_id=1, source_target_pairs={{0,32},{4,228},{32,64},{36,4},{64,96},{68,36},{96,128},{100,68},{1... | collective-permute-start | bytes 3932168 | tf_op jit(solution)/shard_map/ppermute | solution.py:121
  66.2 2.4 %collective-permute-start.16 = (f32[8,32,768]{2,1,0:T(8,128)S(1)}, f32[8,32,768]{2,1,0:T(8,128)S(1)}, u32[]{:S(2)}, u32[]{:S(2)}) collective-permute-start(f32[8,32,768]{2,1,0:T(8,128)S(1)} %slice.94), channel_id=1, source_target_pairs={{0,4},{4,0},{1,5},{5,1},{2,6},{6,2},{3,7},{7,3},{8,12},{12,8},{9,1... | collective-permute-start | bytes 2359304 | tf_op jit(solution)/shard_map/ppermute | solution.py:116
  68.8 14.1 %collective-permute-start.17 = (f32[1,32,768]{2,1,0:T(8,128)S(1)}, f32[1,32,768]{2,1,0:T(8,128)S(1)}, u32[]{:S(2)}, u32[]{:S(2)}) collective-permute-start(f32[1,32,768]{2,1,0:T(8,128)S(1)} %slice.99), channel_id=1, source_target_pairs={{0,32},{4,228},{32,64},{36,4},{64,96},{68,36},{96,128},{100,68},{1... | collective-permute-start | bytes 294920 | tf_op jit(solution)/shard_map/ppermute | solution.py:121
  81.8 8.1 %collective-permute-start.9 = (f32[4,32,1280]{2,1,0:T(8,128)S(1)}, f32[4,32,1280]{2,1,0:T(8,128)S(1)}, u32[]{:S(2)}, u32[]{:S(2)}) collective-permute-start(f32[4,32,1280]{2,1,0:T(8,128)S(1)} %slice.86), channel_id=1, source_target_pairs={{0,4},{4,0},{1,5},{5,1},{2,6},{6,2},{3,7},{7,3},{8,12},{12,8},{9,1... | collective-permute-start | bytes 1966088 | tf_op jit(solution)/shard_map/ppermute | solution.py:116
  82.9 7.0 %collective-permute-start.18 = (f32[2,32,768]{2,1,0:T(8,128)S(1)}, f32[2,32,768]{2,1,0:T(8,128)S(1)}, u32[]{:S(2)}, u32[]{:S(2)}) collective-permute-start(f32[2,32,768]{2,1,0:T(8,128)S(1)} %slice_add_fusion.6), channel_id=1, source_target_pairs={{0,32},{4,228},{32,64},{36,4},{64,96},{68,36},{96,128},{100,68},{1... | collective-permute-start | bytes 589832 | tf_op jit(solution)/shard_map/ppermute | solution.py:121
  89.9 7.0 %collective-permute-start.19 = (f32[2,32,768]{2,1,0:T(8,128)S(1)}, f32[2,32,768]{2,1,0:T(8,128)S(1)}, u32[]{:S(2)}, u32[]{:S(2)}) collective-permute-start(f32[2,32,768]{2,1,0:T(8,128)S(1)} %slice_add_fusion.7), channel_id=1, source_target_pairs={{0,32},{4,228},{32,64},{36,4},{64,96},{68,36},{96,128},{100,68},{1... | collective-permute-start | bytes 589832 | tf_op jit(solution)/shard_map/ppermute | solution.py:121
  96.9 7.0 %collective-permute-start.20 = (f32[2,32,768]{2,1,0:T(8,128)S(1)}, f32[2,32,768]{2,1,0:T(8,128)S(1)}, u32[]{:S(2)}, u32[]{:S(2)}) collective-permute-start(f32[2,32,768]{2,1,0:T(8,128)S(1)} %slice_add_fusion.8), channel_id=1, source_target_pairs={{0,32},{4,228},{32,64},{36,4},{64,96},{68,36},{96,128},{100,68},{1... | collective-permute-start | bytes 589832 | tf_op jit(solution)/shard_map/ppermute | solution.py:121
  97.0 38.5 %copy-start.3 = (f32[32,2048]{1,0:T(8,128)S(1)}, f32[32,2048]{1,0:T(8,128)}, u32[]{:S(2)}) copy-start(f32[32,2048]{1,0:T(8,128)} %param.9) | copy-start | bytes 786436
  97.0 38.5 %copy-start.4 = (f32[32,2048]{1,0:T(8,128)S(1)}, f32[32,2048]{1,0:T(8,128)}, u32[]{:S(2)}) copy-start(f32[32,2048]{1,0:T(8,128)} %param.11) | copy-start | bytes 786436
  97.0 7.0 %collective-permute-start.11 = (f32[32,1280]{1,0:T(8,128)S(1)}, f32[32,1280]{1,0:T(8,128)S(1)}, u32[]{:S(2)}, u32[]{:S(2)}) collective-permute-start(f32[32,1280]{1,0:T(8,128)S(1)} %get-tuple-element.43), channel_id=1, source_target_pairs={{0,16},{8,24},{16,0},{24,8},{1,17},{9,25},{17,1},{25,9},{2,18},{10... | collective-permute-start | bytes 491528 | tf_op jit(solution)/shard_map/ppermute | solution.py:126
  100.1 5.6 %collective-permute-start.12 = (f32[32,1280]{1,0:T(8,128)S(1)}, f32[32,1280]{1,0:T(8,128)S(1)}, u32[]{:S(2)}, u32[]{:S(2)}) collective-permute-start(f32[32,1280]{1,0:T(8,128)S(1)} %get-tuple-element.44), channel_id=1, source_target_pairs={{0,24},{8,0},{16,8},{24,16},{1,25},{9,1},{17,9},{25,17},{2,26},{10... | collective-permute-start | bytes 491528 | tf_op jit(solution)/shard_map/ppermute | solution.py:126
  101.3 6.5 %collective-permute-start.10 = (f32[32,1280]{1,0:T(8,128)S(1)}, f32[32,1280]{1,0:T(8,128)S(1)}, u32[]{:S(2)}, u32[]{:S(2)}) collective-permute-start(f32[32,1280]{1,0:T(8,128)S(1)} %get-tuple-element.45), channel_id=1, source_target_pairs={{0,8},{8,16},{16,24},{24,0},{1,9},{9,17},{17,25},{25,1},{2,10},{10... | collective-permute-start | bytes 491528 | tf_op jit(solution)/shard_map/ppermute | solution.py:126
  103.8 4.0 %collective-permute-start.21 = (f32[32,768]{1,0:T(8,128)S(1)}, f32[32,768]{1,0:T(8,128)S(1)}, u32[]{:S(2)}, u32[]{:S(2)}) collective-permute-start(f32[32,768]{1,0:T(8,128)S(1)} %slice_bitcast_fusion.5), channel_id=1, source_target_pairs={{0,4},{4,0},{1,5},{5,1},{2,6},{6,2},{3,7},{7,3},{8,12},{12,8},{9,1... | collective-permute-start | bytes 294920 | tf_op jit(solution)/shard_map/ppermute | solution.py:116
  (4 other events, 53.9 us)

commit v4 on v3

--- a/solution.py
+++ b/solution.py
@@ -15,7 +15,7 @@
 DP = ("z", "x", "c")
 NZ, NX = 8, 4
 SIZE = {"z": NZ, "x": NX}
-COLS_Z = 1280
+COLS_Z = 1152
 
 
 def dot(lhs_ref, rhs_ref, z, start, cols):
@@ -187,12 +187,12 @@
     moving = onward(sum_x[6:7], "z")
     moving = onward(add(sum_x[4:6], moving), "z")
     moving = onward(sum_x[2:4] + moving, "z")
-    moving = onward(sum_x[0:2] + moving, "z")
+    moving = onward(sum_x[0:2] + after(moving, batch_z), "z")
     batch_x = moving[0] + other_core(moving[1]) + sum_x[7]
     gradient = grad_acc + jnp.concatenate([batch_z, batch_x], axis=1)
 
     energy = jnp.sum((gradient * gradient).reshape(4, 8, 16, 128), axis=(0, 2))
-    energy = sum_over(sum_over(energy, ("z", "x"), NZ * NX), ("c", "y"), 8)
+    energy = sum_over(sum_over(energy, ("z", "c"), 16), ("x", "y"), 16)
     divisor = jnp.sqrt(jnp.sum(energy) / entry_count + epsilon)
     clipped = gradient / divisor
     moment_new = beta_first * moment_m + (1.0 - beta_first) * clipped

time: 147 us -> 147 us (level)
    ppermute x9, waiting for transfers between devices: 2.29 us -> 4.26 us  [other_core(): return lax.ppermute(value, 'c', [(0, 1), (1, 0)])]
  transfers between devices with their start and end apart: 22 -> 22, of which waited for: 13 -> 15; matrix products, arithmetic and copies ran while one was open for 1% -> 1% of each run, Pallas kernels for 10% -> 10%
where the time goes in v4:
time: 147 us; the launch traced here: 146 us
  waiting for transfers between devices  66 us (45%)
  blocking collectives  34.8 us (24%)
  starting transfers between devices  18.2 us (12%)
  Pallas kernels  16.5 us (11%)
  other arithmetic  4.76 us (3%)
  local copies, waits for them, and re-layouts  4.58 us (3%)
  between operations  1.63 us (1%)
    ppermute x10, waiting for transfers between devices, onward(): lax.ppermute(value, (axis, 'c'), [(2 * i + c, 2 * ((i + 1 - 2 * c) % n) +...  58.4 us
    all_to_all x2, blocking collectives, sum_over(): return jnp.sum(lax.all_to_all(copies, axes, 0, 0, tiled=True), axis=0)  25.6 us
    pallas_call x5, Pallas kernels, product(): pl.pallas_call(kernel, in_specs=[pl.BlockSpec(memory_space=pltpu.SMEM), V...  16.5 us
    psum x1, blocking collectives, shards(): norms = jnp.sqrt(lax.psum(squares, 'y'))  9.19 us
    ppermute x9, starting transfers between devices, other_core(): return lax.ppermute(value, 'c', [(0, 1), (1, 0)])  7.49 us
    ppermute x10, starting transfers between devices, onward(): lax.ppermute(value, (axis, 'c'), [(2 * i + c, 2 * ((i + 1 - 2 * c) % n) +...  5.59 us
    ppermute x3, starting transfers between devices, shift(): return lax.ppermute(value, axis, [(i, (i + by) % n) for i in range(n)])  5.1 us
    unnamed x12, local copies, waits for them, and re-layouts  4.4 us
  transfers between devices with their start and end apart: 22, of which 15 were waited for; matrix products, arithmetic and copies ran while one was open for 1% of the time, Pallas kernels for 10%

profile of v4, /device:TPU:8, one launch (start us, length us, event | category | flops | bytes accessed | tf_op | source)
XLA Modules:
  0.0 146.4 jit_solution(640130140112453017)
XLA Ops:
  0.7 2.2 %copy-done = bf16[1024,2048]{1,0:T(8,128)(2,1)S(1)} copy-done((bf16[1024,2048]{1,0:T(8,128)(2,1)S(1)}, bf16[1024,2048]{1,0:T(8,128)(2,1)}, u32[]{:S(2)}) %copy-start) | copy-done | bytes 4194328
  2.9 2.2 %copy-done.1 = bf16[1024,2048]{1,0:T(8,128)(2,1)S(1)} copy-done((bf16[1024,2048]{1,0:T(8,128)(2,1)S(1)}, bf16[1024,2048]{1,0:T(8,128)(2,1)}, u32[]{:S(2)}) %copy-start.1) | copy-done | bytes 4194328
  5.1 1.5 %shard_map.85 = (f32[4,32,1152]{2,1,0:T(8,128)S(1)}, f32[4,32,1152]{2,1,0:T(8,128)S(1)}) custom-call(s32[3]{0:T(128)S(1)} %pad_add_fusion.1.where_ref, bf16[1024,2048]{1,0:T(8,128)(2,1)S(1)} %copy-done, bf16[1024,2048]{1,0:T(8,128)(2,1)S(1)} %copy-done.1), custom_call_target="tpu_custom_call" | custom-call | flops 294912 | bytes 256 | tf_op jit(solution)/shard_map/pallas_call | solution.py:100
  6.7 2.3 %shard_map.86 = (f32[8,32,1152]{2,1,0:T(8,128)S(1)}, f32[8,32,1152]{2,1,0:T(8,128)S(1)}) custom-call(s32[3]{0:T(128)S(1)} %pad_add_fusion.1.where_ref, bf16[1024,2048]{1,0:T(8,128)(2,1)S(1)} %copy-done, bf16[1024,2048]{1,0:T(8,128)(2,1)S(1)} %copy-done.1), custom_call_target="tpu_custom_call" | custom-call | flops 589824 | bytes 512 | tf_op jit(solution)/shard_map/pallas_call | solution.py:100
  9.7 2.0 %collective-permute-start.2 = (f32[4,32,1152]{2,1,0:T(8,128)S(1)}, f32[4,32,1152]{2,1,0:T(8,128)S(1)}, u32[]{:S(2)}, u32[]{:S(2)}) collective-permute-start(f32[4,32,1152]{2,1,0:T(8,128)S(1)} %add.108), channel_id=1, source_target_pairs={{0,32},{4,228},{32,64},{36,4},{64,96},{68,36},{96,128},{100,68},{1... | collective-permute-start | bytes 1769480 | tf_op jit(solution)/shard_map/ppermute | solution.py:121
  11.7 7.3 %shard_map.87 = (f32[8,32,896]{2,1,0:T(8,128)S(1)}, f32[8,32,896]{2,1,0:T(8,128)S(1)}, f32[24,32,896]{2,1,0:T(8,128)S(1)}, f32[24,32,896]{2,1,0:T(8,128)S(1)}) custom-call(s32[3]{0:T(128)S(1)} %pad_add_fusion.1.where_ref, bf16[1024,2048]{1,0:T(8,128)(2,1)S(1)} %copy-done, bf16[1024,2048]{1,0:T(8,128)(2,1)S(1)} %copy-done.1), custom_call_target="tpu_custom_call" | custom-call | flops 1835008 | bytes 2048 | tf_op jit(solution)/shard_map/pallas_call | solution.py:100
  19.0 3.8 %collective-permute-start.3 = (f32[8,32,896]{2,1,0:T(8,128)S(1)}, f32[8,32,896]{2,1,0:T(8,128)S(1)}, u32[]{:S(2)}, u32[]{:S(2)}) collective-permute-start(f32[8,32,896]{2,1,0:T(8,128)S(1)} %get-tuple-element.31), channel_id=1, source_target_pairs={{0,4},{4,0},{1,5},{5,1},{2,6},{6,2},{3,7},{7,3},{8,12},{12,8},{9,1... | collective-permute-start | bytes 2752520 | tf_op jit(solution)/shard_map/ppermute | solution.py:116
  25.5 2.3 %shard_map.88 = (f32[8,32,1152]{2,1,0:T(8,128)S(1)}, f32[8,32,1152]{2,1,0:T(8,128)S(1)}) custom-call(s32[3]{0:T(128)S(1)} %pad_add_fusion.1.where_ref, bf16[1024,2048]{1,0:T(8,128)(2,1)S(1)} %copy-done, bf16[1024,2048]{1,0:T(8,128)(2,1)S(1)} %copy-done.1), custom_call_target="tpu_custom_call" | custom-call | flops 589824 | bytes 512 | tf_op jit(solution)/shard_map/pallas_call | solution.py:100
  30.2 3.1 %shard_map.89 = (f32[12,32,1152]{2,1,0:T(8,128)S(1)}, f32[12,32,1152]{2,1,0:T(8,128)S(1)}) custom-call(s32[3]{0:T(128)S(1)} %pad_add_fusion.1.where_ref, bf16[1024,2048]{1,0:T(8,128)(2,1)S(1)} %copy-done, bf16[1024,2048]{1,0:T(8,128)(2,1)S(1)} %copy-done.1), custom_call_target="tpu_custom_call" | custom-call | flops 884736 | bytes 768 | tf_op jit(solution)/shard_map/pallas_call | solution.py:100
  34.7 8.2 %collective-permute-done.6 = f32[8,32,1152]{2,1,0:T(8,128)S(1)} collective-permute-done((f32[8,32,1152]{2,1,0:T(8,128)S(1)}, f32[8,32,1152]{2,1,0:T(8,128)S(1)}, u32[]{:S(2)}, u32[]{:S(2)}) %collective-permute-start.6) | collective-permute-done | bytes 1179680 | tf_op jit(solution)/shard_map/ppermute | solution.py:121
  43.8 1.6 %collective-permute-start.15 = (f32[16,32,896]{2,1,0:T(8,128)S(1)}, f32[16,32,896]{2,1,0:T(8,128)S(1)}, u32[]{:S(2)}, u32[]{:S(2)}) collective-permute-start(f32[16,32,896]{2,1,0:T(8,128)S(1)} %slice_add_fusion), channel_id=1, source_target_pairs={{0,8},{4,28},{8,16},{12,4},{16,24},{20,12},{24,0},{28,20},{1,9},{5... | collective-permute-start | bytes 5505032 | tf_op jit(solution)/shard_map/ppermute | solution.py:121
  45.7 15.0 %collective-permute-done.7 = f32[8,32,1152]{2,1,0:T(8,128)S(1)} collective-permute-done((f32[8,32,1152]{2,1,0:T(8,128)S(1)}, f32[8,32,1152]{2,1,0:T(8,128)S(1)}, u32[]{:S(2)}, u32[]{:S(2)}) %collective-permute-start.7) | collective-permute-done | bytes 1179680 | tf_op jit(solution)/shard_map/ppermute | solution.py:121
  60.9 7.5 %collective-permute-done.15 = f32[16,32,896]{2,1,0:T(8,128)S(1)} collective-permute-done((f32[16,32,896]{2,1,0:T(8,128)S(1)}, f32[16,32,896]{2,1,0:T(8,128)S(1)}, u32[]{:S(2)}, u32[]{:S(2)}) %collective-permute-start.15) | collective-permute-done | bytes 1835040 | tf_op jit(solution)/shard_map/ppermute | solution.py:121
  68.5 9.8 %collective-permute-done.8 = f32[8,32,1152]{2,1,0:T(8,128)S(1)} collective-permute-done((f32[8,32,1152]{2,1,0:T(8,128)S(1)}, f32[8,32,1152]{2,1,0:T(8,128)S(1)}, u32[]{:S(2)}, u32[]{:S(2)}) %collective-permute-start.8) | collective-permute-done | bytes 1179680 | tf_op jit(solution)/shard_map/ppermute | solution.py:121
  78.7 1.7 %collective-permute-done.9 = f32[4,32,1152]{2,1,0:T(8,128)S(1)} collective-permute-done((f32[4,32,1152]{2,1,0:T(8,128)S(1)}, f32[4,32,1152]{2,1,0:T(8,128)S(1)}, u32[]{:S(2)}, u32[]{:S(2)}) %collective-permute-start.9) | collective-permute-done | bytes 589856 | tf_op jit(solution)/shard_map/ppermute | solution.py:116
  80.6 4.2 %collective-permute-done.17 = f32[1,32,896]{2,1,0:T(8,128)S(1)} collective-permute-done((f32[1,32,896]{2,1,0:T(8,128)S(1)}, f32[1,32,896]{2,1,0:T(8,128)S(1)}, u32[]{:S(2)}, u32[]{:S(2)}) %collective-permute-start.17) | collective-permute-done | bytes 114720 | tf_op jit(solution)/shard_map/ppermute | solution.py:121
  84.9 3.1 %collective-permute-start.11 = (f32[32,1152]{1,0:T(8,128)S(1)}, f32[32,1152]{1,0:T(8,128)S(1)}, u32[]{:S(2)}, u32[]{:S(2)}) collective-permute-start(f32[32,1152]{1,0:T(8,128)S(1)} %get-tuple-element.45), channel_id=1, source_target_pairs={{0,16},{8,24},{16,0},{24,8},{1,17},{9,25},{17,1},{25,9},{2,18},{10... | collective-permute-start | bytes 442376 | tf_op jit(solution)/shard_map/ppermute | solution.py:126
  90.0 2.1 %collective-permute-done.18 = f32[2,32,896]{2,1,0:T(8,128)S(1)} collective-permute-done((f32[2,32,896]{2,1,0:T(8,128)S(1)}, f32[2,32,896]{2,1,0:T(8,128)S(1)}, u32[]{:S(2)}, u32[]{:S(2)}) %collective-permute-start.18) | collective-permute-done | bytes 229408 | tf_op jit(solution)/shard_map/ppermute | solution.py:121
  93.0 1.8 %collective-permute-done.12 = f32[32,1152]{1,0:T(8,128)S(1)} collective-permute-done((f32[32,1152]{1,0:T(8,128)S(1)}, f32[32,1152]{1,0:T(8,128)S(1)}, u32[]{:S(2)}, u32[]{:S(2)}) %collective-permute-start.12) | collective-permute-done | bytes 147488 | tf_op jit(solution)/shard_map/ppermute | solution.py:126
  95.6 3.8 %collective-permute-done.19 = f32[2,32,896]{2,1,0:T(8,128)S(1)} collective-permute-done((f32[2,32,896]{2,1,0:T(8,128)S(1)}, f32[2,32,896]{2,1,0:T(8,128)S(1)}, u32[]{:S(2)}, u32[]{:S(2)}) %collective-permute-start.19) | collective-permute-done | bytes 229408 | tf_op jit(solution)/shard_map/ppermute | solution.py:121
  99.6 7.2 %collective-permute-done.20 = f32[2,32,896]{2,1,0:T(8,128)S(1)} collective-permute-done((f32[2,32,896]{2,1,0:T(8,128)S(1)}, f32[2,32,896]{2,1,0:T(8,128)S(1)}, u32[]{:S(2)}, u32[]{:S(2)}) %collective-permute-start.20) | collective-permute-done | bytes 229408 | tf_op jit(solution)/shard_map/ppermute | solution.py:121
  108.3 12.1 %all_to_all.10 = f32[16,8,128]{2,1,0:T(8,128)S(1)} all-to-all(f32[16,8,128]{2,1,0:T(8,128)S(1)} %broadcast_in_dim.4), channel_id=1, replica_groups=mesh['z'=8,'x'=4,'c'=2,'y'=4] {'z','c'}, dimensions={0} | all-to-all | bytes 131072 | tf_op jit(solution)/shard_map/all_to_all | solution.py:135
  120.4 13.5 %all_to_all.11 = f32[16,8,128]{2,1,0:T(8,128)S(1)} all-to-all(f32[16,8,128]{2,1,0:T(8,128)S(1)} %broadcast_in_dim.5), channel_id=1, replica_groups=mesh['z'=8,'x'=4,'c'=2,'y'=4] {'x','y'}, dimensions={0} | all-to-all | bytes 131072 | tf_op jit(solution)/shard_map/all_to_all | solution.py:135
  136.4 9.2 %psum.7 = f32[2,32]{1,0:T(2,128)S(1)} all-reduce(f32[2,32]{1,0:T(2,128)S(1)} %pad_maximum_fusion), channel_id=1, replica_groups=mesh['z'=8,'x'=4,'c'=2,'y'=4] {'y'}, use_global_device_ids=true, to_apply=%region_5.0 | all-reduce | flops 64 | bytes 512 | tf_op jit(solution)/shard_map/psum | solution.py:202
  (71 shorter events, 17.4 us)
Async XLA Ops:
  6.6 3.0 %collective-permute-start = (f32[4,32,1152]{2,1,0:T(8,128)S(1)}, f32[4,32,1152]{2,1,0:T(8,128)S(1)}, u32[]{:S(2)}, u32[]{:S(2)}) collective-permute-start(f32[4,32,1152]{2,1,0:T(8,128)S(1)} %get-tuple-element.25), channel_id=1, source_target_pairs={{0,4},{4,0},{1,5},{5,1},{2,6},{6,2},{3,7},{7,3},{8,12},{12,8},{9,1... | collective-permute-start | bytes 1769480 | tf_op jit(solution)/shard_map/ppermute | solution.py:116
  9.0 14.4 %collective-permute-start.1 = (f32[8,32,1152]{2,1,0:T(8,128)S(1)}, f32[8,32,1152]{2,1,0:T(8,128)S(1)}, u32[]{:S(2)}, u32[]{:S(2)}) collective-permute-start(f32[8,32,1152]{2,1,0:T(8,128)S(1)} %get-tuple-element.28), channel_id=1, source_target_pairs={{0,4},{4,0},{1,5},{5,1},{2,6},{6,2},{3,7},{7,3},{8,12},{12,8},{9,1... | collective-permute-start | bytes 3538952 | tf_op jit(solution)/shard_map/ppermute | solution.py:116
  9.7 13.8 %collective-permute-start.2 = (f32[4,32,1152]{2,1,0:T(8,128)S(1)}, f32[4,32,1152]{2,1,0:T(8,128)S(1)}, u32[]{:S(2)}, u32[]{:S(2)}) collective-permute-start(f32[4,32,1152]{2,1,0:T(8,128)S(1)} %add.108), channel_id=1, source_target_pairs={{0,32},{4,228},{32,64},{36,4},{64,96},{68,36},{96,128},{100,68},{1... | collective-permute-start | bytes 1769480 | tf_op jit(solution)/shard_map/ppermute | solution.py:121
  19.0 5.9 %collective-permute-start.3 = (f32[8,32,896]{2,1,0:T(8,128)S(1)}, f32[8,32,896]{2,1,0:T(8,128)S(1)}, u32[]{:S(2)}, u32[]{:S(2)}) collective-permute-start(f32[8,32,896]{2,1,0:T(8,128)S(1)} %get-tuple-element.31), channel_id=1, source_target_pairs={{0,4},{4,0},{1,5},{5,1},{2,6},{6,2},{3,7},{7,3},{8,12},{12,8},{9,1... | collective-permute-start | bytes 2752520 | tf_op jit(solution)/shard_map/ppermute | solution.py:116
  25.0 18.2 %collective-permute-start.13 = (f32[24,32,896]{2,1,0:T(8,128)S(1)}, f32[24,32,896]{2,1,0:T(8,128)S(1)}, u32[]{:S(2)}, u32[]{:S(2)}) collective-permute-start(f32[24,32,896]{2,1,0:T(8,128)S(1)} %get-tuple-element.39), channel_id=1, source_target_pairs={{0,4},{4,0},{1,5},{5,1},{2,6},{6,2},{3,7},{7,3},{8,12},{12,8},{9,1... | collective-permute-start | bytes 8257544 | tf_op jit(solution)/shard_map/ppermute | solution.py:116
  25.5 17.4 %collective-permute-start.6 = (f32[8,32,1152]{2,1,0:T(8,128)S(1)}, f32[8,32,1152]{2,1,0:T(8,128)S(1)}, u32[]{:S(2)}, u32[]{:S(2)}) collective-permute-start(f32[8,32,1152]{2,1,0:T(8,128)S(1)} %pad_add_fusion), channel_id=1, source_target_pairs={{0,32},{4,228},{32,64},{36,4},{64,96},{68,36},{96,128},{100,68},{1... | collective-permute-start | bytes 3538952 | tf_op jit(solution)/shard_map/ppermute | solution.py:121
  27.8 15.1 %collective-permute-start.5 = (f32[8,32,1152]{2,1,0:T(8,128)S(1)}, f32[8,32,1152]{2,1,0:T(8,128)S(1)}, u32[]{:S(2)}, u32[]{:S(2)}) collective-permute-start(f32[8,32,1152]{2,1,0:T(8,128)S(1)} %get-tuple-element.36), channel_id=1, source_target_pairs={{0,4},{4,0},{1,5},{5,1},{2,6},{6,2},{3,7},{7,3},{8,12},{12,8},{9,1... | collective-permute-start | bytes 3538952 | tf_op jit(solution)/shard_map/ppermute | solution.py:116
  28.7 14.9 %collective-permute-start.14 = (f32[8,32,896]{2,1,0:T(8,128)S(1)}, f32[8,32,896]{2,1,0:T(8,128)S(1)}, u32[]{:S(2)}, u32[]{:S(2)}) collective-permute-start(f32[8,32,896]{2,1,0:T(8,128)S(1)} %add.111), channel_id=1, source_target_pairs={{0,8},{4,28},{8,16},{12,4},{16,24},{20,12},{24,0},{28,20},{1,9},{5... | collective-permute-start | bytes 2752520 | tf_op jit(solution)/shard_map/ppermute | solution.py:121
  33.3 12.1 %collective-permute-start.4 = (f32[12,32,1152]{2,1,0:T(8,128)S(1)}, f32[12,32,1152]{2,1,0:T(8,128)S(1)}, u32[]{:S(2)}, u32[]{:S(2)}) collective-permute-start(f32[12,32,1152]{2,1,0:T(8,128)S(1)} %get-tuple-element.35), channel_id=1, source_target_pairs={{0,4},{4,0},{1,5},{5,1},{2,6},{6,2},{3,7},{7,3},{8,12},{12,8},{9,1... | collective-permute-start | bytes 5308424 | tf_op jit(solution)/shard_map/ppermute | solution.py:116
  43.1 17.5 %collective-permute-start.7 = (f32[8,32,1152]{2,1,0:T(8,128)S(1)}, f32[8,32,1152]{2,1,0:T(8,128)S(1)}, u32[]{:S(2)}, u32[]{:S(2)}) collective-permute-start(f32[8,32,1152]{2,1,0:T(8,128)S(1)} %add_add_fusion), channel_id=1, source_target_pairs={{0,32},{4,228},{32,64},{36,4},{64,96},{68,36},{96,128},{100,68},{1... | collective-permute-start | bytes 3538952 | tf_op jit(solution)/shard_map/ppermute | solution.py:121
  43.8 24.5 %collective-permute-start.15 = (f32[16,32,896]{2,1,0:T(8,128)S(1)}, f32[16,32,896]{2,1,0:T(8,128)S(1)}, u32[]{:S(2)}, u32[]{:S(2)}) collective-permute-start(f32[16,32,896]{2,1,0:T(8,128)S(1)} %slice_add_fusion), channel_id=1, source_target_pairs={{0,8},{4,28},{8,16},{12,4},{16,24},{20,12},{24,0},{28,20},{1,9},{5... | collective-permute-start | bytes 5505032 | tf_op jit(solution)/shard_map/ppermute | solution.py:121
  60.8 17.5 %collective-permute-start.8 = (f32[8,32,1152]{2,1,0:T(8,128)S(1)}, f32[8,32,1152]{2,1,0:T(8,128)S(1)}, u32[]{:S(2)}, u32[]{:S(2)}) collective-permute-start(f32[8,32,1152]{2,1,0:T(8,128)S(1)} %slice_add_fusion.1), channel_id=1, source_target_pairs={{0,32},{4,228},{32,64},{36,4},{64,96},{68,36},{96,128},{100,68},{1... | collective-permute-start | bytes 3538952 | tf_op jit(solution)/shard_map/ppermute | solution.py:121
  68.4 10.0 %collective-permute-start.16 = (f32[8,32,896]{2,1,0:T(8,128)S(1)}, f32[8,32,896]{2,1,0:T(8,128)S(1)}, u32[]{:S(2)}, u32[]{:S(2)}) collective-permute-start(f32[8,32,896]{2,1,0:T(8,128)S(1)} %slice.94), channel_id=1, source_target_pairs={{0,4},{4,0},{1,5},{5,1},{2,6},{6,2},{3,7},{7,3},{8,12},{12,8},{9,1... | collective-permute-start | bytes 2752520 | tf_op jit(solution)/shard_map/ppermute | solution.py:116
  78.3 2.1 %collective-permute-start.9 = (f32[4,32,1152]{2,1,0:T(8,128)S(1)}, f32[4,32,1152]{2,1,0:T(8,128)S(1)}, u32[]{:S(2)}, u32[]{:S(2)}) collective-permute-start(f32[4,32,1152]{2,1,0:T(8,128)S(1)} %slice.86), channel_id=1, source_target_pairs={{0,4},{4,0},{1,5},{5,1},{2,6},{6,2},{3,7},{7,3},{8,12},{12,8},{9,1... | collective-permute-start | bytes 1769480 | tf_op jit(solution)/shard_map/ppermute | solution.py:116
  78.7 6.1 %collective-permute-start.17 = (f32[1,32,896]{2,1,0:T(8,128)S(1)}, f32[1,32,896]{2,1,0:T(8,128)S(1)}, u32[]{:S(2)}, u32[]{:S(2)}) collective-permute-start(f32[1,32,896]{2,1,0:T(8,128)S(1)} %slice.99), channel_id=1, source_target_pairs={{0,32},{4,228},{32,64},{36,4},{64,96},{68,36},{96,128},{100,68},{1... | collective-permute-start | bytes 344072 | tf_op jit(solution)/shard_map/ppermute | solution.py:121
  84.8 7.3 %collective-permute-start.18 = (f32[2,32,896]{2,1,0:T(8,128)S(1)}, f32[2,32,896]{2,1,0:T(8,128)S(1)}, u32[]{:S(2)}, u32[]{:S(2)}) collective-permute-start(f32[2,32,896]{2,1,0:T(8,128)S(1)} %slice_add_fusion.6), channel_id=1, source_target_pairs={{0,32},{4,228},{32,64},{36,4},{64,96},{68,36},{96,128},{100,68},{1... | collective-permute-start | bytes 688136 | tf_op jit(solution)/shard_map/ppermute | solution.py:121
  84.9 8.1 %collective-permute-start.11 = (f32[32,1152]{1,0:T(8,128)S(1)}, f32[32,1152]{1,0:T(8,128)S(1)}, u32[]{:S(2)}, u32[]{:S(2)}) collective-permute-start(f32[32,1152]{1,0:T(8,128)S(1)} %get-tuple-element.45), channel_id=1, source_target_pairs={{0,16},{8,24},{16,0},{24,8},{1,17},{9,25},{17,1},{25,9},{2,18},{10... | collective-permute-start | bytes 442376 | tf_op jit(solution)/shard_map/ppermute | solution.py:126
  88.0 6.8 %collective-permute-start.12 = (f32[32,1152]{1,0:T(8,128)S(1)}, f32[32,1152]{1,0:T(8,128)S(1)}, u32[]{:S(2)}, u32[]{:S(2)}) collective-permute-start(f32[32,1152]{1,0:T(8,128)S(1)} %get-tuple-element.46), channel_id=1, source_target_pairs={{0,24},{8,0},{16,8},{24,16},{1,25},{9,1},{17,9},{25,17},{2,26},{10... | collective-permute-start | bytes 442376 | tf_op jit(solution)/shard_map/ppermute | solution.py:126
  89.2 6.4 %collective-permute-start.10 = (f32[32,1152]{1,0:T(8,128)S(1)}, f32[32,1152]{1,0:T(8,128)S(1)}, u32[]{:S(2)}, u32[]{:S(2)}) collective-permute-start(f32[32,1152]{1,0:T(8,128)S(1)} %get-tuple-element.47), channel_id=1, source_target_pairs={{0,8},{8,16},{16,24},{24,0},{1,9},{9,17},{17,25},{25,1},{2,10},{10... | collective-permute-start | bytes 442376 | tf_op jit(solution)/shard_map/ppermute | solution.py:126
  92.1 7.3 %collective-permute-start.19 = (f32[2,32,896]{2,1,0:T(8,128)S(1)}, f32[2,32,896]{2,1,0:T(8,128)S(1)}, u32[]{:S(2)}, u32[]{:S(2)}) collective-permute-start(f32[2,32,896]{2,1,0:T(8,128)S(1)} %slice_add_fusion.7), channel_id=1, source_target_pairs={{0,32},{4,228},{32,64},{36,4},{64,96},{68,36},{96,128},{100,68},{1... | collective-permute-start | bytes 688136 | tf_op jit(solution)/shard_map/ppermute | solution.py:121
  95.5 39.7 %copy-start.3 = (f32[32,2048]{1,0:T(8,128)S(1)}, f32[32,2048]{1,0:T(8,128)}, u32[]{:S(2)}) copy-start(f32[32,2048]{1,0:T(8,128)} %param.9) | copy-start | bytes 786436
  95.6 39.7 %copy-start.4 = (f32[32,2048]{1,0:T(8,128)S(1)}, f32[32,2048]{1,0:T(8,128)}, u32[]{:S(2)}) copy-start(f32[32,2048]{1,0:T(8,128)} %param.11) | copy-start | bytes 786436
  99.5 7.3 %collective-permute-start.20 = (f32[2,32,896]{2,1,0:T(8,128)S(1)}, f32[2,32,896]{2,1,0:T(8,128)S(1)}, u32[]{:S(2)}, u32[]{:S(2)}) collective-permute-start(f32[2,32,896]{2,1,0:T(8,128)S(1)} %slice_add_fusion.8), channel_id=1, source_target_pairs={{0,32},{4,228},{32,64},{36,4},{64,96},{68,36},{96,128},{100,68},{1... | collective-permute-start | bytes 688136 | tf_op jit(solution)/shard_map/ppermute | solution.py:121
  106.8 1.4 collective-permute-start.21
  (4 other events, 60.2 us)

commit v5 on v4

--- a/solution.py
+++ b/solution.py
@@ -52,6 +52,34 @@
             at += 8
 
 
+def product_far_kernel(
+    cols, where_ref, lhs_hbm, rhs_hbm, lhs_ref, rhs_ref, keep_ref, send_ref, acc, lhs_sems, rhs_sems
+):
+    z, x, c = where_ref[0], where_ref[1], where_ref[2]
+    far = lax.rem(z + NZ // 2, NZ)
+
+    def bring(hbm, ref, part, sem):
+        copy = pltpu.make_async_copy(hbm.at[:, part], ref.at[:, part], sem)
+        copy.start()
+        return copy
+
+    first = bring(rhs_hbm, rhs_ref, pl.ds(0, cols), rhs_sems.at[0])
+    blocks = [
+        bring(lhs_hbm, lhs_ref, pl.ds(pl.multiple_of(lax.rem(far + k, NZ) * 256, 256), 256), lhs_sems.at[k])
+        for k in range(NZ)
+    ]
+    rest = bring(rhs_hbm, rhs_ref, pl.ds(cols, rhs_ref.shape[1] - cols), rhs_sems.at[1])
+    first.wait()
+    blocks[0].wait()
+    acc[...] = dot(lhs_ref, rhs_ref, far, 0, cols)
+    for ref, core in ((keep_ref, c), (send_ref, 1 - c)):
+        for i, (gx, gc) in enumerate(near_x(x, core)):
+            ref[i] = acc[pl.ds(pl.multiple_of(gx * 64 + gc * 32, 32), 32), :]
+    for block in blocks[1:]:
+        block.wait()
+    rest.wait()
+
+
 def product_x_kernel(start, cols, where_ref, lhs_ref, rhs_ref, keep2_ref, send2_ref, keep_ref, send_ref, acc):
     z, x, c = where_ref[0], where_ref[1], where_ref[2]
     s = 1 - 2 * c
@@ -108,6 +136,25 @@
     )(where, grad_out, attn_out)
 
 
+def product_far(where, grad_out, attn_out):
+    hbm = pl.BlockSpec(memory_space=pltpu.HBM)
+    return pl.pallas_call(
+        functools.partial(product_far_kernel, COLS_Z),
+        in_specs=[pl.BlockSpec(memory_space=pltpu.SMEM), hbm, hbm],
+        out_specs=[VMEM] * 4,
+        out_shape=[jax.ShapeDtypeStruct(v.shape, v.dtype) for v in (grad_out, attn_out)]
+        + [jax.ShapeDtypeStruct((4, 32, COLS_Z), jnp.float32)] * 2,
+        scratch_shapes=[
+            pltpu.VMEM((256, COLS_Z), jnp.float32),
+            pltpu.SemaphoreType.DMA((NZ,)),
+            pltpu.SemaphoreType.DMA((2,)),
+        ],
+        compiler_params=pltpu.CompilerParams(vmem_limit_bytes=VFAR),
+        cost_estimate=pl.CostEstimate(flops=COST * 256 * COLS_Z, bytes_accessed=COST * 256, transcendentals=0),
+    )(where, grad_out, attn_out)
+
+
+VFAR = 43 << 20
 VLIM = 24 << 20
 COST = 1
 
@@ -157,8 +204,8 @@
     def add(here, moving):
         return here + (moving if moving.shape == here.shape else at_front(moving, here.shape[0]))
 
-    pair4 = product_z(where, (4,))
-    pair4 = (pair4[0], other_core(pair4[1]))
+    grad_out, attn_out, keep4, send4 = product_far(where, grad_out, attn_out)
+    pair4 = (keep4, other_core(send4))
     pair3 = product_z(after(where, pair4[0]), (3,))
     pair3 = (pair3[0], other_core(pair3[1]))
     first_z = lax.optimization_barrier(both(pair4))
@@ -178,14 +225,16 @@
     z = onward(next_z, "z")
     for pair in (pair2, pair1):
         z = onward(add(both(pair)[:8], z), "z")
-    sum_z = z[:4] + other_core(z[4:]) + both(pair1)[8:12]
     x = onward(first_x, "x")
     x = onward(add(both(pair_x)[:16], x), "x")
     sum_x = x[:8] + other_core(x[8:]) + both(pair_x)[16:24]
 
+    moving = onward(sum_x[6:7], "z")
+    z = after(z, moving)
+    moving = add(sum_x[4:6], after(moving, z))
+    sum_z = z[:4] + other_core(after(z[4:], moving)) + both(pair1)[8:12]
     batch_z = sum_z[0] + sum(shift(sum_z[k], "x", k) for k in (1, 2, 3))
-    moving = onward(sum_x[6:7], "z")
-    moving = onward(add(sum_x[4:6], moving), "z")
+    moving = onward(moving, "z")
     moving = onward(sum_x[2:4] + moving, "z")
     moving = onward(sum_x[0:2] + after(moving, batch_z), "z")
     batch_x = moving[0] + other_core(moving[1]) + sum_x[7]

time: 147 us -> 142 us (0.966)
  local copies, waits for them, and re-layouts: 4.58 us -> 0.2 us
  starting transfers between devices: 18.2 us -> 14.5 us
  waiting for transfers between devices: 66 us -> 69 us
  Pallas kernels: 16.5 us -> 19 us
  blocking collectives: 34.8 us -> 32.9 us
    unnamed x12 -> x8, local copies, waits for them, and re-layouts: 4.4 us -> 0.02 us
    pallas_call x0 -> x1, Pallas kernels: none -> 4.07 us  [product_far(): pl.pallas_call(functools.partial(product_far_kernel, COLS_Z), in_specs=[p...]
    ppermute x9, waiting for transfers between devices: 4.26 us -> 6.69 us  [other_core(): return lax.ppermute(value, 'c', [(0, 1), (1, 0)])]
    ppermute x3, starting transfers between devices: 5.1 us -> 2.74 us  [shift(): return lax.ppermute(value, axis, [(i, (i + by) % n) for i in range(n)])]
    ppermute x3, waiting for transfers between devices: 3.3 us -> 5.59 us  [shift(): return lax.ppermute(value, axis, [(i, (i + by) % n) for i in range(n)])]
    all_to_all x2, blocking collectives: 25.6 us -> 23.7 us  [sum_over(): return jnp.sum(lax.all_to_all(copies, axes, 0, 0, tiled=True), axis=0)]
    ppermute x10, waiting for transfers between devices: 58.4 us -> 56.7 us  [onward(): lax.ppermute(value, (axis, 'c'), [(2 * i + c, 2 * ((i + 1 - 2 * c) % n) +...]
    pallas_call x5 -> x4, Pallas kernels: 16.5 us -> 15 us  [product(): pl.pallas_call(kernel, in_specs=[pl.BlockSpec(memory_space=pltpu.SMEM), V...]
  transfers between devices with their start and end apart: 22 -> 22, of which waited for: 15 -> 15; matrix products, arithmetic and copies ran while one was open for 1% -> 1% of each run, Pallas kernels for 10% -> 11%
where the time goes in v5:
time: 142 us
  waiting for transfers between devices  69 us (49%)
  blocking collectives  32.9 us (23%)
  Pallas kernels  19 us (13%)
  starting transfers between devices  14.5 us (10%)
  other arithmetic  4.57 us (3%)
  between operations  1.64 us (1%)
    ppermute x10, waiting for transfers between devices, onward(): lax.ppermute(value, (axis, 'c'), [(2 * i + c, 2 * ((i + 1 - 2 * c) % n) +...  56.7 us
    all_to_all x2, blocking collectives, sum_over(): return jnp.sum(lax.all_to_all(copies, axes, 0, 0, tiled=True), axis=0)  23.7 us
    pallas_call x4, Pallas kernels, product(): pl.pallas_call(kernel, in_specs=[pl.BlockSpec(memory_space=pltpu.SMEM), V...  15 us
    psum x1, blocking collectives, shards(): norms = jnp.sqrt(lax.psum(squares, 'y'))  9.19 us
    ppermute x9, starting transfers between devices, other_core(): return lax.ppermute(value, 'c', [(0, 1), (1, 0)])  7.44 us
    ppermute x9, waiting for transfers between devices, other_core(): return lax.ppermute(value, 'c', [(0, 1), (1, 0)])  6.69 us
    ppermute x3, waiting for transfers between devices, shift(): return lax.ppermute(value, axis, [(i, (i + by) % n) for i in range(n)])  5.59 us
    ppermute x10, starting transfers between devices, onward(): lax.ppermute(value, (axis, 'c'), [(2 * i + c, 2 * ((i + 1 - 2 * c) % n) +...  4.37 us
  transfers between devices with their start and end apart: 22, of which 15 were waited for; matrix products, arithmetic and copies ran while one was open for 1% of the time, Pallas kernels for 11%

profile of v5, /device:TPU:8, one launch (start us, length us, event | category | flops | bytes accessed | tf_op | source)
XLA Modules:
  0.0 141.9 jit_solution(4598766493123529582)
XLA Ops:
  0.7 4.1 %shard_map.85 = (bf16[1024,2048]{1,0:T(8,128)(2,1)S(1)}, bf16[1024,2048]{1,0:T(8,128)(2,1)S(1)}, f32[4,32,1152]{2,1,0:T(8,128)S(1)}, f32[4,32,1152]{2,1,0:T(8,128)S(1)}) custom-call(s32[3]{0:T(128)S(1)} %pad_add_fusion.1.where_ref, bf16[1024,2048]{1,0:T(8,128)(2,1)} %lhs_hbm.1, bf16[1024,2048]{1,0:T(8,128)(2,1)} %rhs_hbm.1), custom_call_target="tpu_custom_call" | custom-call | flops 294912 | bytes 256 | tf_op jit(solution)/shard_map/pallas_call | solution.py:141
  4.9 2.3 %shard_map.86 = (f32[8,32,1152]{2,1,0:T(8,128)S(1)}, f32[8,32,1152]{2,1,0:T(8,128)S(1)}) custom-call(s32[3]{0:T(128)S(1)} %pad_add_fusion.1.where_ref, bf16[1024,2048]{1,0:T(8,128)(2,1)S(1)} %get-tuple-element.29.lhs_ref, bf16[1024,2048]{1,0:T(8,128)(2,1)S(1)} %get-tuple-element.30.rhs_ref), custom_call_target="tpu_custom_call" | custom-call | flops 589824 | bytes 512 | tf_op jit(solution)/shard_map/pallas_call | solution.py:128
  7.8 2.0 %collective-permute-start.2 = (f32[4,32,1152]{2,1,0:T(8,128)S(1)}, f32[4,32,1152]{2,1,0:T(8,128)S(1)}, u32[]{:S(2)}, u32[]{:S(2)}) collective-permute-start(f32[4,32,1152]{2,1,0:T(8,128)S(1)} %add.108), channel_id=1, source_target_pairs={{0,32},{4,228},{32,64},{36,4},{64,96},{68,36},{96,128},{100,68},{1... | collective-permute-start | bytes 1769480 | tf_op jit(solution)/shard_map/ppermute | solution.py:168
  9.8 7.3 %shard_map.87 = (f32[8,32,896]{2,1,0:T(8,128)S(1)}, f32[8,32,896]{2,1,0:T(8,128)S(1)}, f32[24,32,896]{2,1,0:T(8,128)S(1)}, f32[24,32,896]{2,1,0:T(8,128)S(1)}) custom-call(s32[3]{0:T(128)S(1)} %pad_add_fusion.1.where_ref, bf16[1024,2048]{1,0:T(8,128)(2,1)S(1)} %get-tuple-element.29.lhs_ref, bf16[1024,2048]{1,0:T(8,128)(2,1)S(1)} %get-tuple-element.30.rhs_ref), custom_call_target="tpu_custom_call" | custom-call | flops 1835008 | bytes 2048 | tf_op jit(solution)/shard_map/pallas_call | solution.py:128
  17.2 3.8 %collective-permute-start.3 = (f32[8,32,896]{2,1,0:T(8,128)S(1)}, f32[8,32,896]{2,1,0:T(8,128)S(1)}, u32[]{:S(2)}, u32[]{:S(2)}) collective-permute-start(f32[8,32,896]{2,1,0:T(8,128)S(1)} %get-tuple-element.38), channel_id=1, source_target_pairs={{0,4},{4,0},{1,5},{5,1},{2,6},{6,2},{3,7},{7,3},{8,12},{12,8},{9,1... | collective-permute-start | bytes 2752520 | tf_op jit(solution)/shard_map/ppermute | solution.py:163
  23.6 1.5 %collective-permute-start.10 = (f32[8,32,896]{2,1,0:T(8,128)S(1)}, f32[8,32,896]{2,1,0:T(8,128)S(1)}, u32[]{:S(2)}, u32[]{:S(2)}) collective-permute-start(f32[8,32,896]{2,1,0:T(8,128)S(1)} %add.111), channel_id=1, source_target_pairs={{0,8},{4,28},{8,16},{12,4},{16,24},{20,12},{24,0},{28,20},{1,9},{5... | collective-permute-start | bytes 2752520 | tf_op jit(solution)/shard_map/ppermute | solution.py:168
  25.1 2.3 %shard_map.88 = (f32[8,32,1152]{2,1,0:T(8,128)S(1)}, f32[8,32,1152]{2,1,0:T(8,128)S(1)}) custom-call(s32[3]{0:T(128)S(1)} %pad_add_fusion.1.where_ref, bf16[1024,2048]{1,0:T(8,128)(2,1)S(1)} %get-tuple-element.29.lhs_ref, bf16[1024,2048]{1,0:T(8,128)(2,1)S(1)} %get-tuple-element.30.rhs_ref), custom_call_target="tpu_custom_call" | custom-call | flops 589824 | bytes 512 | tf_op jit(solution)/shard_map/pallas_call | solution.py:128
  27.4 2.2 %collective-permute-start.5 = (f32[8,32,1152]{2,1,0:T(8,128)S(1)}, f32[8,32,1152]{2,1,0:T(8,128)S(1)}, u32[]{:S(2)}, u32[]{:S(2)}) collective-permute-start(f32[8,32,1152]{2,1,0:T(8,128)S(1)} %get-tuple-element.43), channel_id=1, source_target_pairs={{0,4},{4,0},{1,5},{5,1},{2,6},{6,2},{3,7},{7,3},{8,12},{12,8},{9,1... | collective-permute-start | bytes 3538952 | tf_op jit(solution)/shard_map/ppermute | solution.py:163
  29.5 3.1 %shard_map.89 = (f32[12,32,1152]{2,1,0:T(8,128)S(1)}, f32[12,32,1152]{2,1,0:T(8,128)S(1)}) custom-call(s32[3]{0:T(128)S(1)} %pad_add_fusion.1.where_ref, bf16[1024,2048]{1,0:T(8,128)(2,1)S(1)} %get-tuple-element.29.lhs_ref, bf16[1024,2048]{1,0:T(8,128)(2,1)S(1)} %get-tuple-element.30.rhs_ref), custom_call_target="tpu_custom_call" | custom-call | flops 884736 | bytes 768 | tf_op jit(solution)/shard_map/pallas_call | solution.py:128
  33.1 5.1 %collective-permute-done.10 = f32[8,32,896]{2,1,0:T(8,128)S(1)} collective-permute-done((f32[8,32,896]{2,1,0:T(8,128)S(1)}, f32[8,32,896]{2,1,0:T(8,128)S(1)}, u32[]{:S(2)}, u32[]{:S(2)}) %collective-permute-start.10) | collective-permute-done | bytes 917536 | tf_op jit(solution)/shard_map/ppermute | solution.py:168
  38.8 3.7 %collective-permute-done.6 = f32[8,32,1152]{2,1,0:T(8,128)S(1)} collective-permute-done((f32[8,32,1152]{2,1,0:T(8,128)S(1)}, f32[8,32,1152]{2,1,0:T(8,128)S(1)}, u32[]{:S(2)}, u32[]{:S(2)}) %collective-permute-start.6) | collective-permute-done | bytes 1179680 | tf_op jit(solution)/shard_map/ppermute | solution.py:168
  43.0 19.9 %collective-permute-done.11 = f32[16,32,896]{2,1,0:T(8,128)S(1)} collective-permute-done((f32[16,32,896]{2,1,0:T(8,128)S(1)}, f32[16,32,896]{2,1,0:T(8,128)S(1)}, u32[]{:S(2)}, u32[]{:S(2)}) %collective-permute-start.11) | collective-permute-done | bytes 1835040 | tf_op jit(solution)/shard_map/ppermute | solution.py:168
  63.3 2.2 %collective-permute-done.12 = f32[8,32,896]{2,1,0:T(8,128)S(1)} collective-permute-done((f32[8,32,896]{2,1,0:T(8,128)S(1)}, f32[8,32,896]{2,1,0:T(8,128)S(1)}, u32[]{:S(2)}, u32[]{:S(2)}) %collective-permute-start.12) | collective-permute-done | bytes 917536 | tf_op jit(solution)/shard_map/ppermute | solution.py:163
  65.8 14.9 %collective-permute-done.8 = f32[8,32,1152]{2,1,0:T(8,128)S(1)} collective-permute-done((f32[8,32,1152]{2,1,0:T(8,128)S(1)}, f32[8,32,1152]{2,1,0:T(8,128)S(1)}, u32[]{:S(2)}, u32[]{:S(2)}) %collective-permute-start.8) | collective-permute-done | bytes 1179680 | tf_op jit(solution)/shard_map/ppermute | solution.py:168
  82.2 1.9 %collective-permute-done.14 = f32[4,32,1152]{2,1,0:T(8,128)S(1)} collective-permute-done((f32[4,32,1152]{2,1,0:T(8,128)S(1)}, f32[4,32,1152]{2,1,0:T(8,128)S(1)}, u32[]{:S(2)}, u32[]{:S(2)}) %collective-permute-start.14) | collective-permute-done | bytes 589856 | tf_op jit(solution)/shard_map/ppermute | solution.py:163
  87.0 2.4 %collective-permute-done.18 = f32[2,32,896]{2,1,0:T(8,128)S(1)} collective-permute-done((f32[2,32,896]{2,1,0:T(8,128)S(1)}, f32[2,32,896]{2,1,0:T(8,128)S(1)}, u32[]{:S(2)}, u32[]{:S(2)}) %collective-permute-start.18) | collective-permute-done | bytes 229408 | tf_op jit(solution)/shard_map/ppermute | solution.py:168
  89.6 1.4 collective-permute-done.17
  90.9 4.2 %collective-permute-done.15 = f32[32,1152]{1,0:T(8,128)S(1)} collective-permute-done((f32[32,1152]{1,0:T(8,128)S(1)}, f32[32,1152]{1,0:T(8,128)S(1)}, u32[]{:S(2)}, u32[]{:S(2)}) %collective-permute-start.15) | collective-permute-done | bytes 147488 | tf_op jit(solution)/shard_map/ppermute | solution.py:173
  95.2 1.5 %collective-permute-done.19 = f32[2,32,896]{2,1,0:T(8,128)S(1)} collective-permute-done((f32[2,32,896]{2,1,0:T(8,128)S(1)}, f32[2,32,896]{2,1,0:T(8,128)S(1)}, u32[]{:S(2)}, u32[]{:S(2)}) %collective-permute-start.19) | collective-permute-done | bytes 229408 | tf_op jit(solution)/shard_map/ppermute | solution.py:168
  96.9 7.2 %collective-permute-done.20 = f32[2,32,896]{2,1,0:T(8,128)S(1)} collective-permute-done((f32[2,32,896]{2,1,0:T(8,128)S(1)}, f32[2,32,896]{2,1,0:T(8,128)S(1)}, u32[]{:S(2)}, u32[]{:S(2)}) %collective-permute-start.20) | collective-permute-done | bytes 229408 | tf_op jit(solution)/shard_map/ppermute | solution.py:168
  104.2 1.3 collective-permute-done.21
  105.7 12.1 %all_to_all.10 = f32[16,8,128]{2,1,0:T(8,128)S(1)} all-to-all(f32[16,8,128]{2,1,0:T(8,128)S(1)} %broadcast_in_dim.4), channel_id=1, replica_groups=mesh['z'=8,'x'=4,'c'=2,'y'=4] {'z','c'}, dimensions={0} | all-to-all | bytes 131072 | tf_op jit(solution)/shard_map/all_to_all | solution.py:182
  117.8 11.6 %all_to_all.11 = f32[16,8,128]{2,1,0:T(8,128)S(1)} all-to-all(f32[16,8,128]{2,1,0:T(8,128)S(1)} %broadcast_in_dim.5), channel_id=1, replica_groups=mesh['z'=8,'x'=4,'c'=2,'y'=4] {'x','y'}, dimensions={0} | all-to-all | bytes 131072 | tf_op jit(solution)/shard_map/all_to_all | solution.py:182
  131.9 9.2 %psum.7 = f32[2,32]{1,0:T(2,128)S(1)} all-reduce(f32[2,32]{1,0:T(2,128)S(1)} %pad_maximum_fusion), channel_id=1, replica_groups=mesh['z'=8,'x'=4,'c'=2,'y'=4] {'y'}, use_global_device_ids=true, to_apply=%region_5.0 | all-reduce | flops 64 | bytes 512 | tf_op jit(solution)/shard_map/psum | solution.py:251
  (67 shorter events, 13.1 us)
Async XLA Ops:
  4.8 3.0 %collective-permute-start = (f32[4,32,1152]{2,1,0:T(8,128)S(1)}, f32[4,32,1152]{2,1,0:T(8,128)S(1)}, u32[]{:S(2)}, u32[]{:S(2)}) collective-permute-start(f32[4,32,1152]{2,1,0:T(8,128)S(1)} %get-tuple-element.32), channel_id=1, source_target_pairs={{0,4},{4,0},{1,5},{5,1},{2,6},{6,2},{3,7},{7,3},{8,12},{12,8},{9,1... | collective-permute-start | bytes 1769480 | tf_op jit(solution)/shard_map/ppermute | solution.py:163
  7.2 14.4 %collective-permute-start.1 = (f32[8,32,1152]{2,1,0:T(8,128)S(1)}, f32[8,32,1152]{2,1,0:T(8,128)S(1)}, u32[]{:S(2)}, u32[]{:S(2)}) collective-permute-start(f32[8,32,1152]{2,1,0:T(8,128)S(1)} %get-tuple-element.35), channel_id=1, source_target_pairs={{0,4},{4,0},{1,5},{5,1},{2,6},{6,2},{3,7},{7,3},{8,12},{12,8},{9,1... | collective-permute-start | bytes 3538952 | tf_op jit(solution)/shard_map/ppermute | solution.py:163
  7.8 13.8 %collective-permute-start.2 = (f32[4,32,1152]{2,1,0:T(8,128)S(1)}, f32[4,32,1152]{2,1,0:T(8,128)S(1)}, u32[]{:S(2)}, u32[]{:S(2)}) collective-permute-start(f32[4,32,1152]{2,1,0:T(8,128)S(1)} %add.108), channel_id=1, source_target_pairs={{0,32},{4,228},{32,64},{36,4},{64,96},{68,36},{96,128},{100,68},{1... | collective-permute-start | bytes 1769480 | tf_op jit(solution)/shard_map/ppermute | solution.py:168
  17.2 5.9 %collective-permute-start.3 = (f32[8,32,896]{2,1,0:T(8,128)S(1)}, f32[8,32,896]{2,1,0:T(8,128)S(1)}, u32[]{:S(2)}, u32[]{:S(2)}) collective-permute-start(f32[8,32,896]{2,1,0:T(8,128)S(1)} %get-tuple-element.38), channel_id=1, source_target_pairs={{0,4},{4,0},{1,5},{5,1},{2,6},{6,2},{3,7},{7,3},{8,12},{12,8},{9,1... | collective-permute-start | bytes 2752520 | tf_op jit(solution)/shard_map/ppermute | solution.py:163
  23.1 9.6 %collective-permute-start.9 = (f32[24,32,896]{2,1,0:T(8,128)S(1)}, f32[24,32,896]{2,1,0:T(8,128)S(1)}, u32[]{:S(2)}, u32[]{:S(2)}) collective-permute-start(f32[24,32,896]{2,1,0:T(8,128)S(1)} %get-tuple-element.46), channel_id=1, source_target_pairs={{0,4},{4,0},{1,5},{5,1},{2,6},{6,2},{3,7},{7,3},{8,12},{12,8},{9,1... | collective-permute-start | bytes 8257544 | tf_op jit(solution)/shard_map/ppermute | solution.py:163
  23.6 14.6 %collective-permute-start.10 = (f32[8,32,896]{2,1,0:T(8,128)S(1)}, f32[8,32,896]{2,1,0:T(8,128)S(1)}, u32[]{:S(2)}, u32[]{:S(2)}) collective-permute-start(f32[8,32,896]{2,1,0:T(8,128)S(1)} %add.111), channel_id=1, source_target_pairs={{0,8},{4,28},{8,16},{12,4},{16,24},{20,12},{24,0},{28,20},{1,9},{5... | collective-permute-start | bytes 2752520 | tf_op jit(solution)/shard_map/ppermute | solution.py:168
  25.1 17.4 %collective-permute-start.6 = (f32[8,32,1152]{2,1,0:T(8,128)S(1)}, f32[8,32,1152]{2,1,0:T(8,128)S(1)}, u32[]{:S(2)}, u32[]{:S(2)}) collective-permute-start(f32[8,32,1152]{2,1,0:T(8,128)S(1)} %pad_add_fusion), channel_id=1, source_target_pairs={{0,32},{4,228},{32,64},{36,4},{64,96},{68,36},{96,128},{100,68},{1... | collective-permute-start | bytes 3538952 | tf_op jit(solution)/shard_map/ppermute | solution.py:168
  27.4 15.1 %collective-permute-start.5 = (f32[8,32,1152]{2,1,0:T(8,128)S(1)}, f32[8,32,1152]{2,1,0:T(8,128)S(1)}, u32[]{:S(2)}, u32[]{:S(2)}) collective-permute-start(f32[8,32,1152]{2,1,0:T(8,128)S(1)} %get-tuple-element.43), channel_id=1, source_target_pairs={{0,4},{4,0},{1,5},{5,1},{2,6},{6,2},{3,7},{7,3},{8,12},{12,8},{9,1... | collective-permute-start | bytes 3538952 | tf_op jit(solution)/shard_map/ppermute | solution.py:163
  32.6 10.2 %collective-permute-start.4 = (f32[12,32,1152]{2,1,0:T(8,128)S(1)}, f32[12,32,1152]{2,1,0:T(8,128)S(1)}, u32[]{:S(2)}, u32[]{:S(2)}) collective-permute-start(f32[12,32,1152]{2,1,0:T(8,128)S(1)} %get-tuple-element.42), channel_id=1, source_target_pairs={{0,4},{4,0},{1,5},{5,1},{2,6},{6,2},{3,7},{7,3},{8,12},{12,8},{9,1... | collective-permute-start | bytes 5308424 | tf_op jit(solution)/shard_map/ppermute | solution.py:163
  38.4 24.5 %collective-permute-start.11 = (f32[16,32,896]{2,1,0:T(8,128)S(1)}, f32[16,32,896]{2,1,0:T(8,128)S(1)}, u32[]{:S(2)}, u32[]{:S(2)}) collective-permute-start(f32[16,32,896]{2,1,0:T(8,128)S(1)} %slice_add_fusion), channel_id=1, source_target_pairs={{0,8},{4,28},{8,16},{12,4},{16,24},{20,12},{24,0},{28,20},{1,9},{5... | collective-permute-start | bytes 5505032 | tf_op jit(solution)/shard_map/ppermute | solution.py:168
  42.7 20.4 %collective-permute-start.7 = (f32[8,32,1152]{2,1,0:T(8,128)S(1)}, f32[8,32,1152]{2,1,0:T(8,128)S(1)}, u32[]{:S(2)}, u32[]{:S(2)}) collective-permute-start(f32[8,32,1152]{2,1,0:T(8,128)S(1)} %add_add_fusion), channel_id=1, source_target_pairs={{0,32},{4,228},{32,64},{36,4},{64,96},{68,36},{96,128},{100,68},{1... | collective-permute-start | bytes 3538952 | tf_op jit(solution)/shard_map/ppermute | solution.py:168
  63.0 2.6 %collective-permute-start.12 = (f32[8,32,896]{2,1,0:T(8,128)S(1)}, f32[8,32,896]{2,1,0:T(8,128)S(1)}, u32[]{:S(2)}, u32[]{:S(2)}) collective-permute-start(f32[8,32,896]{2,1,0:T(8,128)S(1)} %slice.87), channel_id=1, source_target_pairs={{0,4},{4,0},{1,5},{5,1},{2,6},{6,2},{3,7},{7,3},{8,12},{12,8},{9,1... | collective-permute-start | bytes 2752520 | tf_op jit(solution)/shard_map/ppermute | solution.py:163
  63.2 17.5 %collective-permute-start.8 = (f32[8,32,1152]{2,1,0:T(8,128)S(1)}, f32[8,32,1152]{2,1,0:T(8,128)S(1)}, u32[]{:S(2)}, u32[]{:S(2)}) collective-permute-start(f32[8,32,1152]{2,1,0:T(8,128)S(1)} %slice_add_fusion.1), channel_id=1, source_target_pairs={{0,32},{4,228},{32,64},{36,4},{64,96},{68,36},{96,128},{100,68},{1... | collective-permute-start | bytes 3538952 | tf_op jit(solution)/shard_map/ppermute | solution.py:168
  65.7 16.2 %collective-permute-start.13 = (f32[1,32,896]{2,1,0:T(8,128)S(1)}, f32[1,32,896]{2,1,0:T(8,128)S(1)}, u32[]{:S(2)}, u32[]{:S(2)}) collective-permute-start(f32[1,32,896]{2,1,0:T(8,128)S(1)} %slice.89), channel_id=1, source_target_pairs={{0,32},{4,228},{32,64},{36,4},{64,96},{68,36},{96,128},{100,68},{1... | collective-permute-start | bytes 344072 | tf_op jit(solution)/shard_map/ppermute | solution.py:168
  82.0 2.1 %collective-permute-start.14 = (f32[4,32,1152]{2,1,0:T(8,128)S(1)}, f32[4,32,1152]{2,1,0:T(8,128)S(1)}, u32[]{:S(2)}, u32[]{:S(2)}) collective-permute-start(f32[4,32,1152]{2,1,0:T(8,128)S(1)} %slice.70), channel_id=1, source_target_pairs={{0,4},{4,0},{1,5},{5,1},{2,6},{6,2},{3,7},{7,3},{8,12},{12,8},{9,1... | collective-permute-start | bytes 1769480 | tf_op jit(solution)/shard_map/ppermute | solution.py:163
  82.1 7.3 %collective-permute-start.18 = (f32[2,32,896]{2,1,0:T(8,128)S(1)}, f32[2,32,896]{2,1,0:T(8,128)S(1)}, u32[]{:S(2)}, u32[]{:S(2)}) collective-permute-start(f32[2,32,896]{2,1,0:T(8,128)S(1)} %slice_add_fusion.7), channel_id=1, source_target_pairs={{0,32},{4,228},{32,64},{36,4},{64,96},{68,36},{96,128},{100,68},{1... | collective-permute-start | bytes 688136 | tf_op jit(solution)/shard_map/ppermute | solution.py:168
  84.2 6.7 %collective-permute-start.17 = (f32[32,1152]{1,0:T(8,128)S(1)}, f32[32,1152]{1,0:T(8,128)S(1)}, u32[]{:S(2)}, u32[]{:S(2)}) collective-permute-start(f32[32,1152]{1,0:T(8,128)S(1)} %get-tuple-element.56), channel_id=1, source_target_pairs={{0,24},{8,0},{16,8},{24,16},{1,25},{9,1},{17,9},{25,17},{2,26},{10... | collective-permute-start | bytes 442376 | tf_op jit(solution)/shard_map/ppermute | solution.py:173
  85.2 10.0 %collective-permute-start.15 = (f32[32,1152]{1,0:T(8,128)S(1)}, f32[32,1152]{1,0:T(8,128)S(1)}, u32[]{:S(2)}, u32[]{:S(2)}) collective-permute-start(f32[32,1152]{1,0:T(8,128)S(1)} %get-tuple-element.57), channel_id=1, source_target_pairs={{0,8},{8,16},{16,24},{24,0},{1,9},{9,17},{17,25},{25,1},{2,10},{10... | collective-permute-start | bytes 442376 | tf_op jit(solution)/shard_map/ppermute | solution.py:173
  86.3 8.8 %collective-permute-start.16 = (f32[32,1152]{1,0:T(8,128)S(1)}, f32[32,1152]{1,0:T(8,128)S(1)}, u32[]{:S(2)}, u32[]{:S(2)}) collective-permute-start(f32[32,1152]{1,0:T(8,128)S(1)} %get-tuple-element.55), channel_id=1, source_target_pairs={{0,16},{8,24},{16,0},{24,8},{1,17},{9,25},{17,1},{25,9},{2,18},{10... | collective-permute-start | bytes 442376 | tf_op jit(solution)/shard_map/ppermute | solution.py:173
  89.5 7.3 %collective-permute-start.19 = (f32[2,32,896]{2,1,0:T(8,128)S(1)}, f32[2,32,896]{2,1,0:T(8,128)S(1)}, u32[]{:S(2)}, u32[]{:S(2)}) collective-permute-start(f32[2,32,896]{2,1,0:T(8,128)S(1)} %slice_add_fusion.5), channel_id=1, source_target_pairs={{0,32},{4,228},{32,64},{36,4},{64,96},{68,36},{96,128},{100,68},{1... | collective-permute-start | bytes 688136 | tf_op jit(solution)/shard_map/ppermute | solution.py:168
  95.2 35.5 %copy-start.1 = (f32[32,2048]{1,0:T(8,128)S(1)}, f32[32,2048]{1,0:T(8,128)}, u32[]{:S(2)}) copy-start(f32[32,2048]{1,0:T(8,128)} %param.9) | copy-start | bytes 786436
  95.2 35.5 %copy-start.2 = (f32[32,2048]{1,0:T(8,128)S(1)}, f32[32,2048]{1,0:T(8,128)}, u32[]{:S(2)}) copy-start(f32[32,2048]{1,0:T(8,128)} %param.11) | copy-start | bytes 786436
  96.8 7.3 %collective-permute-start.20 = (f32[2,32,896]{2,1,0:T(8,128)S(1)}, f32[2,32,896]{2,1,0:T(8,128)S(1)}, u32[]{:S(2)}, u32[]{:S(2)}) collective-permute-start(f32[2,32,896]{2,1,0:T(8,128)S(1)} %slice_add_fusion.6), channel_id=1, source_target_pairs={{0,32},{4,228},{32,64},{36,4},{64,96},{68,36},{96,128},{100,68},{1... | collective-permute-start | bytes 688136 | tf_op jit(solution)/shard_map/ppermute | solution.py:168
  104.1 1.4 collective-permute-start.21
  (2 other events, 51.6 us)

commit v6 on v5

--- a/solution.py
+++ b/solution.py
@@ -204,6 +204,12 @@
     def add(here, moving):
         return here + (moving if moving.shape == here.shape else at_front(moving, here.shape[0]))
 
+    cuts = (slice(0, 640), slice(640, COLS_Z))
+
+    def hop_z(pair, parts):
+        ahead = add(both(pair)[:8, :, cuts[0]], parts[0])
+        return ahead, add(both(pair)[:8, :, cuts[1]], after(parts[1], ahead))
+
     grad_out, attn_out, keep4, send4 = product_far(where, grad_out, attn_out)
     pair4 = (keep4, other_core(send4))
     pair3 = product_z(after(where, pair4[0]), (3,))
@@ -213,26 +219,30 @@
         functools.partial(product_x_kernel, COLS_Z, cols_x),
         [8, 8, 24, 24], cols_x, 2048, after(where, pair3[0], first_z), grad_out, attn_out,
     )
-    next_z = add(both(pair3)[:8], onward(first_z, "z"))
+    pair2 = product_z(after(where, keep_far), (2,))
+    next_z = add(both(pair3)[:8], after(onward(first_z, "z"), pair2[0]))
     far_x = (keep_far, after(other_core(send_far), next_z))
-    pair2 = product_z(after(where, keep_far, next_z), (2,))
     pair2 = (pair2[0], other_core(pair2[1]))
     first_x = lax.optimization_barrier(both(far_x))
     pair_x = (keep_x, other_core(after(send_x, first_x)))
     pair1 = product_z(after(where, pair2[0], first_x), (1, 0))
     pair1 = (pair1[0], other_core(pair1[1]))
 
-    z = onward(next_z, "z")
+    next_z = onward(next_z, "z")
+    z = [next_z[..., cut] for cut in cuts]
     for pair in (pair2, pair1):
-        z = onward(add(both(pair)[:8], z), "z")
-    x = onward(first_x, "x")
-    x = onward(add(both(pair_x)[:16], x), "x")
+        steps = hop_z(pair, z)
+        z = [onward(part, "z") for part in steps]
+    x = after(onward(first_x, "x"), pair1[0])
+    x = after(onward(add(both(pair_x)[:16], x), "x"), z[0], steps[1])
     sum_x = x[:8] + other_core(x[8:]) + both(pair_x)[16:24]
 
     moving = onward(sum_x[6:7], "z")
-    z = after(z, moving)
-    moving = add(sum_x[4:6], after(moving, z))
-    sum_z = z[:4] + other_core(after(z[4:], moving)) + both(pair1)[8:12]
+    far = [other_core(z[0][4:])]
+    z[1] = after(z[1], moving)
+    moving = add(sum_x[4:6], after(moving, z[1]))
+    far.append(other_core(after(z[1][4:], moving)))
+    sum_z = jnp.concatenate([z[i][:4] + far[i] for i in range(2)], axis=2) + both(pair1)[8:12]
     batch_z = sum_z[0] + sum(shift(sum_z[k], "x", k) for k in (1, 2, 3))
     moving = onward(moving, "z")
     moving = onward(sum_x[2:4] + moving, "z")

time: 142 us -> 141 us (level)
  waiting for transfers between devices: 69 us -> 63.8 us
  starting transfers between devices: 14.5 us -> 16.9 us
  blocking collectives: 32.9 us -> 34.4 us
    ppermute x10 -> x12, waiting for transfers between devices: 56.7 us -> 53.4 us  [onward(): lax.ppermute(value, (axis, 'c'), [(2 * i + c, 2 * ((i + 1 - 2 * c) % n) +...]
    ppermute x3, starting transfers between devices: 2.74 us -> 4.83 us  [shift(): return lax.ppermute(value, axis, [(i, (i + by) % n) for i in range(n)])]
    ppermute x9 -> x10, waiting for transfers between devices: 6.69 us -> 5.07 us  [other_core(): return lax.ppermute(value, 'c', [(0, 1), (1, 0)])]
    all_to_all x2, blocking collectives: 23.7 us -> 25.2 us  [sum_over(): return jnp.sum(lax.all_to_all(copies, axes, 0, 0, tiled=True), axis=0)]
    ppermute x10 -> x12, starting transfers between devices: 4.37 us -> 4.54 us  [onward(): lax.ppermute(value, (axis, 'c'), [(2 * i + c, 2 * ((i + 1 - 2 * c) % n) +...]
    ppermute x9 -> x10, starting transfers between devices: 7.44 us -> 7.49 us  [other_core(): return lax.ppermute(value, 'c', [(0, 1), (1, 0)])]
  transfers between devices with their start and end apart: 22 -> 25, of which waited for: 15 -> 16; matrix products, arithmetic and copies ran while one was open for 1% -> 2% of each run, Pallas kernels for 11% -> 11%
where the time goes in v6:
time: 141 us
  waiting for transfers between devices  63.8 us (45%)
  blocking collectives  34.4 us (24%)
  Pallas kernels  19 us (13%)
  starting transfers between devices  16.9 us (12%)
  other arithmetic  4.97 us (4%)
  between operations  1.67 us (1%)
    ppermute x12, waiting for transfers between devices, onward(): lax.ppermute(value, (axis, 'c'), [(2 * i + c, 2 * ((i + 1 - 2 * c) % n) +...  53.4 us
    all_to_all x2, blocking collectives, sum_over(): return jnp.sum(lax.all_to_all(copies, axes, 0, 0, tiled=True), axis=0)  25.2 us
    pallas_call x4, Pallas kernels, product(): pl.pallas_call(kernel, in_specs=[pl.BlockSpec(memory_space=pltpu.SMEM), V...  15 us
    psum x1, blocking collectives, shards(): norms = jnp.sqrt(lax.psum(squares, 'y'))  9.19 us
    ppermute x10, starting transfers between devices, other_core(): return lax.ppermute(value, 'c', [(0, 1), (1, 0)])  7.49 us
    ppermute x3, waiting for transfers between devices, shift(): return lax.ppermute(value, axis, [(i, (i + by) % n) for i in range(n)])  5.35 us
    ppermute x10, waiting for transfers between devices, other_core(): return lax.ppermute(value, 'c', [(0, 1), (1, 0)])  5.07 us
    ppermute x3, starting transfers between devices, shift(): return lax.ppermute(value, axis, [(i, (i + by) % n) for i in range(n)])  4.83 us
  transfers between devices with their start and end apart: 25, of which 16 were waited for; matrix products, arithmetic and copies ran while one was open for 2% of the time, Pallas kernels for 11%

profile of v6, /device:TPU:8, one launch (start us, length us, event | category | flops | bytes accessed | tf_op | source)
XLA Modules:
  0.0 141.0 jit_solution(4512735734215939869)
XLA Ops:
  0.7 4.1 %shard_map.85 = (bf16[1024,2048]{1,0:T(8,128)(2,1)S(1)}, bf16[1024,2048]{1,0:T(8,128)(2,1)S(1)}, f32[4,32,1152]{2,1,0:T(8,128)S(1)}, f32[4,32,1152]{2,1,0:T(8,128)S(1)}) custom-call(s32[3]{0:T(128)S(1)} %pad_add_fusion.1.where_ref, bf16[1024,2048]{1,0:T(8,128)(2,1)} %lhs_hbm.1, bf16[1024,2048]{1,0:T(8,128)(2,1)} %rhs_hbm.1), custom_call_target="tpu_custom_call" | custom-call | flops 294912 | bytes 256 | tf_op jit(solution)/shard_map/pallas_call | solution.py:141
  4.9 2.3 %shard_map.86 = (f32[8,32,1152]{2,1,0:T(8,128)S(1)}, f32[8,32,1152]{2,1,0:T(8,128)S(1)}) custom-call(s32[3]{0:T(128)S(1)} %pad_add_fusion.1.where_ref, bf16[1024,2048]{1,0:T(8,128)(2,1)S(1)} %get-tuple-element.34.lhs_ref, bf16[1024,2048]{1,0:T(8,128)(2,1)S(1)} %get-tuple-element.35.rhs_ref), custom_call_target="tpu_custom_call" | custom-call | flops 589824 | bytes 512 | tf_op jit(solution)/shard_map/pallas_call | solution.py:128
  7.8 2.0 %collective-permute-start.3 = (f32[4,32,1152]{2,1,0:T(8,128)S(1)}, f32[4,32,1152]{2,1,0:T(8,128)S(1)}, u32[]{:S(2)}, u32[]{:S(2)}) collective-permute-start(f32[4,32,1152]{2,1,0:T(8,128)S(1)} %add.119), channel_id=1, source_target_pairs={{0,32},{4,228},{32,64},{36,4},{64,96},{68,36},{96,128},{100,68},{1... | collective-permute-start | bytes 1769480 | tf_op jit(solution)/shard_map/ppermute | solution.py:168
  9.8 7.3 %shard_map.87 = (f32[8,32,896]{2,1,0:T(8,128)S(1)}, f32[8,32,896]{2,1,0:T(8,128)S(1)}, f32[24,32,896]{2,1,0:T(8,128)S(1)}, f32[24,32,896]{2,1,0:T(8,128)S(1)}) custom-call(s32[3]{0:T(128)S(1)} %pad_add_fusion.1.where_ref, bf16[1024,2048]{1,0:T(8,128)(2,1)S(1)} %get-tuple-element.34.lhs_ref, bf16[1024,2048]{1,0:T(8,128)(2,1)S(1)} %get-tuple-element.35.rhs_ref), custom_call_target="tpu_custom_call" | custom-call | flops 1835008 | bytes 2048 | tf_op jit(solution)/shard_map/pallas_call | solution.py:128
  17.2 3.8 %collective-permute-start.1 = (f32[8,32,896]{2,1,0:T(8,128)S(1)}, f32[8,32,896]{2,1,0:T(8,128)S(1)}, u32[]{:S(2)}, u32[]{:S(2)}) collective-permute-start(f32[8,32,896]{2,1,0:T(8,128)S(1)} %get-tuple-element.42), channel_id=1, source_target_pairs={{0,4},{4,0},{1,5},{5,1},{2,6},{6,2},{3,7},{7,3},{8,12},{12,8},{9,1... | collective-permute-start | bytes 2752520 | tf_op jit(solution)/shard_map/ppermute | solution.py:163
  20.9 2.3 %shard_map.88 = (f32[8,32,1152]{2,1,0:T(8,128)S(1)}, f32[8,32,1152]{2,1,0:T(8,128)S(1)}) custom-call(s32[3]{0:T(128)S(1)} %pad_add_fusion.1.where_ref, bf16[1024,2048]{1,0:T(8,128)(2,1)S(1)} %get-tuple-element.34.lhs_ref, bf16[1024,2048]{1,0:T(8,128)(2,1)S(1)} %get-tuple-element.35.rhs_ref), custom_call_target="tpu_custom_call" | custom-call | flops 589824 | bytes 512 | tf_op jit(solution)/shard_map/pallas_call | solution.py:128
  24.2 1.5 %collective-permute-start.13 = (f32[8,32,896]{2,1,0:T(8,128)S(1)}, f32[8,32,896]{2,1,0:T(8,128)S(1)}, u32[]{:S(2)}, u32[]{:S(2)}) collective-permute-start(f32[8,32,896]{2,1,0:T(8,128)S(1)} %add.122), channel_id=1, source_target_pairs={{0,8},{4,28},{8,16},{12,4},{16,24},{20,12},{24,0},{28,20},{1,9},{5... | collective-permute-start | bytes 2752520 | tf_op jit(solution)/shard_map/ppermute | solution.py:168
  25.7 3.1 %shard_map.89 = (f32[12,32,1152]{2,1,0:T(8,128)S(1)}, f32[12,32,1152]{2,1,0:T(8,128)S(1)}) custom-call(s32[3]{0:T(128)S(1)} %pad_add_fusion.1.where_ref, bf16[1024,2048]{1,0:T(8,128)(2,1)S(1)} %get-tuple-element.34.lhs_ref, bf16[1024,2048]{1,0:T(8,128)(2,1)S(1)} %get-tuple-element.35.rhs_ref), custom_call_target="tpu_custom_call" | custom-call | flops 884736 | bytes 768 | tf_op jit(solution)/shard_map/pallas_call | solution.py:128
  28.7 2.0 %collective-permute-start.4 = (f32[12,32,1152]{2,1,0:T(8,128)S(1)}, f32[12,32,1152]{2,1,0:T(8,128)S(1)}, u32[]{:S(2)}, u32[]{:S(2)}) collective-permute-start(f32[12,32,1152]{2,1,0:T(8,128)S(1)} %get-tuple-element.48), channel_id=1, source_target_pairs={{0,4},{4,0},{1,5},{5,1},{2,6},{6,2},{3,7},{7,3},{8,12},{12,8},{9,1... | collective-permute-start | bytes 5308424 | tf_op jit(solution)/shard_map/ppermute | solution.py:163
  30.9 7.9 %collective-permute-done.13 = f32[8,32,896]{2,1,0:T(8,128)S(1)} collective-permute-done((f32[8,32,896]{2,1,0:T(8,128)S(1)}, f32[8,32,896]{2,1,0:T(8,128)S(1)}, u32[]{:S(2)}, u32[]{:S(2)}) %collective-permute-start.13) | collective-permute-done | bytes 917536 | tf_op jit(solution)/shard_map/ppermute | solution.py:168
  39.7 3.3 %collective-permute-done.6 = f32[8,32,1152]{2,1,0:T(8,128)S(1)} collective-permute-done((f32[8,32,1152]{2,1,0:T(8,128)S(1)}, f32[8,32,1152]{2,1,0:T(8,128)S(1)}, u32[]{:S(2)}, u32[]{:S(2)}) %collective-permute-start.6) | collective-permute-done | bytes 1179680 | tf_op jit(solution)/shard_map/ppermute | solution.py:168
  43.8 11.3 %collective-permute-done.7 = f32[8,32,640]{2,1,0:T(8,128)S(1)} collective-permute-done((f32[8,32,640]{2,1,0:T(8,128)S(1)}, f32[8,32,640]{2,1,0:T(8,128)S(1)}, u32[]{:S(2)}, u32[]{:S(2)}) %collective-permute-start.7) | collective-permute-done | bytes 655392 | tf_op jit(solution)/shard_map/ppermute | solution.py:168
  55.2 5.5 %collective-permute-done.10 = f32[8,32,512]{2,1,0:T(8,128)S(1)} collective-permute-done((f32[8,32,512]{2,1,0:T(8,128)S(1)}, f32[8,32,512]{2,1,0:T(8,128)S(1)}, u32[]{:S(2)}, u32[]{:S(2)}) %collective-permute-start.10) | collective-permute-done | bytes 524320 | tf_op jit(solution)/shard_map/ppermute | solution.py:168
  60.8 6.9 %collective-permute-done.8 = f32[8,32,640]{2,1,0:T(8,128)S(1)} collective-permute-done((f32[8,32,640]{2,1,0:T(8,128)S(1)}, f32[8,32,640]{2,1,0:T(8,128)S(1)}, u32[]{:S(2)}, u32[]{:S(2)}) %collective-permute-start.8) | collective-permute-done | bytes 655392 | tf_op jit(solution)/shard_map/ppermute | solution.py:168
  67.9 2.4 %collective-permute-done.15 = f32[8,32,896]{2,1,0:T(8,128)S(1)} collective-permute-done((f32[8,32,896]{2,1,0:T(8,128)S(1)}, f32[8,32,896]{2,1,0:T(8,128)S(1)}, u32[]{:S(2)}, u32[]{:S(2)}) %collective-permute-start.15) | collective-permute-done | bytes 917536 | tf_op jit(solution)/shard_map/ppermute | solution.py:163
  70.9 7.4 %collective-permute-done.11 = f32[8,32,512]{2,1,0:T(8,128)S(1)} collective-permute-done((f32[8,32,512]{2,1,0:T(8,128)S(1)}, f32[8,32,512]{2,1,0:T(8,128)S(1)}, u32[]{:S(2)}, u32[]{:S(2)}) %collective-permute-start.11) | collective-permute-done | bytes 524320 | tf_op jit(solution)/shard_map/ppermute | solution.py:168
  81.4 2.8 %collective-permute-start.19 = (f32[32,1152]{1,0:T(8,128)S(1)}, f32[32,1152]{1,0:T(8,128)S(1)}, u32[]{:S(2)}, u32[]{:S(2)}) collective-permute-start(f32[32,1152]{1,0:T(8,128)S(1)} %get-tuple-element.65), channel_id=1, source_target_pairs={{0,16},{8,24},{16,0},{24,8},{1,17},{9,25},{17,1},{25,9},{2,18},{10... | collective-permute-start | bytes 442376 | tf_op jit(solution)/shard_map/ppermute | solution.py:173
  84.2 1.5 %collective-permute-start.20 = (f32[32,1152]{1,0:T(8,128)S(1)}, f32[32,1152]{1,0:T(8,128)S(1)}, u32[]{:S(2)}, u32[]{:S(2)}) collective-permute-start(f32[32,1152]{1,0:T(8,128)S(1)} %get-tuple-element.66), channel_id=1, source_target_pairs={{0,24},{8,0},{16,8},{24,16},{1,25},{9,1},{17,9},{25,17},{2,26},{10... | collective-permute-start | bytes 442376 | tf_op jit(solution)/shard_map/ppermute | solution.py:173
  87.2 2.5 %collective-permute-done.19 = f32[32,1152]{1,0:T(8,128)S(1)} collective-permute-done((f32[32,1152]{1,0:T(8,128)S(1)}, f32[32,1152]{1,0:T(8,128)S(1)}, u32[]{:S(2)}, u32[]{:S(2)}) %collective-permute-start.19) | collective-permute-done | bytes 147488 | tf_op jit(solution)/shard_map/ppermute | solution.py:173
  92.6 1.8 %collective-permute-done.22 = f32[2,32,896]{2,1,0:T(8,128)S(1)} collective-permute-done((f32[2,32,896]{2,1,0:T(8,128)S(1)}, f32[2,32,896]{2,1,0:T(8,128)S(1)}, u32[]{:S(2)}, u32[]{:S(2)}) %collective-permute-start.22) | collective-permute-done | bytes 229408 | tf_op jit(solution)/shard_map/ppermute | solution.py:168
  94.5 7.2 %collective-permute-done.23 = f32[2,32,896]{2,1,0:T(8,128)S(1)} collective-permute-done((f32[2,32,896]{2,1,0:T(8,128)S(1)}, f32[2,32,896]{2,1,0:T(8,128)S(1)}, u32[]{:S(2)}, u32[]{:S(2)}) %collective-permute-start.23) | collective-permute-done | bytes 229408 | tf_op jit(solution)/shard_map/ppermute | solution.py:168
  103.3 12.0 %all_to_all.10 = f32[16,8,128]{2,1,0:T(8,128)S(1)} all-to-all(f32[16,8,128]{2,1,0:T(8,128)S(1)} %broadcast_in_dim.4), channel_id=1, replica_groups=mesh['z'=8,'x'=4,'c'=2,'y'=4] {'z','c'}, dimensions={0} | all-to-all | bytes 131072 | tf_op jit(solution)/shard_map/all_to_all | solution.py:182
  115.3 13.2 %all_to_all.11 = f32[16,8,128]{2,1,0:T(8,128)S(1)} all-to-all(f32[16,8,128]{2,1,0:T(8,128)S(1)} %broadcast_in_dim.5), channel_id=1, replica_groups=mesh['z'=8,'x'=4,'c'=2,'y'=4] {'x','y'}, dimensions={0} | all-to-all | bytes 131072 | tf_op jit(solution)/shard_map/all_to_all | solution.py:182
  131.0 9.2 %psum.7 = f32[2,32]{1,0:T(2,128)S(1)} all-reduce(f32[2,32]{1,0:T(2,128)S(1)} %pad_maximum_fusion), channel_id=1, replica_groups=mesh['z'=8,'x'=4,'c'=2,'y'=4] {'y'}, use_global_device_ids=true, to_apply=%region_5.0 | all-reduce | flops 64 | bytes 512 | tf_op jit(solution)/shard_map/psum | solution.py:261
  (80 shorter events, 16.2 us)
Async XLA Ops:
  4.8 3.0 %collective-permute-start = (f32[4,32,1152]{2,1,0:T(8,128)S(1)}, f32[4,32,1152]{2,1,0:T(8,128)S(1)}, u32[]{:S(2)}, u32[]{:S(2)}) collective-permute-start(f32[4,32,1152]{2,1,0:T(8,128)S(1)} %get-tuple-element.37), channel_id=1, source_target_pairs={{0,4},{4,0},{1,5},{5,1},{2,6},{6,2},{3,7},{7,3},{8,12},{12,8},{9,1... | collective-permute-start | bytes 1769480 | tf_op jit(solution)/shard_map/ppermute | solution.py:163
  7.2 16.0 %collective-permute-start.2 = (f32[8,32,1152]{2,1,0:T(8,128)S(1)}, f32[8,32,1152]{2,1,0:T(8,128)S(1)}, u32[]{:S(2)}, u32[]{:S(2)}) collective-permute-start(f32[8,32,1152]{2,1,0:T(8,128)S(1)} %get-tuple-element.43), channel_id=1, source_target_pairs={{0,4},{4,0},{1,5},{5,1},{2,6},{6,2},{3,7},{7,3},{8,12},{12,8},{9,1... | collective-permute-start | bytes 3538952 | tf_op jit(solution)/shard_map/ppermute | solution.py:163
  7.8 15.4 %collective-permute-start.3 = (f32[4,32,1152]{2,1,0:T(8,128)S(1)}, f32[4,32,1152]{2,1,0:T(8,128)S(1)}, u32[]{:S(2)}, u32[]{:S(2)}) collective-permute-start(f32[4,32,1152]{2,1,0:T(8,128)S(1)} %add.119), channel_id=1, source_target_pairs={{0,32},{4,228},{32,64},{36,4},{64,96},{68,36},{96,128},{100,68},{1... | collective-permute-start | bytes 1769480 | tf_op jit(solution)/shard_map/ppermute | solution.py:168
  17.2 6.3 %collective-permute-start.1 = (f32[8,32,896]{2,1,0:T(8,128)S(1)}, f32[8,32,896]{2,1,0:T(8,128)S(1)}, u32[]{:S(2)}, u32[]{:S(2)}) collective-permute-start(f32[8,32,896]{2,1,0:T(8,128)S(1)} %get-tuple-element.42), channel_id=1, source_target_pairs={{0,4},{4,0},{1,5},{5,1},{2,6},{6,2},{3,7},{7,3},{8,12},{12,8},{9,1... | collective-permute-start | bytes 2752520 | tf_op jit(solution)/shard_map/ppermute | solution.py:163
  23.6 15.2 %collective-permute-start.12 = (f32[24,32,896]{2,1,0:T(8,128)S(1)}, f32[24,32,896]{2,1,0:T(8,128)S(1)}, u32[]{:S(2)}, u32[]{:S(2)}) collective-permute-start(f32[24,32,896]{2,1,0:T(8,128)S(1)} %get-tuple-element.54), channel_id=1, source_target_pairs={{0,4},{4,0},{1,5},{5,1},{2,6},{6,2},{3,7},{7,3},{8,12},{12,8},{9,1... | collective-permute-start | bytes 8257544 | tf_op jit(solution)/shard_map/ppermute | solution.py:163
  23.7 7.0 %collective-permute-start.5 = (f32[8,32,1152]{2,1,0:T(8,128)S(1)}, f32[8,32,1152]{2,1,0:T(8,128)S(1)}, u32[]{:S(2)}, u32[]{:S(2)}) collective-permute-start(f32[8,32,1152]{2,1,0:T(8,128)S(1)} %get-tuple-element.49), channel_id=1, source_target_pairs={{0,4},{4,0},{1,5},{5,1},{2,6},{6,2},{3,7},{7,3},{8,12},{12,8},{9,1... | collective-permute-start | bytes 3538952 | tf_op jit(solution)/shard_map/ppermute | solution.py:163
  24.2 14.6 %collective-permute-start.13 = (f32[8,32,896]{2,1,0:T(8,128)S(1)}, f32[8,32,896]{2,1,0:T(8,128)S(1)}, u32[]{:S(2)}, u32[]{:S(2)}) collective-permute-start(f32[8,32,896]{2,1,0:T(8,128)S(1)} %add.122), channel_id=1, source_target_pairs={{0,8},{4,28},{8,16},{12,4},{16,24},{20,12},{24,0},{28,20},{1,9},{5... | collective-permute-start | bytes 2752520 | tf_op jit(solution)/shard_map/ppermute | solution.py:168
  25.7 17.4 %collective-permute-start.6 = (f32[8,32,1152]{2,1,0:T(8,128)S(1)}, f32[8,32,1152]{2,1,0:T(8,128)S(1)}, u32[]{:S(2)}, u32[]{:S(2)}) collective-permute-start(f32[8,32,1152]{2,1,0:T(8,128)S(1)} %pad_add_fusion), channel_id=1, source_target_pairs={{0,32},{4,228},{32,64},{36,4},{64,96},{68,36},{96,128},{100,68},{1... | collective-permute-start | bytes 3538952 | tf_op jit(solution)/shard_map/ppermute | solution.py:168
  28.7 14.8 %collective-permute-start.4 = (f32[12,32,1152]{2,1,0:T(8,128)S(1)}, f32[12,32,1152]{2,1,0:T(8,128)S(1)}, u32[]{:S(2)}, u32[]{:S(2)}) collective-permute-start(f32[12,32,1152]{2,1,0:T(8,128)S(1)} %get-tuple-element.48), channel_id=1, source_target_pairs={{0,4},{4,0},{1,5},{5,1},{2,6},{6,2},{3,7},{7,3},{8,12},{12,8},{9,1... | collective-permute-start | bytes 5308424 | tf_op jit(solution)/shard_map/ppermute | solution.py:163
  39.4 28.3 %collective-permute-start.14 = (f32[16,32,896]{2,1,0:T(8,128)S(1)}, f32[16,32,896]{2,1,0:T(8,128)S(1)}, u32[]{:S(2)}, u32[]{:S(2)}) collective-permute-start(f32[16,32,896]{2,1,0:T(8,128)S(1)} %slice_add_fusion), channel_id=1, source_target_pairs={{0,8},{4,28},{8,16},{12,4},{16,24},{20,12},{24,0},{28,20},{1,9},{5... | collective-permute-start | bytes 5505032 | tf_op jit(solution)/shard_map/ppermute | solution.py:168
  43.2 11.9 %collective-permute-start.7 = (f32[8,32,640]{2,1,0:T(8,128)S(1)}, f32[8,32,640]{2,1,0:T(8,128)S(1)}, u32[]{:S(2)}, u32[]{:S(2)}) collective-permute-start(f32[8,32,640]{2,1,0:T(8,128)S(1)} %slice_add_fusion.2), channel_id=1, source_target_pairs={{0,32},{4,228},{32,64},{36,4},{64,96},{68,36},{96,128},{100,68},{1... | collective-permute-start | bytes 1966088 | tf_op jit(solution)/shard_map/ppermute | solution.py:168
  43.4 17.3 %collective-permute-start.10 = (f32[8,32,512]{2,1,0:T(8,128)S(1)}, f32[8,32,512]{2,1,0:T(8,128)S(1)}, u32[]{:S(2)}, u32[]{:S(2)}) collective-permute-start(f32[8,32,512]{2,1,0:T(8,128)S(1)} %slice_add_fusion.5), channel_id=1, source_target_pairs={{0,32},{4,228},{32,64},{36,4},{64,96},{68,36},{96,128},{100,68},{1... | collective-permute-start | bytes 1572872 | tf_op jit(solution)/shard_map/ppermute | solution.py:168
  55.1 12.6 %collective-permute-start.8 = (f32[8,32,640]{2,1,0:T(8,128)S(1)}, f32[8,32,640]{2,1,0:T(8,128)S(1)}, u32[]{:S(2)}, u32[]{:S(2)}) collective-permute-start(f32[8,32,640]{2,1,0:T(8,128)S(1)} %slice_add_fusion.3), channel_id=1, source_target_pairs={{0,32},{4,228},{32,64},{36,4},{64,96},{68,36},{96,128},{100,68},{1... | collective-permute-start | bytes 1966088 | tf_op jit(solution)/shard_map/ppermute | solution.py:168
  67.8 2.6 %collective-permute-start.15 = (f32[8,32,896]{2,1,0:T(8,128)S(1)}, f32[8,32,896]{2,1,0:T(8,128)S(1)}, u32[]{:S(2)}, u32[]{:S(2)}) collective-permute-start(f32[8,32,896]{2,1,0:T(8,128)S(1)} %slice.94), channel_id=1, source_target_pairs={{0,4},{4,0},{1,5},{5,1},{2,6},{6,2},{3,7},{7,3},{8,12},{12,8},{9,1... | collective-permute-start | bytes 2752520 | tf_op jit(solution)/shard_map/ppermute | solution.py:163
  67.9 10.5 %collective-permute-start.11 = (f32[8,32,512]{2,1,0:T(8,128)S(1)}, f32[8,32,512]{2,1,0:T(8,128)S(1)}, u32[]{:S(2)}, u32[]{:S(2)}) collective-permute-start(f32[8,32,512]{2,1,0:T(8,128)S(1)} %slice_add_fusion.6), channel_id=1, source_target_pairs={{0,32},{4,228},{32,64},{36,4},{64,96},{68,36},{96,128},{100,68},{1... | collective-permute-start | bytes 1572872 | tf_op jit(solution)/shard_map/ppermute | solution.py:168
  70.5 9.0 %collective-permute-start.16 = (f32[1,32,896]{2,1,0:T(8,128)S(1)}, f32[1,32,896]{2,1,0:T(8,128)S(1)}, u32[]{:S(2)}, u32[]{:S(2)}) collective-permute-start(f32[1,32,896]{2,1,0:T(8,128)S(1)} %slice.122), channel_id=1, source_target_pairs={{0,32},{4,228},{32,64},{36,4},{64,96},{68,36},{96,128},{100,68},{1... | collective-permute-start | bytes 344072 | tf_op jit(solution)/shard_map/ppermute | solution.py:168
  70.7 9.0 %collective-permute-start.9 = (f32[4,32,640]{2,1,0:T(8,128)S(1)}, f32[4,32,640]{2,1,0:T(8,128)S(1)}, u32[]{:S(2)}, u32[]{:S(2)}) collective-permute-start(f32[4,32,640]{2,1,0:T(8,128)S(1)} %slice.116), channel_id=1, source_target_pairs={{0,4},{4,0},{1,5},{5,1},{2,6},{6,2},{3,7},{7,3},{8,12},{12,8},{9,1... | collective-permute-start | bytes 983048 | tf_op jit(solution)/shard_map/ppermute | solution.py:163
  79.6 1.6 %collective-permute-start.17 = (f32[4,32,512]{2,1,0:T(8,128)S(1)}, f32[4,32,512]{2,1,0:T(8,128)S(1)}, u32[]{:S(2)}, u32[]{:S(2)}) collective-permute-start(f32[4,32,512]{2,1,0:T(8,128)S(1)} %slice.98), channel_id=1, source_target_pairs={{0,4},{4,0},{1,5},{5,1},{2,6},{6,2},{3,7},{7,3},{8,12},{12,8},{9,1... | collective-permute-start | bytes 786440 | tf_op jit(solution)/shard_map/ppermute | solution.py:163
  79.8 7.3 %collective-permute-start.21 = (f32[2,32,896]{2,1,0:T(8,128)S(1)}, f32[2,32,896]{2,1,0:T(8,128)S(1)}, u32[]{:S(2)}, u32[]{:S(2)}) collective-permute-start(f32[2,32,896]{2,1,0:T(8,128)S(1)} %slice_add_fusion.11), channel_id=1, source_target_pairs={{0,32},{4,228},{32,64},{36,4},{64,96},{68,36},{96,128},{100,68},{1... | collective-permute-start | bytes 688136 | tf_op jit(solution)/shard_map/ppermute | solution.py:168
  81.4 8.3 %collective-permute-start.19 = (f32[32,1152]{1,0:T(8,128)S(1)}, f32[32,1152]{1,0:T(8,128)S(1)}, u32[]{:S(2)}, u32[]{:S(2)}) collective-permute-start(f32[32,1152]{1,0:T(8,128)S(1)} %get-tuple-element.65), channel_id=1, source_target_pairs={{0,16},{8,24},{16,0},{24,8},{1,17},{9,25},{17,1},{25,9},{2,18},{10... | collective-permute-start | bytes 442376 | tf_op jit(solution)/shard_map/ppermute | solution.py:173
  84.2 6.9 %collective-permute-start.20 = (f32[32,1152]{1,0:T(8,128)S(1)}, f32[32,1152]{1,0:T(8,128)S(1)}, u32[]{:S(2)}, u32[]{:S(2)}) collective-permute-start(f32[32,1152]{1,0:T(8,128)S(1)} %get-tuple-element.66), channel_id=1, source_target_pairs={{0,24},{8,0},{16,8},{24,16},{1,25},{9,1},{17,9},{25,17},{2,26},{10... | collective-permute-start | bytes 442376 | tf_op jit(solution)/shard_map/ppermute | solution.py:173
  85.7 6.8 %collective-permute-start.18 = (f32[32,1152]{1,0:T(8,128)S(1)}, f32[32,1152]{1,0:T(8,128)S(1)}, u32[]{:S(2)}, u32[]{:S(2)}) collective-permute-start(f32[32,1152]{1,0:T(8,128)S(1)} %get-tuple-element.67), channel_id=1, source_target_pairs={{0,8},{8,16},{16,24},{24,0},{1,9},{9,17},{17,25},{25,1},{2,10},{10... | collective-permute-start | bytes 442376 | tf_op jit(solution)/shard_map/ppermute | solution.py:173
  87.1 7.3 %collective-permute-start.22 = (f32[2,32,896]{2,1,0:T(8,128)S(1)}, f32[2,32,896]{2,1,0:T(8,128)S(1)}, u32[]{:S(2)}, u32[]{:S(2)}) collective-permute-start(f32[2,32,896]{2,1,0:T(8,128)S(1)} %slice_add_fusion.9), channel_id=1, source_target_pairs={{0,32},{4,228},{32,64},{36,4},{64,96},{68,36},{96,128},{100,68},{1... | collective-permute-start | bytes 688136 | tf_op jit(solution)/shard_map/ppermute | solution.py:168
  94.5 7.3 %collective-permute-start.23 = (f32[2,32,896]{2,1,0:T(8,128)S(1)}, f32[2,32,896]{2,1,0:T(8,128)S(1)}, u32[]{:S(2)}, u32[]{:S(2)}) collective-permute-start(f32[2,32,896]{2,1,0:T(8,128)S(1)} %slice_add_fusion.10), channel_id=1, source_target_pairs={{0,32},{4,228},{32,64},{36,4},{64,96},{68,36},{96,128},{100,68},{1... | collective-permute-start | bytes 688136 | tf_op jit(solution)/shard_map/ppermute | solution.py:168
  (5 other events, 155.7 us)

commit v7 on v6

--- a/solution.py
+++ b/solution.py
@@ -15,7 +15,7 @@
 DP = ("z", "x", "c")
 NZ, NX = 8, 4
 SIZE = {"z": NZ, "x": NX}
-COLS_Z = 1152
+COLS_Z = 1280
 
 
 def dot(lhs_ref, rhs_ref, z, start, cols):
@@ -230,11 +230,12 @@
 
     next_z = onward(next_z, "z")
     z = [next_z[..., cut] for cut in cuts]
+    steps = []
     for pair in (pair2, pair1):
-        steps = hop_z(pair, z)
-        z = [onward(part, "z") for part in steps]
+        steps.append(hop_z(pair, z))
+        z = [onward(part, "z") for part in steps[-1]]
     x = after(onward(first_x, "x"), pair1[0])
-    x = after(onward(add(both(pair_x)[:16], x), "x"), z[0], steps[1])
+    x = after(onward(add(both(pair_x)[:16], x), "x"), steps[0][1])
     sum_x = x[:8] + other_core(x[8:]) + both(pair_x)[16:24]
 
     moving = onward(sum_x[6:7], "z")

time: 141 us -> 140 us (level)
    ppermute x10, waiting for transfers between devices: 5.07 us -> 2.77 us  [other_core(): return lax.ppermute(value, 'c', [(0, 1), (1, 0)])]
  transfers between devices with their start and end apart: 25 -> 25, of which waited for: 16 -> 16; matrix products, arithmetic and copies ran while one was open for 2% -> 2% of each run, Pallas kernels for 11% -> 10%
where the time goes in v7:
time: 140 us; the launch traced here: 139 us
  waiting for transfers between devices  63.5 us (45%)
  blocking collectives  34.6 us (25%)
  Pallas kernels  18.2 us (13%)
  starting transfers between devices  16.4 us (12%)
  other arithmetic  4.83 us (3%)
  between operations  1.71 us (1%)
    ppermute x12, waiting for transfers between devices, onward(): lax.ppermute(value, (axis, 'c'), [(2 * i + c, 2 * ((i + 1 - 2 * c) % n) +...  54.7 us
    all_to_all x2, blocking collectives, sum_over(): return jnp.sum(lax.all_to_all(copies, axes, 0, 0, tiled=True), axis=0)  25.4 us
    pallas_call x4, Pallas kernels, product(): pl.pallas_call(kernel, in_specs=[pl.BlockSpec(memory_space=pltpu.SMEM), V...  14.1 us
    psum x1, blocking collectives, shards(): norms = jnp.sqrt(lax.psum(squares, 'y'))  9.19 us
    ppermute x10, starting transfers between devices, other_core(): return lax.ppermute(value, 'c', [(0, 1), (1, 0)])  8.35 us
    ppermute x3, waiting for transfers between devices, shift(): return lax.ppermute(value, axis, [(i, (i + by) % n) for i in range(n)])  5.96 us
    ppermute x12, starting transfers between devices, onward(): lax.ppermute(value, (axis, 'c'), [(2 * i + c, 2 * ((i + 1 - 2 * c) % n) +...  4.56 us
    pallas_call x1, Pallas kernels, product_far(): pl.pallas_call(functools.partial(product_far_kernel, COLS_Z), in_specs=[p...  4.07 us
  transfers between devices with their start and end apart: 25, of which 16 were waited for; matrix products, arithmetic and copies ran while one was open for 2% of the time, Pallas kernels for 10%

profile of v7, /device:TPU:8, one launch (start us, length us, event | category | flops | bytes accessed | tf_op | source)
XLA Modules:
  0.0 139.3 jit_solution(3018845765319062031)
XLA Ops:
  0.7 4.1 %shard_map.85 = (bf16[1024,2048]{1,0:T(8,128)(2,1)S(1)}, bf16[1024,2048]{1,0:T(8,128)(2,1)S(1)}, f32[4,32,1280]{2,1,0:T(8,128)S(1)}, f32[4,32,1280]{2,1,0:T(8,128)S(1)}) custom-call(s32[3]{0:T(128)S(1)} %pad_add_fusion.1.where_ref, bf16[1024,2048]{1,0:T(8,128)(2,1)} %lhs_hbm.1, bf16[1024,2048]{1,0:T(8,128)(2,1)} %rhs_hbm.1), custom_call_target="tpu_custom_call" | custom-call | flops 327680 | bytes 256 | tf_op jit(solution)/shard_map/pallas_call | solution.py:141
  4.9 2.3 %shard_map.86 = (f32[8,32,1280]{2,1,0:T(8,128)S(1)}, f32[8,32,1280]{2,1,0:T(8,128)S(1)}) custom-call(s32[3]{0:T(128)S(1)} %pad_add_fusion.1.where_ref, bf16[1024,2048]{1,0:T(8,128)(2,1)S(1)} %get-tuple-element.34.lhs_ref, bf16[1024,2048]{1,0:T(8,128)(2,1)S(1)} %get-tuple-element.35.rhs_ref), custom_call_target="tpu_custom_call" | custom-call | flops 655360 | bytes 512 | tf_op jit(solution)/shard_map/pallas_call | solution.py:128
  7.9 2.0 %collective-permute-start.3 = (f32[4,32,1280]{2,1,0:T(8,128)S(1)}, f32[4,32,1280]{2,1,0:T(8,128)S(1)}, u32[]{:S(2)}, u32[]{:S(2)}) collective-permute-start(f32[4,32,1280]{2,1,0:T(8,128)S(1)} %add.119), channel_id=1, source_target_pairs={{0,32},{4,228},{32,64},{36,4},{64,96},{68,36},{96,128},{100,68},{1... | collective-permute-start | bytes 1966088 | tf_op jit(solution)/shard_map/ppermute | solution.py:168
  9.8 6.3 %shard_map.87 = (f32[8,32,768]{2,1,0:T(8,128)S(1)}, f32[8,32,768]{2,1,0:T(8,128)S(1)}, f32[24,32,768]{2,1,0:T(8,128)S(1)}, f32[24,32,768]{2,1,0:T(8,128)S(1)}) custom-call(s32[3]{0:T(128)S(1)} %pad_add_fusion.1.where_ref, bf16[1024,2048]{1,0:T(8,128)(2,1)S(1)} %get-tuple-element.34.lhs_ref, bf16[1024,2048]{1,0:T(8,128)(2,1)S(1)} %get-tuple-element.35.rhs_ref), custom_call_target="tpu_custom_call" | custom-call | flops 1572864 | bytes 2048 | tf_op jit(solution)/shard_map/pallas_call | solution.py:128
  16.2 3.8 %collective-permute-start.1 = (f32[8,32,768]{2,1,0:T(8,128)S(1)}, f32[8,32,768]{2,1,0:T(8,128)S(1)}, u32[]{:S(2)}, u32[]{:S(2)}) collective-permute-start(f32[8,32,768]{2,1,0:T(8,128)S(1)} %get-tuple-element.42), channel_id=1, source_target_pairs={{0,4},{4,0},{1,5},{5,1},{2,6},{6,2},{3,7},{7,3},{8,12},{12,8},{9,1... | collective-permute-start | bytes 2359304 | tf_op jit(solution)/shard_map/ppermute | solution.py:163
  20.0 2.3 %shard_map.88 = (f32[8,32,1280]{2,1,0:T(8,128)S(1)}, f32[8,32,1280]{2,1,0:T(8,128)S(1)}) custom-call(s32[3]{0:T(128)S(1)} %pad_add_fusion.1.where_ref, bf16[1024,2048]{1,0:T(8,128)(2,1)S(1)} %get-tuple-element.34.lhs_ref, bf16[1024,2048]{1,0:T(8,128)(2,1)S(1)} %get-tuple-element.35.rhs_ref), custom_call_target="tpu_custom_call" | custom-call | flops 655360 | bytes 512 | tf_op jit(solution)/shard_map/pallas_call | solution.py:128
  22.8 1.6 %collective-permute-start.13 = (f32[8,32,768]{2,1,0:T(8,128)S(1)}, f32[8,32,768]{2,1,0:T(8,128)S(1)}, u32[]{:S(2)}, u32[]{:S(2)}) collective-permute-start(f32[8,32,768]{2,1,0:T(8,128)S(1)} %add.122), channel_id=1, source_target_pairs={{0,8},{4,28},{8,16},{12,4},{16,24},{20,12},{24,0},{28,20},{1,9},{5... | collective-permute-start | bytes 2359304 | tf_op jit(solution)/shard_map/ppermute | solution.py:168
  25.8 3.1 %shard_map.89 = (f32[12,32,1280]{2,1,0:T(8,128)S(1)}, f32[12,32,1280]{2,1,0:T(8,128)S(1)}) custom-call(s32[3]{0:T(128)S(1)} %pad_add_fusion.1.where_ref, bf16[1024,2048]{1,0:T(8,128)(2,1)S(1)} %get-tuple-element.34.lhs_ref, bf16[1024,2048]{1,0:T(8,128)(2,1)S(1)} %get-tuple-element.35.rhs_ref), custom_call_target="tpu_custom_call" | custom-call | flops 983040 | bytes 768 | tf_op jit(solution)/shard_map/pallas_call | solution.py:128
  28.9 2.0 %collective-permute-start.4 = (f32[12,32,1280]{2,1,0:T(8,128)S(1)}, f32[12,32,1280]{2,1,0:T(8,128)S(1)}, u32[]{:S(2)}, u32[]{:S(2)}) collective-permute-start(f32[12,32,1280]{2,1,0:T(8,128)S(1)} %get-tuple-element.48), channel_id=1, source_target_pairs={{0,4},{4,0},{1,5},{5,1},{2,6},{6,2},{3,7},{7,3},{8,12},{12,8},{9,1... | collective-permute-start | bytes 5898248 | tf_op jit(solution)/shard_map/ppermute | solution.py:163
  30.9 5.1 %collective-permute-done.13 = f32[8,32,768]{2,1,0:T(8,128)S(1)} collective-permute-done((f32[8,32,768]{2,1,0:T(8,128)S(1)}, f32[8,32,768]{2,1,0:T(8,128)S(1)}, u32[]{:S(2)}, u32[]{:S(2)}) %collective-permute-start.13) | collective-permute-done | bytes 786464 | tf_op jit(solution)/shard_map/ppermute | solution.py:168
  37.1 7.5 %collective-permute-done.6 = f32[8,32,1280]{2,1,0:T(8,128)S(1)} collective-permute-done((f32[8,32,1280]{2,1,0:T(8,128)S(1)}, f32[8,32,1280]{2,1,0:T(8,128)S(1)}, u32[]{:S(2)}, u32[]{:S(2)}) %collective-permute-start.6) | collective-permute-done | bytes 1310752 | tf_op jit(solution)/shard_map/ppermute | solution.py:168
  45.3 13.0 %collective-permute-done.14 = f32[16,32,768]{2,1,0:T(8,128)S(1)} collective-permute-done((f32[16,32,768]{2,1,0:T(8,128)S(1)}, f32[16,32,768]{2,1,0:T(8,128)S(1)}, u32[]{:S(2)}, u32[]{:S(2)}) %collective-permute-start.14) | collective-permute-done | bytes 1572896 | tf_op jit(solution)/shard_map/ppermute | solution.py:168
  58.6 5.0 %collective-permute-done.10 = f32[8,32,640]{2,1,0:T(8,128)S(1)} collective-permute-done((f32[8,32,640]{2,1,0:T(8,128)S(1)}, f32[8,32,640]{2,1,0:T(8,128)S(1)}, u32[]{:S(2)}, u32[]{:S(2)}) %collective-permute-start.10) | collective-permute-done | bytes 655392 | tf_op jit(solution)/shard_map/ppermute | solution.py:168
  64.1 6.5 %collective-permute-done.8 = f32[8,32,640]{2,1,0:T(8,128)S(1)} collective-permute-done((f32[8,32,640]{2,1,0:T(8,128)S(1)}, f32[8,32,640]{2,1,0:T(8,128)S(1)}, u32[]{:S(2)}, u32[]{:S(2)}) %collective-permute-start.8) | collective-permute-done | bytes 655392 | tf_op jit(solution)/shard_map/ppermute | solution.py:168
  70.8 6.9 %collective-permute-done.11 = f32[8,32,640]{2,1,0:T(8,128)S(1)} collective-permute-done((f32[8,32,640]{2,1,0:T(8,128)S(1)}, f32[8,32,640]{2,1,0:T(8,128)S(1)}, u32[]{:S(2)}, u32[]{:S(2)}) %collective-permute-start.11) | collective-permute-done | bytes 655392 | tf_op jit(solution)/shard_map/ppermute | solution.py:168
  79.0 1.5 %collective-permute-done.17 = f32[4,32,640]{2,1,0:T(8,128)S(1)} collective-permute-done((f32[4,32,640]{2,1,0:T(8,128)S(1)}, f32[4,32,640]{2,1,0:T(8,128)S(1)}, u32[]{:S(2)}, u32[]{:S(2)}) %collective-permute-start.17) | collective-permute-done | bytes 327712 | tf_op jit(solution)/shard_map/ppermute | solution.py:163
  82.1 1.4 %collective-permute-start.20 = (f32[32,1280]{1,0:T(8,128)S(1)}, f32[32,1280]{1,0:T(8,128)S(1)}, u32[]{:S(2)}, u32[]{:S(2)}) collective-permute-start(f32[32,1280]{1,0:T(8,128)S(1)} %get-tuple-element.68), channel_id=1, source_target_pairs={{0,24},{8,0},{16,8},{24,16},{1,25},{9,1},{17,9},{25,17},{2,26},{10... | collective-permute-start | bytes 491528 | tf_op jit(solution)/shard_map/ppermute | solution.py:173
  84.1 1.8 %collective-permute-done.21 = f32[2,32,768]{2,1,0:T(8,128)S(1)} collective-permute-done((f32[2,32,768]{2,1,0:T(8,128)S(1)}, f32[2,32,768]{2,1,0:T(8,128)S(1)}, u32[]{:S(2)}, u32[]{:S(2)}) %collective-permute-start.21) | collective-permute-done | bytes 196640 | tf_op jit(solution)/shard_map/ppermute | solution.py:168
  86.0 3.3 %collective-permute-done.19 = f32[32,1280]{1,0:T(8,128)S(1)} collective-permute-done((f32[32,1280]{1,0:T(8,128)S(1)}, f32[32,1280]{1,0:T(8,128)S(1)}, u32[]{:S(2)}, u32[]{:S(2)}) %collective-permute-start.19) | collective-permute-done | bytes 163872 | tf_op jit(solution)/shard_map/ppermute | solution.py:173
  90.5 1.5 %collective-permute-done.18 = f32[32,1280]{1,0:T(8,128)S(1)} collective-permute-done((f32[32,1280]{1,0:T(8,128)S(1)}, f32[32,1280]{1,0:T(8,128)S(1)}, u32[]{:S(2)}, u32[]{:S(2)}) %collective-permute-start.18) | collective-permute-done | bytes 163872 | tf_op jit(solution)/shard_map/ppermute | solution.py:173
  93.0 6.9 %collective-permute-done.23 = f32[2,32,768]{2,1,0:T(8,128)S(1)} collective-permute-done((f32[2,32,768]{2,1,0:T(8,128)S(1)}, f32[2,32,768]{2,1,0:T(8,128)S(1)}, u32[]{:S(2)}, u32[]{:S(2)}) %collective-permute-start.23) | collective-permute-done | bytes 196640 | tf_op jit(solution)/shard_map/ppermute | solution.py:168
  101.4 13.6 %all_to_all.10 = f32[16,8,128]{2,1,0:T(8,128)S(1)} all-to-all(f32[16,8,128]{2,1,0:T(8,128)S(1)} %broadcast_in_dim.4), channel_id=1, replica_groups=mesh['z'=8,'x'=4,'c'=2,'y'=4] {'z','c'}, dimensions={0} | all-to-all | bytes 131072 | tf_op jit(solution)/shard_map/all_to_all | solution.py:182
  115.1 11.8 %all_to_all.11 = f32[16,8,128]{2,1,0:T(8,128)S(1)} all-to-all(f32[16,8,128]{2,1,0:T(8,128)S(1)} %broadcast_in_dim.5), channel_id=1, replica_groups=mesh['z'=8,'x'=4,'c'=2,'y'=4] {'x','y'}, dimensions={0} | all-to-all | bytes 131072 | tf_op jit(solution)/shard_map/all_to_all | solution.py:182
  129.3 9.2 %psum.7 = f32[2,32]{1,0:T(2,128)S(1)} all-reduce(f32[2,32]{1,0:T(2,128)S(1)} %pad_maximum_fusion), channel_id=1, replica_groups=mesh['z'=8,'x'=4,'c'=2,'y'=4] {'y'}, use_global_device_ids=true, to_apply=%region_5.0 | all-reduce | flops 64 | bytes 512 | tf_op jit(solution)/shard_map/psum | solution.py:262
  (79 shorter events, 15.2 us)
Async XLA Ops:
  4.8 3.0 %collective-permute-start = (f32[4,32,1280]{2,1,0:T(8,128)S(1)}, f32[4,32,1280]{2,1,0:T(8,128)S(1)}, u32[]{:S(2)}, u32[]{:S(2)}) collective-permute-start(f32[4,32,1280]{2,1,0:T(8,128)S(1)} %get-tuple-element.37), channel_id=1, source_target_pairs={{0,4},{4,0},{1,5},{5,1},{2,6},{6,2},{3,7},{7,3},{8,12},{12,8},{9,1... | collective-permute-start | bytes 1966088 | tf_op jit(solution)/shard_map/ppermute | solution.py:163
  7.2 15.2 %collective-permute-start.2 = (f32[8,32,1280]{2,1,0:T(8,128)S(1)}, f32[8,32,1280]{2,1,0:T(8,128)S(1)}, u32[]{:S(2)}, u32[]{:S(2)}) collective-permute-start(f32[8,32,1280]{2,1,0:T(8,128)S(1)} %get-tuple-element.43), channel_id=1, source_target_pairs={{0,4},{4,0},{1,5},{5,1},{2,6},{6,2},{3,7},{7,3},{8,12},{12,8},{9,1... | collective-permute-start | bytes 3932168 | tf_op jit(solution)/shard_map/ppermute | solution.py:163
  7.9 14.5 %collective-permute-start.3 = (f32[4,32,1280]{2,1,0:T(8,128)S(1)}, f32[4,32,1280]{2,1,0:T(8,128)S(1)}, u32[]{:S(2)}, u32[]{:S(2)}) collective-permute-start(f32[4,32,1280]{2,1,0:T(8,128)S(1)} %add.119), channel_id=1, source_target_pairs={{0,32},{4,228},{32,64},{36,4},{64,96},{68,36},{96,128},{100,68},{1... | collective-permute-start | bytes 1966088 | tf_op jit(solution)/shard_map/ppermute | solution.py:168
  16.2 6.4 %collective-permute-start.1 = (f32[8,32,768]{2,1,0:T(8,128)S(1)}, f32[8,32,768]{2,1,0:T(8,128)S(1)}, u32[]{:S(2)}, u32[]{:S(2)}) collective-permute-start(f32[8,32,768]{2,1,0:T(8,128)S(1)} %get-tuple-element.42), channel_id=1, source_target_pairs={{0,4},{4,0},{1,5},{5,1},{2,6},{6,2},{3,7},{7,3},{8,12},{12,8},{9,1... | collective-permute-start | bytes 2359304 | tf_op jit(solution)/shard_map/ppermute | solution.py:163
  22.7 13.4 %collective-permute-start.12 = (f32[24,32,768]{2,1,0:T(8,128)S(1)}, f32[24,32,768]{2,1,0:T(8,128)S(1)}, u32[]{:S(2)}, u32[]{:S(2)}) collective-permute-start(f32[24,32,768]{2,1,0:T(8,128)S(1)} %get-tuple-element.54), channel_id=1, source_target_pairs={{0,4},{4,0},{1,5},{5,1},{2,6},{6,2},{3,7},{7,3},{8,12},{12,8},{9,1... | collective-permute-start | bytes 7077896 | tf_op jit(solution)/shard_map/ppermute | solution.py:163
  22.8 13.3 %collective-permute-start.13 = (f32[8,32,768]{2,1,0:T(8,128)S(1)}, f32[8,32,768]{2,1,0:T(8,128)S(1)}, u32[]{:S(2)}, u32[]{:S(2)}) collective-permute-start(f32[8,32,768]{2,1,0:T(8,128)S(1)} %add.122), channel_id=1, source_target_pairs={{0,8},{4,28},{8,16},{12,4},{16,24},{20,12},{24,0},{28,20},{1,9},{5... | collective-permute-start | bytes 2359304 | tf_op jit(solution)/shard_map/ppermute | solution.py:168
  24.4 12.5 %collective-permute-start.5 = (f32[8,32,1280]{2,1,0:T(8,128)S(1)}, f32[8,32,1280]{2,1,0:T(8,128)S(1)}, u32[]{:S(2)}, u32[]{:S(2)}) collective-permute-start(f32[8,32,1280]{2,1,0:T(8,128)S(1)} %get-tuple-element.49), channel_id=1, source_target_pairs={{0,4},{4,0},{1,5},{5,1},{2,6},{6,2},{3,7},{7,3},{8,12},{12,8},{9,1... | collective-permute-start | bytes 3932168 | tf_op jit(solution)/shard_map/ppermute | solution.py:163
  25.8 18.8 %collective-permute-start.6 = (f32[8,32,1280]{2,1,0:T(8,128)S(1)}, f32[8,32,1280]{2,1,0:T(8,128)S(1)}, u32[]{:S(2)}, u32[]{:S(2)}) collective-permute-start(f32[8,32,1280]{2,1,0:T(8,128)S(1)} %pad_add_fusion), channel_id=1, source_target_pairs={{0,32},{4,228},{32,64},{36,4},{64,96},{68,36},{96,128},{100,68},{1... | collective-permute-start | bytes 3932168 | tf_op jit(solution)/shard_map/ppermute | solution.py:168
  28.9 16.1 %collective-permute-start.4 = (f32[12,32,1280]{2,1,0:T(8,128)S(1)}, f32[12,32,1280]{2,1,0:T(8,128)S(1)}, u32[]{:S(2)}, u32[]{:S(2)}) collective-permute-start(f32[12,32,1280]{2,1,0:T(8,128)S(1)} %get-tuple-element.48), channel_id=1, source_target_pairs={{0,4},{4,0},{1,5},{5,1},{2,6},{6,2},{3,7},{7,3},{8,12},{12,8},{9,1... | collective-permute-start | bytes 5898248 | tf_op jit(solution)/shard_map/ppermute | solution.py:163
  36.5 21.7 %collective-permute-start.14 = (f32[16,32,768]{2,1,0:T(8,128)S(1)}, f32[16,32,768]{2,1,0:T(8,128)S(1)}, u32[]{:S(2)}, u32[]{:S(2)}) collective-permute-start(f32[16,32,768]{2,1,0:T(8,128)S(1)} %slice_add_fusion), channel_id=1, source_target_pairs={{0,8},{4,28},{8,16},{12,4},{16,24},{20,12},{24,0},{28,20},{1,9},{5... | collective-permute-start | bytes 4718600 | tf_op jit(solution)/shard_map/ppermute | solution.py:168
  44.7 13.7 %collective-permute-start.7 = (f32[8,32,640]{2,1,0:T(8,128)S(1)}, f32[8,32,640]{2,1,0:T(8,128)S(1)}, u32[]{:S(2)}, u32[]{:S(2)}) collective-permute-start(f32[8,32,640]{2,1,0:T(8,128)S(1)} %get-tuple-element.65), channel_id=1, source_target_pairs={{0,32},{4,228},{32,64},{36,4},{64,96},{68,36},{96,128},{100,68},{1... | collective-permute-start | bytes 1966088 | tf_op jit(solution)/shard_map/ppermute | solution.py:168
  44.9 18.7 %collective-permute-start.10 = (f32[8,32,640]{2,1,0:T(8,128)S(1)}, f32[8,32,640]{2,1,0:T(8,128)S(1)}, u32[]{:S(2)}, u32[]{:S(2)}) collective-permute-start(f32[8,32,640]{2,1,0:T(8,128)S(1)} %slice_add_fusion.3), channel_id=1, source_target_pairs={{0,32},{4,228},{32,64},{36,4},{64,96},{68,36},{96,128},{100,68},{1... | collective-permute-start | bytes 1966088 | tf_op jit(solution)/shard_map/ppermute | solution.py:168
  58.3 5.5 %collective-permute-start.15 = (f32[8,32,768]{2,1,0:T(8,128)S(1)}, f32[8,32,768]{2,1,0:T(8,128)S(1)}, u32[]{:S(2)}, u32[]{:S(2)}) collective-permute-start(f32[8,32,768]{2,1,0:T(8,128)S(1)} %slice.94), channel_id=1, source_target_pairs={{0,4},{4,0},{1,5},{5,1},{2,6},{6,2},{3,7},{7,3},{8,12},{12,8},{9,1... | collective-permute-start | bytes 2359304 | tf_op jit(solution)/shard_map/ppermute | solution.py:163
  58.5 12.1 %collective-permute-start.8 = (f32[8,32,640]{2,1,0:T(8,128)S(1)}, f32[8,32,640]{2,1,0:T(8,128)S(1)}, u32[]{:S(2)}, u32[]{:S(2)}) collective-permute-start(f32[8,32,640]{2,1,0:T(8,128)S(1)} %slice_add_fusion.6), channel_id=1, source_target_pairs={{0,32},{4,228},{32,64},{36,4},{64,96},{68,36},{96,128},{100,68},{1... | collective-permute-start | bytes 1966088 | tf_op jit(solution)/shard_map/ppermute | solution.py:168
  63.7 14.0 %collective-permute-start.11 = (f32[8,32,640]{2,1,0:T(8,128)S(1)}, f32[8,32,640]{2,1,0:T(8,128)S(1)}, u32[]{:S(2)}, u32[]{:S(2)}) collective-permute-start(f32[8,32,640]{2,1,0:T(8,128)S(1)} %slice_add_fusion.4), channel_id=1, source_target_pairs={{0,32},{4,228},{32,64},{36,4},{64,96},{68,36},{96,128},{100,68},{1... | collective-permute-start | bytes 1966088 | tf_op jit(solution)/shard_map/ppermute | solution.py:168
  64.0 14.7 %collective-permute-start.16 = (f32[1,32,768]{2,1,0:T(8,128)S(1)}, f32[1,32,768]{2,1,0:T(8,128)S(1)}, u32[]{:S(2)}, u32[]{:S(2)}) collective-permute-start(f32[1,32,768]{2,1,0:T(8,128)S(1)} %slice.122), channel_id=1, source_target_pairs={{0,32},{4,228},{32,64},{36,4},{64,96},{68,36},{96,128},{100,68},{1... | collective-permute-start | bytes 294920 | tf_op jit(solution)/shard_map/ppermute | solution.py:168
  70.7 8.2 %collective-permute-start.9 = (f32[4,32,640]{2,1,0:T(8,128)S(1)}, f32[4,32,640]{2,1,0:T(8,128)S(1)}, u32[]{:S(2)}, u32[]{:S(2)}) collective-permute-start(f32[4,32,640]{2,1,0:T(8,128)S(1)} %slice.116), channel_id=1, source_target_pairs={{0,4},{4,0},{1,5},{5,1},{2,6},{6,2},{3,7},{7,3},{8,12},{12,8},{9,1... | collective-permute-start | bytes 983048 | tf_op jit(solution)/shard_map/ppermute | solution.py:163
  78.8 1.7 %collective-permute-start.17 = (f32[4,32,640]{2,1,0:T(8,128)S(1)}, f32[4,32,640]{2,1,0:T(8,128)S(1)}, u32[]{:S(2)}, u32[]{:S(2)}) collective-permute-start(f32[4,32,640]{2,1,0:T(8,128)S(1)} %slice.98), channel_id=1, source_target_pairs={{0,4},{4,0},{1,5},{5,1},{2,6},{6,2},{3,7},{7,3},{8,12},{12,8},{9,1... | collective-permute-start | bytes 983048 | tf_op jit(solution)/shard_map/ppermute | solution.py:163
  78.9 7.0 %collective-permute-start.21 = (f32[2,32,768]{2,1,0:T(8,128)S(1)}, f32[2,32,768]{2,1,0:T(8,128)S(1)}, u32[]{:S(2)}, u32[]{:S(2)}) collective-permute-start(f32[2,32,768]{2,1,0:T(8,128)S(1)} %slice_add_fusion.11), channel_id=1, source_target_pairs={{0,32},{4,228},{32,64},{36,4},{64,96},{68,36},{96,128},{100,68},{1... | collective-permute-start | bytes 589832 | tf_op jit(solution)/shard_map/ppermute | solution.py:168
  80.7 8.6 %collective-permute-start.19 = (f32[32,1280]{1,0:T(8,128)S(1)}, f32[32,1280]{1,0:T(8,128)S(1)}, u32[]{:S(2)}, u32[]{:S(2)}) collective-permute-start(f32[32,1280]{1,0:T(8,128)S(1)} %get-tuple-element.67), channel_id=1, source_target_pairs={{0,16},{8,24},{16,0},{24,8},{1,17},{9,25},{17,1},{25,9},{2,18},{10... | collective-permute-start | bytes 491528 | tf_op jit(solution)/shard_map/ppermute | solution.py:173
  82.1 8.5 %collective-permute-start.20 = (f32[32,1280]{1,0:T(8,128)S(1)}, f32[32,1280]{1,0:T(8,128)S(1)}, u32[]{:S(2)}, u32[]{:S(2)}) collective-permute-start(f32[32,1280]{1,0:T(8,128)S(1)} %get-tuple-element.68), channel_id=1, source_target_pairs={{0,24},{8,0},{16,8},{24,16},{1,25},{9,1},{17,9},{25,17},{2,26},{10... | collective-permute-start | bytes 491528 | tf_op jit(solution)/shard_map/ppermute | solution.py:173
  83.5 8.5 %collective-permute-start.18 = (f32[32,1280]{1,0:T(8,128)S(1)}, f32[32,1280]{1,0:T(8,128)S(1)}, u32[]{:S(2)}, u32[]{:S(2)}) collective-permute-start(f32[32,1280]{1,0:T(8,128)S(1)} %get-tuple-element.69), channel_id=1, source_target_pairs={{0,8},{8,16},{16,24},{24,0},{1,9},{9,17},{17,25},{25,1},{2,10},{10... | collective-permute-start | bytes 491528 | tf_op jit(solution)/shard_map/ppermute | solution.py:173
  86.0 7.0 %collective-permute-start.22 = (f32[2,32,768]{2,1,0:T(8,128)S(1)}, f32[2,32,768]{2,1,0:T(8,128)S(1)}, u32[]{:S(2)}, u32[]{:S(2)}) collective-permute-start(f32[2,32,768]{2,1,0:T(8,128)S(1)} %slice_add_fusion.9), channel_id=1, source_target_pairs={{0,32},{4,228},{32,64},{36,4},{64,96},{68,36},{96,128},{100,68},{1... | collective-permute-start | bytes 589832 | tf_op jit(solution)/shard_map/ppermute | solution.py:168
  92.9 7.0 %collective-permute-start.23 = (f32[2,32,768]{2,1,0:T(8,128)S(1)}, f32[2,32,768]{2,1,0:T(8,128)S(1)}, u32[]{:S(2)}, u32[]{:S(2)}) collective-permute-start(f32[2,32,768]{2,1,0:T(8,128)S(1)} %slice_add_fusion.10), channel_id=1, source_target_pairs={{0,32},{4,228},{32,64},{36,4},{64,96},{68,36},{96,128},{100,68},{1... | collective-permute-start | bytes 589832 | tf_op jit(solution)/shard_map/ppermute | solution.py:168
  (5 other events, 148.9 us)

commit v8 on v7

--- a/solution.py
+++ b/solution.py
@@ -171,6 +171,12 @@
 def shift(value, axis, by):
     n = SIZE[axis]
     return lax.ppermute(value, axis, [(i, (i + by) % n) for i in range(n)])
+
+
+def onward_apart(value, axis):
+    n, half = SIZE[axis], value.shape[0] // 2
+    cross = [(2 * i + c, 2 * ((i + 1 - 2 * c) % n) + 1 - c) for i in range(n) for c in range(2)]
+    return onward(value[:half], axis) + lax.ppermute(value[half:], (axis, "c"), cross)
 
 
 def at_front(part, whole):
@@ -247,8 +253,7 @@
     batch_z = sum_z[0] + sum(shift(sum_z[k], "x", k) for k in (1, 2, 3))
     moving = onward(moving, "z")
     moving = onward(sum_x[2:4] + moving, "z")
-    moving = onward(sum_x[0:2] + after(moving, batch_z), "z")
-    batch_x = moving[0] + other_core(moving[1]) + sum_x[7]
+    batch_x = onward_apart(sum_x[0:2] + after(moving, batch_z), "z")[0] + sum_x[7]
     gradient = grad_acc + jnp.concatenate([batch_z, batch_x], axis=1)
 
     energy = jnp.sum((gradient * gradient).reshape(4, 8, 16, 128), axis=(0, 2))

time: 140 us -> 137 us (0.979)
  waiting for transfers between devices: 63.5 us -> 61.1 us
    ppermute x12, waiting for transfers between devices: 54.7 us -> 49.7 us  [onward(): lax.ppermute(value, (axis, 'c'), [(2 * i + c, 2 * ((i + 1 - 2 * c) % n) +...]
    ppermute x0 -> x1, waiting for transfers between devices: none -> 3.94 us  [onward_apart(): lax.ppermute(value[half:], (axis, 'c'), cross)]
    ppermute x10 -> x9, starting transfers between devices: 8.35 us -> 8.26 us  [other_core(): return lax.ppermute(value, 'c', [(0, 1), (1, 0)])]
where the time goes in v8:
time: 137 us
  waiting for transfers between devices  61.1 us (45%)
  blocking collectives  34.6 us (25%)
  Pallas kernels  18.2 us (13%)
  starting transfers between devices  16.4 us (12%)
  other arithmetic  4.83 us (4%)
  between operations  1.72 us (1%)
    ppermute x12, waiting for transfers between devices, onward(): lax.ppermute(value, (axis, 'c'), [(2 * i + c, 2 * ((i + 1 - 2 * c) % n) +...  49.7 us
    all_to_all x2, blocking collectives, sum_over(): return jnp.sum(lax.all_to_all(copies, axes, 0, 0, tiled=True), axis=0)  25.4 us
    pallas_call x4, Pallas kernels, product(): pl.pallas_call(kernel, in_specs=[pl.BlockSpec(memory_space=pltpu.SMEM), V...  14.1 us
    psum x1, blocking collectives, shards(): norms = jnp.sqrt(lax.psum(squares, 'y'))  9.19 us
    ppermute x9, starting transfers between devices, other_core(): return lax.ppermute(value, 'c', [(0, 1), (1, 0)])  8.26 us
    ppermute x3, waiting for transfers between devices, shift(): return lax.ppermute(value, axis, [(i, (i + by) % n) for i in range(n)])  5.96 us
    ppermute x12, starting transfers between devices, onward(): lax.ppermute(value, (axis, 'c'), [(2 * i + c, 2 * ((i + 1 - 2 * c) % n) +...  4.56 us
    pallas_call x1, Pallas kernels, product_far(): pl.pallas_call(functools.partial(product_far_kernel, COLS_Z), in_specs=[p...  4.07 us
  transfers between devices with their start and end apart: 25, of which 16 were waited for; matrix products, arithmetic and copies ran while one was open for 2% of the time, Pallas kernels for 10%

profile of v8, /device:TPU:8, one launch (start us, length us, event | category | flops | bytes accessed | tf_op | source)
XLA Modules:
  0.0 137.0 jit_solution(13082279462502592964)
XLA Ops:
  0.7 4.1 %shard_map.85 = (bf16[1024,2048]{1,0:T(8,128)(2,1)S(1)}, bf16[1024,2048]{1,0:T(8,128)(2,1)S(1)}, f32[4,32,1280]{2,1,0:T(8,128)S(1)}, f32[4,32,1280]{2,1,0:T(8,128)S(1)}) custom-call(s32[3]{0:T(128)S(1)} %pad_add_fusion.1.where_ref, bf16[1024,2048]{1,0:T(8,128)(2,1)} %lhs_hbm.1, bf16[1024,2048]{1,0:T(8,128)(2,1)} %rhs_hbm.1), custom_call_target="tpu_custom_call" | custom-call | flops 327680 | bytes 256 | tf_op jit(solution)/shard_map/pallas_call | solution.py:141
  4.9 2.3 %shard_map.86 = (f32[8,32,1280]{2,1,0:T(8,128)S(1)}, f32[8,32,1280]{2,1,0:T(8,128)S(1)}) custom-call(s32[3]{0:T(128)S(1)} %pad_add_fusion.1.where_ref, bf16[1024,2048]{1,0:T(8,128)(2,1)S(1)} %get-tuple-element.34.lhs_ref, bf16[1024,2048]{1,0:T(8,128)(2,1)S(1)} %get-tuple-element.35.rhs_ref), custom_call_target="tpu_custom_call" | custom-call | flops 655360 | bytes 512 | tf_op jit(solution)/shard_map/pallas_call | solution.py:128
  7.9 2.0 %collective-permute-start.3 = (f32[4,32,1280]{2,1,0:T(8,128)S(1)}, f32[4,32,1280]{2,1,0:T(8,128)S(1)}, u32[]{:S(2)}, u32[]{:S(2)}) collective-permute-start(f32[4,32,1280]{2,1,0:T(8,128)S(1)} %add.122), channel_id=1, source_target_pairs={{0,32},{4,228},{32,64},{36,4},{64,96},{68,36},{96,128},{100,68},{1... | collective-permute-start | bytes 1966088 | tf_op jit(solution)/shard_map/ppermute | solution.py:168
  9.8 6.3 %shard_map.87 = (f32[8,32,768]{2,1,0:T(8,128)S(1)}, f32[8,32,768]{2,1,0:T(8,128)S(1)}, f32[24,32,768]{2,1,0:T(8,128)S(1)}, f32[24,32,768]{2,1,0:T(8,128)S(1)}) custom-call(s32[3]{0:T(128)S(1)} %pad_add_fusion.1.where_ref, bf16[1024,2048]{1,0:T(8,128)(2,1)S(1)} %get-tuple-element.34.lhs_ref, bf16[1024,2048]{1,0:T(8,128)(2,1)S(1)} %get-tuple-element.35.rhs_ref), custom_call_target="tpu_custom_call" | custom-call | flops 1572864 | bytes 2048 | tf_op jit(solution)/shard_map/pallas_call | solution.py:128
  16.2 3.8 %collective-permute-start.1 = (f32[8,32,768]{2,1,0:T(8,128)S(1)}, f32[8,32,768]{2,1,0:T(8,128)S(1)}, u32[]{:S(2)}, u32[]{:S(2)}) collective-permute-start(f32[8,32,768]{2,1,0:T(8,128)S(1)} %get-tuple-element.42), channel_id=1, source_target_pairs={{0,4},{4,0},{1,5},{5,1},{2,6},{6,2},{3,7},{7,3},{8,12},{12,8},{9,1... | collective-permute-start | bytes 2359304 | tf_op jit(solution)/shard_map/ppermute | solution.py:163
  20.0 2.3 %shard_map.88 = (f32[8,32,1280]{2,1,0:T(8,128)S(1)}, f32[8,32,1280]{2,1,0:T(8,128)S(1)}) custom-call(s32[3]{0:T(128)S(1)} %pad_add_fusion.1.where_ref, bf16[1024,2048]{1,0:T(8,128)(2,1)S(1)} %get-tuple-element.34.lhs_ref, bf16[1024,2048]{1,0:T(8,128)(2,1)S(1)} %get-tuple-element.35.rhs_ref), custom_call_target="tpu_custom_call" | custom-call | flops 655360 | bytes 512 | tf_op jit(solution)/shard_map/pallas_call | solution.py:128
  22.8 1.6 %collective-permute-start.13 = (f32[8,32,768]{2,1,0:T(8,128)S(1)}, f32[8,32,768]{2,1,0:T(8,128)S(1)}, u32[]{:S(2)}, u32[]{:S(2)}) collective-permute-start(f32[8,32,768]{2,1,0:T(8,128)S(1)} %add.125), channel_id=1, source_target_pairs={{0,8},{4,28},{8,16},{12,4},{16,24},{20,12},{24,0},{28,20},{1,9},{5... | collective-permute-start | bytes 2359304 | tf_op jit(solution)/shard_map/ppermute | solution.py:168
  25.8 3.1 %shard_map.89 = (f32[12,32,1280]{2,1,0:T(8,128)S(1)}, f32[12,32,1280]{2,1,0:T(8,128)S(1)}) custom-call(s32[3]{0:T(128)S(1)} %pad_add_fusion.1.where_ref, bf16[1024,2048]{1,0:T(8,128)(2,1)S(1)} %get-tuple-element.34.lhs_ref, bf16[1024,2048]{1,0:T(8,128)(2,1)S(1)} %get-tuple-element.35.rhs_ref), custom_call_target="tpu_custom_call" | custom-call | flops 983040 | bytes 768 | tf_op jit(solution)/shard_map/pallas_call | solution.py:128
  28.9 2.0 %collective-permute-start.4 = (f32[12,32,1280]{2,1,0:T(8,128)S(1)}, f32[12,32,1280]{2,1,0:T(8,128)S(1)}, u32[]{:S(2)}, u32[]{:S(2)}) collective-permute-start(f32[12,32,1280]{2,1,0:T(8,128)S(1)} %get-tuple-element.48), channel_id=1, source_target_pairs={{0,4},{4,0},{1,5},{5,1},{2,6},{6,2},{3,7},{7,3},{8,12},{12,8},{9,1... | collective-permute-start | bytes 5898248 | tf_op jit(solution)/shard_map/ppermute | solution.py:163
  30.9 5.1 %collective-permute-done.13 = f32[8,32,768]{2,1,0:T(8,128)S(1)} collective-permute-done((f32[8,32,768]{2,1,0:T(8,128)S(1)}, f32[8,32,768]{2,1,0:T(8,128)S(1)}, u32[]{:S(2)}, u32[]{:S(2)}) %collective-permute-start.13) | collective-permute-done | bytes 786464 | tf_op jit(solution)/shard_map/ppermute | solution.py:168
  37.1 7.5 %collective-permute-done.6 = f32[8,32,1280]{2,1,0:T(8,128)S(1)} collective-permute-done((f32[8,32,1280]{2,1,0:T(8,128)S(1)}, f32[8,32,1280]{2,1,0:T(8,128)S(1)}, u32[]{:S(2)}, u32[]{:S(2)}) %collective-permute-start.6) | collective-permute-done | bytes 1310752 | tf_op jit(solution)/shard_map/ppermute | solution.py:168
  45.3 13.0 %collective-permute-done.14 = f32[16,32,768]{2,1,0:T(8,128)S(1)} collective-permute-done((f32[16,32,768]{2,1,0:T(8,128)S(1)}, f32[16,32,768]{2,1,0:T(8,128)S(1)}, u32[]{:S(2)}, u32[]{:S(2)}) %collective-permute-start.14) | collective-permute-done | bytes 1572896 | tf_op jit(solution)/shard_map/ppermute | solution.py:168
  58.6 5.0 %collective-permute-done.10 = f32[8,32,640]{2,1,0:T(8,128)S(1)} collective-permute-done((f32[8,32,640]{2,1,0:T(8,128)S(1)}, f32[8,32,640]{2,1,0:T(8,128)S(1)}, u32[]{:S(2)}, u32[]{:S(2)}) %collective-permute-start.10) | collective-permute-done | bytes 655392 | tf_op jit(solution)/shard_map/ppermute | solution.py:168
  64.1 6.5 %collective-permute-done.8 = f32[8,32,640]{2,1,0:T(8,128)S(1)} collective-permute-done((f32[8,32,640]{2,1,0:T(8,128)S(1)}, f32[8,32,640]{2,1,0:T(8,128)S(1)}, u32[]{:S(2)}, u32[]{:S(2)}) %collective-permute-start.8) | collective-permute-done | bytes 655392 | tf_op jit(solution)/shard_map/ppermute | solution.py:168
  70.8 6.9 %collective-permute-done.11 = f32[8,32,640]{2,1,0:T(8,128)S(1)} collective-permute-done((f32[8,32,640]{2,1,0:T(8,128)S(1)}, f32[8,32,640]{2,1,0:T(8,128)S(1)}, u32[]{:S(2)}, u32[]{:S(2)}) %collective-permute-start.11) | collective-permute-done | bytes 655392 | tf_op jit(solution)/shard_map/ppermute | solution.py:168
  79.0 1.5 %collective-permute-done.17 = f32[4,32,640]{2,1,0:T(8,128)S(1)} collective-permute-done((f32[4,32,640]{2,1,0:T(8,128)S(1)}, f32[4,32,640]{2,1,0:T(8,128)S(1)}, u32[]{:S(2)}, u32[]{:S(2)}) %collective-permute-start.17) | collective-permute-done | bytes 327712 | tf_op jit(solution)/shard_map/ppermute | solution.py:163
  84.1 1.8 %collective-permute-done.21 = f32[2,32,768]{2,1,0:T(8,128)S(1)} collective-permute-done((f32[2,32,768]{2,1,0:T(8,128)S(1)}, f32[2,32,768]{2,1,0:T(8,128)S(1)}, u32[]{:S(2)}, u32[]{:S(2)}) %collective-permute-start.21) | collective-permute-done | bytes 196640 | tf_op jit(solution)/shard_map/ppermute | solution.py:168
  86.0 3.3 %collective-permute-done.19 = f32[32,1280]{1,0:T(8,128)S(1)} collective-permute-done((f32[32,1280]{1,0:T(8,128)S(1)}, f32[32,1280]{1,0:T(8,128)S(1)}, u32[]{:S(2)}, u32[]{:S(2)}) %collective-permute-start.19) | collective-permute-done | bytes 163872 | tf_op jit(solution)/shard_map/ppermute | solution.py:173
  90.5 1.5 %collective-permute-done.18 = f32[32,1280]{1,0:T(8,128)S(1)} collective-permute-done((f32[32,1280]{1,0:T(8,128)S(1)}, f32[32,1280]{1,0:T(8,128)S(1)}, u32[]{:S(2)}, u32[]{:S(2)}) %collective-permute-start.18) | collective-permute-done | bytes 163872 | tf_op jit(solution)/shard_map/ppermute | solution.py:173
  93.2 3.9 %collective-permute-done.24 = f32[1,32,768]{2,1,0:T(8,128)S(1)} collective-permute-done((f32[1,32,768]{2,1,0:T(8,128)S(1)}, f32[1,32,768]{2,1,0:T(8,128)S(1)}, u32[]{:S(2)}, u32[]{:S(2)}) %collective-permute-start.24) | collective-permute-done | bytes 98336 | tf_op jit(solution)/shard_map/ppermute | solution.py:179
  97.1 1.9 %collective-permute-done.23 = f32[1,32,768]{2,1,0:T(8,128)S(1)} collective-permute-done((f32[1,32,768]{2,1,0:T(8,128)S(1)}, f32[1,32,768]{2,1,0:T(8,128)S(1)}, u32[]{:S(2)}, u32[]{:S(2)}) %collective-permute-start.23) | collective-permute-done | bytes 98336 | tf_op jit(solution)/shard_map/ppermute | solution.py:168
  99.1 13.6 %all_to_all.10 = f32[16,8,128]{2,1,0:T(8,128)S(1)} all-to-all(f32[16,8,128]{2,1,0:T(8,128)S(1)} %broadcast_in_dim.4), channel_id=1, replica_groups=mesh['z'=8,'x'=4,'c'=2,'y'=4] {'z','c'}, dimensions={0} | all-to-all | bytes 131072 | tf_op jit(solution)/shard_map/all_to_all | solution.py:188
  112.7 11.8 %all_to_all.11 = f32[16,8,128]{2,1,0:T(8,128)S(1)} all-to-all(f32[16,8,128]{2,1,0:T(8,128)S(1)} %broadcast_in_dim.5), channel_id=1, replica_groups=mesh['z'=8,'x'=4,'c'=2,'y'=4] {'x','y'}, dimensions={0} | all-to-all | bytes 131072 | tf_op jit(solution)/shard_map/all_to_all | solution.py:188
  127.0 9.2 %psum.7 = f32[2,32]{1,0:T(2,128)S(1)} all-reduce(f32[2,32]{1,0:T(2,128)S(1)} %pad_maximum_fusion), channel_id=1, replica_groups=mesh['z'=8,'x'=4,'c'=2,'y'=4] {'y'}, use_global_device_ids=true, to_apply=%region_5.0 | all-reduce | flops 64 | bytes 512 | tf_op jit(solution)/shard_map/psum | solution.py:267
  (79 shorter events, 15.3 us)
Async XLA Ops:
  4.8 3.0 %collective-permute-start = (f32[4,32,1280]{2,1,0:T(8,128)S(1)}, f32[4,32,1280]{2,1,0:T(8,128)S(1)}, u32[]{:S(2)}, u32[]{:S(2)}) collective-permute-start(f32[4,32,1280]{2,1,0:T(8,128)S(1)} %get-tuple-element.37), channel_id=1, source_target_pairs={{0,4},{4,0},{1,5},{5,1},{2,6},{6,2},{3,7},{7,3},{8,12},{12,8},{9,1... | collective-permute-start | bytes 1966088 | tf_op jit(solution)/shard_map/ppermute | solution.py:163
  7.2 15.2 %collective-permute-start.2 = (f32[8,32,1280]{2,1,0:T(8,128)S(1)}, f32[8,32,1280]{2,1,0:T(8,128)S(1)}, u32[]{:S(2)}, u32[]{:S(2)}) collective-permute-start(f32[8,32,1280]{2,1,0:T(8,128)S(1)} %get-tuple-element.43), channel_id=1, source_target_pairs={{0,4},{4,0},{1,5},{5,1},{2,6},{6,2},{3,7},{7,3},{8,12},{12,8},{9,1... | collective-permute-start | bytes 3932168 | tf_op jit(solution)/shard_map/ppermute | solution.py:163
  7.9 14.5 %collective-permute-start.3 = (f32[4,32,1280]{2,1,0:T(8,128)S(1)}, f32[4,32,1280]{2,1,0:T(8,128)S(1)}, u32[]{:S(2)}, u32[]{:S(2)}) collective-permute-start(f32[4,32,1280]{2,1,0:T(8,128)S(1)} %add.122), channel_id=1, source_target_pairs={{0,32},{4,228},{32,64},{36,4},{64,96},{68,36},{96,128},{100,68},{1... | collective-permute-start | bytes 1966088 | tf_op jit(solution)/shard_map/ppermute | solution.py:168
  16.2 6.4 %collective-permute-start.1 = (f32[8,32,768]{2,1,0:T(8,128)S(1)}, f32[8,32,768]{2,1,0:T(8,128)S(1)}, u32[]{:S(2)}, u32[]{:S(2)}) collective-permute-start(f32[8,32,768]{2,1,0:T(8,128)S(1)} %get-tuple-element.42), channel_id=1, source_target_pairs={{0,4},{4,0},{1,5},{5,1},{2,6},{6,2},{3,7},{7,3},{8,12},{12,8},{9,1... | collective-permute-start | bytes 2359304 | tf_op jit(solution)/shard_map/ppermute | solution.py:163
  22.7 13.4 %collective-permute-start.12 = (f32[24,32,768]{2,1,0:T(8,128)S(1)}, f32[24,32,768]{2,1,0:T(8,128)S(1)}, u32[]{:S(2)}, u32[]{:S(2)}) collective-permute-start(f32[24,32,768]{2,1,0:T(8,128)S(1)} %get-tuple-element.54), channel_id=1, source_target_pairs={{0,4},{4,0},{1,5},{5,1},{2,6},{6,2},{3,7},{7,3},{8,12},{12,8},{9,1... | collective-permute-start | bytes 7077896 | tf_op jit(solution)/shard_map/ppermute | solution.py:163
  22.8 13.3 %collective-permute-start.13 = (f32[8,32,768]{2,1,0:T(8,128)S(1)}, f32[8,32,768]{2,1,0:T(8,128)S(1)}, u32[]{:S(2)}, u32[]{:S(2)}) collective-permute-start(f32[8,32,768]{2,1,0:T(8,128)S(1)} %add.125), channel_id=1, source_target_pairs={{0,8},{4,28},{8,16},{12,4},{16,24},{20,12},{24,0},{28,20},{1,9},{5... | collective-permute-start | bytes 2359304 | tf_op jit(solution)/shard_map/ppermute | solution.py:168
  24.4 12.5 %collective-permute-start.5 = (f32[8,32,1280]{2,1,0:T(8,128)S(1)}, f32[8,32,1280]{2,1,0:T(8,128)S(1)}, u32[]{:S(2)}, u32[]{:S(2)}) collective-permute-start(f32[8,32,1280]{2,1,0:T(8,128)S(1)} %get-tuple-element.49), channel_id=1, source_target_pairs={{0,4},{4,0},{1,5},{5,1},{2,6},{6,2},{3,7},{7,3},{8,12},{12,8},{9,1... | collective-permute-start | bytes 3932168 | tf_op jit(solution)/shard_map/ppermute | solution.py:163
  25.8 18.8 %collective-permute-start.6 = (f32[8,32,1280]{2,1,0:T(8,128)S(1)}, f32[8,32,1280]{2,1,0:T(8,128)S(1)}, u32[]{:S(2)}, u32[]{:S(2)}) collective-permute-start(f32[8,32,1280]{2,1,0:T(8,128)S(1)} %pad_add_fusion), channel_id=1, source_target_pairs={{0,32},{4,228},{32,64},{36,4},{64,96},{68,36},{96,128},{100,68},{1... | collective-permute-start | bytes 3932168 | tf_op jit(solution)/shard_map/ppermute | solution.py:168
  28.9 16.1 %collective-permute-start.4 = (f32[12,32,1280]{2,1,0:T(8,128)S(1)}, f32[12,32,1280]{2,1,0:T(8,128)S(1)}, u32[]{:S(2)}, u32[]{:S(2)}) collective-permute-start(f32[12,32,1280]{2,1,0:T(8,128)S(1)} %get-tuple-element.48), channel_id=1, source_target_pairs={{0,4},{4,0},{1,5},{5,1},{2,6},{6,2},{3,7},{7,3},{8,12},{12,8},{9,1... | collective-permute-start | bytes 5898248 | tf_op jit(solution)/shard_map/ppermute | solution.py:163
  36.5 21.7 %collective-permute-start.14 = (f32[16,32,768]{2,1,0:T(8,128)S(1)}, f32[16,32,768]{2,1,0:T(8,128)S(1)}, u32[]{:S(2)}, u32[]{:S(2)}) collective-permute-start(f32[16,32,768]{2,1,0:T(8,128)S(1)} %slice_add_fusion), channel_id=1, source_target_pairs={{0,8},{4,28},{8,16},{12,4},{16,24},{20,12},{24,0},{28,20},{1,9},{5... | collective-permute-start | bytes 4718600 | tf_op jit(solution)/shard_map/ppermute | solution.py:168
  44.7 13.7 %collective-permute-start.7 = (f32[8,32,640]{2,1,0:T(8,128)S(1)}, f32[8,32,640]{2,1,0:T(8,128)S(1)}, u32[]{:S(2)}, u32[]{:S(2)}) collective-permute-start(f32[8,32,640]{2,1,0:T(8,128)S(1)} %get-tuple-element.65), channel_id=1, source_target_pairs={{0,32},{4,228},{32,64},{36,4},{64,96},{68,36},{96,128},{100,68},{1... | collective-permute-start | bytes 1966088 | tf_op jit(solution)/shard_map/ppermute | solution.py:168
  44.9 18.7 %collective-permute-start.10 = (f32[8,32,640]{2,1,0:T(8,128)S(1)}, f32[8,32,640]{2,1,0:T(8,128)S(1)}, u32[]{:S(2)}, u32[]{:S(2)}) collective-permute-start(f32[8,32,640]{2,1,0:T(8,128)S(1)} %slice_add_fusion.3), channel_id=1, source_target_pairs={{0,32},{4,228},{32,64},{36,4},{64,96},{68,36},{96,128},{100,68},{1... | collective-permute-start | bytes 1966088 | tf_op jit(solution)/shard_map/ppermute | solution.py:168
  58.3 5.5 %collective-permute-start.15 = (f32[8,32,768]{2,1,0:T(8,128)S(1)}, f32[8,32,768]{2,1,0:T(8,128)S(1)}, u32[]{:S(2)}, u32[]{:S(2)}) collective-permute-start(f32[8,32,768]{2,1,0:T(8,128)S(1)} %slice.94), channel_id=1, source_target_pairs={{0,4},{4,0},{1,5},{5,1},{2,6},{6,2},{3,7},{7,3},{8,12},{12,8},{9,1... | collective-permute-start | bytes 2359304 | tf_op jit(solution)/shard_map/ppermute | solution.py:163
  58.5 12.1 %collective-permute-start.8 = (f32[8,32,640]{2,1,0:T(8,128)S(1)}, f32[8,32,640]{2,1,0:T(8,128)S(1)}, u32[]{:S(2)}, u32[]{:S(2)}) collective-permute-start(f32[8,32,640]{2,1,0:T(8,128)S(1)} %slice_add_fusion.6), channel_id=1, source_target_pairs={{0,32},{4,228},{32,64},{36,4},{64,96},{68,36},{96,128},{100,68},{1... | collective-permute-start | bytes 1966088 | tf_op jit(solution)/shard_map/ppermute | solution.py:168
  63.7 14.0 %collective-permute-start.11 = (f32[8,32,640]{2,1,0:T(8,128)S(1)}, f32[8,32,640]{2,1,0:T(8,128)S(1)}, u32[]{:S(2)}, u32[]{:S(2)}) collective-permute-start(f32[8,32,640]{2,1,0:T(8,128)S(1)} %slice_add_fusion.4), channel_id=1, source_target_pairs={{0,32},{4,228},{32,64},{36,4},{64,96},{68,36},{96,128},{100,68},{1... | collective-permute-start | bytes 1966088 | tf_op jit(solution)/shard_map/ppermute | solution.py:168
  64.0 14.7 %collective-permute-start.16 = (f32[1,32,768]{2,1,0:T(8,128)S(1)}, f32[1,32,768]{2,1,0:T(8,128)S(1)}, u32[]{:S(2)}, u32[]{:S(2)}) collective-permute-start(f32[1,32,768]{2,1,0:T(8,128)S(1)} %slice.122), channel_id=1, source_target_pairs={{0,32},{4,228},{32,64},{36,4},{64,96},{68,36},{96,128},{100,68},{1... | collective-permute-start | bytes 294920 | tf_op jit(solution)/shard_map/ppermute | solution.py:168
  70.7 8.2 %collective-permute-start.9 = (f32[4,32,640]{2,1,0:T(8,128)S(1)}, f32[4,32,640]{2,1,0:T(8,128)S(1)}, u32[]{:S(2)}, u32[]{:S(2)}) collective-permute-start(f32[4,32,640]{2,1,0:T(8,128)S(1)} %slice.116), channel_id=1, source_target_pairs={{0,4},{4,0},{1,5},{5,1},{2,6},{6,2},{3,7},{7,3},{8,12},{12,8},{9,1... | collective-permute-start | bytes 983048 | tf_op jit(solution)/shard_map/ppermute | solution.py:163
  78.9 7.0 %collective-permute-start.21 = (f32[2,32,768]{2,1,0:T(8,128)S(1)}, f32[2,32,768]{2,1,0:T(8,128)S(1)}, u32[]{:S(2)}, u32[]{:S(2)}) collective-permute-start(f32[2,32,768]{2,1,0:T(8,128)S(1)} %slice_add_fusion.11), channel_id=1, source_target_pairs={{0,32},{4,228},{32,64},{36,4},{64,96},{68,36},{96,128},{100,68},{1... | collective-permute-start | bytes 589832 | tf_op jit(solution)/shard_map/ppermute | solution.py:168
  80.7 8.6 %collective-permute-start.19 = (f32[32,1280]{1,0:T(8,128)S(1)}, f32[32,1280]{1,0:T(8,128)S(1)}, u32[]{:S(2)}, u32[]{:S(2)}) collective-permute-start(f32[32,1280]{1,0:T(8,128)S(1)} %get-tuple-element.67), channel_id=1, source_target_pairs={{0,16},{8,24},{16,0},{24,8},{1,17},{9,25},{17,1},{25,9},{2,18},{10... | collective-permute-start | bytes 491528 | tf_op jit(solution)/shard_map/ppermute | solution.py:173
  82.1 8.5 %collective-permute-start.20 = (f32[32,1280]{1,0:T(8,128)S(1)}, f32[32,1280]{1,0:T(8,128)S(1)}, u32[]{:S(2)}, u32[]{:S(2)}) collective-permute-start(f32[32,1280]{1,0:T(8,128)S(1)} %get-tuple-element.68), channel_id=1, source_target_pairs={{0,24},{8,0},{16,8},{24,16},{1,25},{9,1},{17,9},{25,17},{2,26},{10... | collective-permute-start | bytes 491528 | tf_op jit(solution)/shard_map/ppermute | solution.py:173
  83.5 8.5 %collective-permute-start.18 = (f32[32,1280]{1,0:T(8,128)S(1)}, f32[32,1280]{1,0:T(8,128)S(1)}, u32[]{:S(2)}, u32[]{:S(2)}) collective-permute-start(f32[32,1280]{1,0:T(8,128)S(1)} %get-tuple-element.69), channel_id=1, source_target_pairs={{0,8},{8,16},{16,24},{24,0},{1,9},{9,17},{17,25},{25,1},{2,10},{10... | collective-permute-start | bytes 491528 | tf_op jit(solution)/shard_map/ppermute | solution.py:173
  86.0 7.0 %collective-permute-start.22 = (f32[2,32,768]{2,1,0:T(8,128)S(1)}, f32[2,32,768]{2,1,0:T(8,128)S(1)}, u32[]{:S(2)}, u32[]{:S(2)}) collective-permute-start(f32[2,32,768]{2,1,0:T(8,128)S(1)} %slice_add_fusion.9), channel_id=1, source_target_pairs={{0,32},{4,228},{32,64},{36,4},{64,96},{68,36},{96,128},{100,68},{1... | collective-permute-start | bytes 589832 | tf_op jit(solution)/shard_map/ppermute | solution.py:168
  93.0 4.1 %collective-permute-start.24 = (f32[1,32,768]{2,1,0:T(8,128)S(1)}, f32[1,32,768]{2,1,0:T(8,128)S(1)}, u32[]{:S(2)}, u32[]{:S(2)}) collective-permute-start(f32[1,32,768]{2,1,0:T(8,128)S(1)} %get-tuple-element.71), channel_id=1, source_target_pairs={{0,36},{4,224},{32,68},{36,0},{64,100},{68,32},{96,132},{100,64},{... | collective-permute-start | bytes 294920 | tf_op jit(solution)/shard_map/ppermute | solution.py:179
  93.1 5.9 %collective-permute-start.23 = (f32[1,32,768]{2,1,0:T(8,128)S(1)}, f32[1,32,768]{2,1,0:T(8,128)S(1)}, u32[]{:S(2)}, u32[]{:S(2)}) collective-permute-start(f32[1,32,768]{2,1,0:T(8,128)S(1)} %get-tuple-element.72), channel_id=1, source_target_pairs={{0,32},{4,228},{32,64},{36,4},{64,96},{68,36},{96,128},{100,68},{1... | collective-permute-start | bytes 294920 | tf_op jit(solution)/shard_map/ppermute | solution.py:168
  (5 other events, 139.8 us)

commit v9 on v8

--- a/solution.py
+++ b/solution.py
@@ -234,15 +234,13 @@
     pair1 = product_z(after(where, pair2[0], first_x), (1, 0))
     pair1 = (pair1[0], other_core(pair1[1]))
 
-    next_z = onward(next_z, "z")
+    x = after(onward(first_x, "x"), pair1[0])
+    x = add(both(pair_x)[:16], x)
+    next_z = after(onward(next_z, "z"), x)
     z = [next_z[..., cut] for cut in cuts]
-    steps = []
     for pair in (pair2, pair1):
-        steps.append(hop_z(pair, z))
-        z = [onward(part, "z") for part in steps[-1]]
-    x = after(onward(first_x, "x"), pair1[0])
-    x = after(onward(add(both(pair_x)[:16], x), "x"), steps[0][1])
-    sum_x = x[:8] + other_core(x[8:]) + both(pair_x)[16:24]
+        z = [onward(part, "z") for part in hop_z(pair, z)]
+    sum_x = onward_apart(x, "x") + both(pair_x)[16:24]
 
     moving = onward(sum_x[6:7], "z")
     far = [other_core(z[0][4:])]

time: 137 us -> 136 us (level)
  waiting for transfers between devices: 61.1 us -> 52.7 us
  starting transfers between devices: 16.4 us -> 22.3 us
  blocking collectives: 34.6 us -> 36.3 us
    ppermute x12, waiting for transfers between devices: 49.7 us -> 40.9 us  [onward(): lax.ppermute(value, (axis, 'c'), [(2 * i + c, 2 * ((i + 1 - 2 * c) % n) +...]
    ppermute x12, starting transfers between devices: 4.56 us -> 9.7 us  [onward(): lax.ppermute(value, (axis, 'c'), [(2 * i + c, 2 * ((i + 1 - 2 * c) % n) +...]
    ppermute x3, starting transfers between devices: 3.44 us -> 5.14 us  [shift(): return lax.ppermute(value, axis, [(i, (i + by) % n) for i in range(n)])]
    all_to_all x2, blocking collectives: 25.4 us -> 27.1 us  [sum_over(): return jnp.sum(lax.all_to_all(copies, axes, 0, 0, tiled=True), axis=0)]
    ppermute x9 -> x8, starting transfers between devices: 8.26 us -> 7.15 us  [other_core(): return lax.ppermute(value, 'c', [(0, 1), (1, 0)])]
    ppermute x1 -> x2, waiting for transfers between devices: 3.94 us -> 3.94 us  [onward_apart(): lax.ppermute(value[half:], (axis, 'c'), cross)]
  transfers between devices with their start and end apart: 25 -> 25, of which waited for: 16 -> 15; matrix products, arithmetic and copies ran while one was open for 2% -> 2% of each run, Pallas kernels for 10% -> 10%
where the time goes in v9:
time: 136 us
  waiting for transfers between devices  52.7 us (39%)
  blocking collectives  36.3 us (27%)
  starting transfers between devices  22.3 us (16%)
  Pallas kernels  18.2 us (13%)
  other arithmetic  4.8 us (4%)
  between operations  1.69 us (1%)
    ppermute x12, waiting for transfers between devices, onward(): lax.ppermute(value, (axis, 'c'), [(2 * i + c, 2 * ((i + 1 - 2 * c) % n) +...  40.9 us
    all_to_all x2, blocking collectives, sum_over(): return jnp.sum(lax.all_to_all(copies, axes, 0, 0, tiled=True), axis=0)  27.1 us
    pallas_call x4, Pallas kernels, product(): pl.pallas_call(kernel, in_specs=[pl.BlockSpec(memory_space=pltpu.SMEM), V...  14.1 us
    ppermute x12, starting transfers between devices, onward(): lax.ppermute(value, (axis, 'c'), [(2 * i + c, 2 * ((i + 1 - 2 * c) % n) +...  9.7 us
    psum x1, blocking collectives, shards(): norms = jnp.sqrt(lax.psum(squares, 'y'))  9.19 us
    ppermute x8, starting transfers between devices, other_core(): return lax.ppermute(value, 'c', [(0, 1), (1, 0)])  7.15 us
    ppermute x3, waiting for transfers between devices, shift(): return lax.ppermute(value, axis, [(i, (i + by) % n) for i in range(n)])  6.33 us
    ppermute x3, starting transfers between devices, shift(): return lax.ppermute(value, axis, [(i, (i + by) % n) for i in range(n)])  5.14 us
  transfers between devices with their start and end apart: 25, of which 15 were waited for; matrix products, arithmetic and copies ran while one was open for 2% of the time, Pallas kernels for 10%

profile of v9, /device:TPU:8, one launch (start us, length us, event | category | flops | bytes accessed | tf_op | source)
XLA Modules:
  0.0 136.2 jit_solution(16620291942433208841)
XLA Ops:
  0.7 4.1 %shard_map.85 = (bf16[1024,2048]{1,0:T(8,128)(2,1)S(1)}, bf16[1024,2048]{1,0:T(8,128)(2,1)S(1)}, f32[4,32,1280]{2,1,0:T(8,128)S(1)}, f32[4,32,1280]{2,1,0:T(8,128)S(1)}) custom-call(s32[3]{0:T(128)S(1)} %pad_add_fusion.1.where_ref, bf16[1024,2048]{1,0:T(8,128)(2,1)} %lhs_hbm.1, bf16[1024,2048]{1,0:T(8,128)(2,1)} %rhs_hbm.1), custom_call_target="tpu_custom_call" | custom-call | flops 327680 | bytes 256 | tf_op jit(solution)/shard_map/pallas_call | solution.py:141
  4.9 2.3 %shard_map.86 = (f32[8,32,1280]{2,1,0:T(8,128)S(1)}, f32[8,32,1280]{2,1,0:T(8,128)S(1)}) custom-call(s32[3]{0:T(128)S(1)} %pad_add_fusion.1.where_ref, bf16[1024,2048]{1,0:T(8,128)(2,1)S(1)} %get-tuple-element.34.lhs_ref, bf16[1024,2048]{1,0:T(8,128)(2,1)S(1)} %get-tuple-element.35.rhs_ref), custom_call_target="tpu_custom_call" | custom-call | flops 655360 | bytes 512 | tf_op jit(solution)/shard_map/pallas_call | solution.py:128
  7.9 2.0 %collective-permute-start.3 = (f32[4,32,1280]{2,1,0:T(8,128)S(1)}, f32[4,32,1280]{2,1,0:T(8,128)S(1)}, u32[]{:S(2)}, u32[]{:S(2)}) collective-permute-start(f32[4,32,1280]{2,1,0:T(8,128)S(1)} %add.122), channel_id=1, source_target_pairs={{0,32},{4,228},{32,64},{36,4},{64,96},{68,36},{96,128},{100,68},{1... | collective-permute-start | bytes 1966088 | tf_op jit(solution)/shard_map/ppermute | solution.py:168
  9.8 6.3 %shard_map.87 = (f32[8,32,768]{2,1,0:T(8,128)S(1)}, f32[8,32,768]{2,1,0:T(8,128)S(1)}, f32[24,32,768]{2,1,0:T(8,128)S(1)}, f32[24,32,768]{2,1,0:T(8,128)S(1)}) custom-call(s32[3]{0:T(128)S(1)} %pad_add_fusion.1.where_ref, bf16[1024,2048]{1,0:T(8,128)(2,1)S(1)} %get-tuple-element.34.lhs_ref, bf16[1024,2048]{1,0:T(8,128)(2,1)S(1)} %get-tuple-element.35.rhs_ref), custom_call_target="tpu_custom_call" | custom-call | flops 1572864 | bytes 2048 | tf_op jit(solution)/shard_map/pallas_call | solution.py:128
  16.2 3.8 %collective-permute-start.1 = (f32[8,32,768]{2,1,0:T(8,128)S(1)}, f32[8,32,768]{2,1,0:T(8,128)S(1)}, u32[]{:S(2)}, u32[]{:S(2)}) collective-permute-start(f32[8,32,768]{2,1,0:T(8,128)S(1)} %get-tuple-element.42), channel_id=1, source_target_pairs={{0,4},{4,0},{1,5},{5,1},{2,6},{6,2},{3,7},{7,3},{8,12},{12,8},{9,1... | collective-permute-start | bytes 2359304 | tf_op jit(solution)/shard_map/ppermute | solution.py:163
  20.0 2.3 %shard_map.88 = (f32[8,32,1280]{2,1,0:T(8,128)S(1)}, f32[8,32,1280]{2,1,0:T(8,128)S(1)}) custom-call(s32[3]{0:T(128)S(1)} %pad_add_fusion.1.where_ref, bf16[1024,2048]{1,0:T(8,128)(2,1)S(1)} %get-tuple-element.34.lhs_ref, bf16[1024,2048]{1,0:T(8,128)(2,1)S(1)} %get-tuple-element.35.rhs_ref), custom_call_target="tpu_custom_call" | custom-call | flops 655360 | bytes 512 | tf_op jit(solution)/shard_map/pallas_call | solution.py:128
  23.3 3.1 %shard_map.89 = (f32[12,32,1280]{2,1,0:T(8,128)S(1)}, f32[12,32,1280]{2,1,0:T(8,128)S(1)}) custom-call(s32[3]{0:T(128)S(1)} %pad_add_fusion.1.where_ref, bf16[1024,2048]{1,0:T(8,128)(2,1)S(1)} %get-tuple-element.34.lhs_ref, bf16[1024,2048]{1,0:T(8,128)(2,1)S(1)} %get-tuple-element.35.rhs_ref), custom_call_target="tpu_custom_call" | custom-call | flops 983040 | bytes 768 | tf_op jit(solution)/shard_map/pallas_call | solution.py:128
  26.4 1.9 %collective-permute-start.4 = (f32[12,32,1280]{2,1,0:T(8,128)S(1)}, f32[12,32,1280]{2,1,0:T(8,128)S(1)}, u32[]{:S(2)}, u32[]{:S(2)}) collective-permute-start(f32[12,32,1280]{2,1,0:T(8,128)S(1)} %get-tuple-element.48), channel_id=1, source_target_pairs={{0,4},{4,0},{1,5},{5,1},{2,6},{6,2},{3,7},{7,3},{8,12},{12,8},{9,1... | collective-permute-start | bytes 5898248 | tf_op jit(solution)/shard_map/ppermute | solution.py:163
  30.0 11.5 %collective-permute-done.8 = f32[8,32,768]{2,1,0:T(8,128)S(1)} collective-permute-done((f32[8,32,768]{2,1,0:T(8,128)S(1)}, f32[8,32,768]{2,1,0:T(8,128)S(1)}, u32[]{:S(2)}, u32[]{:S(2)}) %collective-permute-start.8) | collective-permute-done | bytes 786464 | tf_op jit(solution)/shard_map/ppermute | solution.py:168
  42.4 1.8 %collective-permute-start.12 = (f32[8,32,640]{2,1,0:T(8,128)S(1)}, f32[8,32,640]{2,1,0:T(8,128)S(1)}, u32[]{:S(2)}, u32[]{:S(2)}) collective-permute-start(f32[8,32,640]{2,1,0:T(8,128)S(1)} %slice_add_fusion.3), channel_id=1, source_target_pairs={{0,32},{4,228},{32,64},{36,4},{64,96},{68,36},{96,128},{100,68},{1... | collective-permute-start | bytes 1966088 | tf_op jit(solution)/shard_map/ppermute | solution.py:168
  44.8 1.5 %collective-permute-start.14 = (f32[8,32,768]{2,1,0:T(8,128)S(1)}, f32[8,32,768]{2,1,0:T(8,128)S(1)}, u32[]{:S(2)}, u32[]{:S(2)}) collective-permute-start(f32[8,32,768]{2,1,0:T(8,128)S(1)} %get-tuple-element.66), channel_id=1, source_target_pairs={{0,8},{4,28},{8,16},{12,4},{16,24},{20,12},{24,0},{28,20},{1,9},{5... | collective-permute-start | bytes 2359304 | tf_op jit(solution)/shard_map/ppermute | solution.py:168
  46.3 7.8 %collective-permute-done.9 = f32[8,32,640]{2,1,0:T(8,128)S(1)} collective-permute-done((f32[8,32,640]{2,1,0:T(8,128)S(1)}, f32[8,32,640]{2,1,0:T(8,128)S(1)}, u32[]{:S(2)}, u32[]{:S(2)}) %collective-permute-start.9) | collective-permute-done | bytes 655392 | tf_op jit(solution)/shard_map/ppermute | solution.py:168
  54.3 6.8 %collective-permute-done.12 = f32[8,32,640]{2,1,0:T(8,128)S(1)} collective-permute-done((f32[8,32,640]{2,1,0:T(8,128)S(1)}, f32[8,32,640]{2,1,0:T(8,128)S(1)}, u32[]{:S(2)}, u32[]{:S(2)}) %collective-permute-start.12) | collective-permute-done | bytes 655392 | tf_op jit(solution)/shard_map/ppermute | solution.py:168
  61.3 3.8 %collective-permute-done.14 = f32[8,32,768]{2,1,0:T(8,128)S(1)} collective-permute-done((f32[8,32,768]{2,1,0:T(8,128)S(1)}, f32[8,32,768]{2,1,0:T(8,128)S(1)}, u32[]{:S(2)}, u32[]{:S(2)}) %collective-permute-start.14) | collective-permute-done | bytes 786464 | tf_op jit(solution)/shard_map/ppermute | solution.py:168
  65.4 2.4 %collective-permute-start.16 = (f32[1,32,768]{2,1,0:T(8,128)S(1)}, f32[1,32,768]{2,1,0:T(8,128)S(1)}, u32[]{:S(2)}, u32[]{:S(2)}) collective-permute-start(f32[1,32,768]{2,1,0:T(8,128)S(1)} %slice.122), channel_id=1, source_target_pairs={{0,32},{4,228},{32,64},{36,4},{64,96},{68,36},{96,128},{100,68},{1... | collective-permute-start | bytes 294920 | tf_op jit(solution)/shard_map/ppermute | solution.py:168
  68.3 7.9 %collective-permute-done.16 = f32[1,32,768]{2,1,0:T(8,128)S(1)} collective-permute-done((f32[1,32,768]{2,1,0:T(8,128)S(1)}, f32[1,32,768]{2,1,0:T(8,128)S(1)}, u32[]{:S(2)}, u32[]{:S(2)}) %collective-permute-start.16) | collective-permute-done | bytes 98336 | tf_op jit(solution)/shard_map/ppermute | solution.py:168
  78.2 3.1 %collective-permute-start.19 = (f32[32,1280]{1,0:T(8,128)S(1)}, f32[32,1280]{1,0:T(8,128)S(1)}, u32[]{:S(2)}, u32[]{:S(2)}) collective-permute-start(f32[32,1280]{1,0:T(8,128)S(1)} %get-tuple-element.69), channel_id=1, source_target_pairs={{0,16},{8,24},{16,0},{24,8},{1,17},{9,25},{17,1},{25,9},{2,18},{10... | collective-permute-start | bytes 491528 | tf_op jit(solution)/shard_map/ppermute | solution.py:173
  83.5 3.3 %collective-permute-done.19 = f32[32,1280]{1,0:T(8,128)S(1)} collective-permute-done((f32[32,1280]{1,0:T(8,128)S(1)}, f32[32,1280]{1,0:T(8,128)S(1)}, u32[]{:S(2)}, u32[]{:S(2)}) %collective-permute-start.19) | collective-permute-done | bytes 163872 | tf_op jit(solution)/shard_map/ppermute | solution.py:173
  86.8 2.8 %collective-permute-done.20 = f32[32,1280]{1,0:T(8,128)S(1)} collective-permute-done((f32[32,1280]{1,0:T(8,128)S(1)}, f32[32,1280]{1,0:T(8,128)S(1)}, u32[]{:S(2)}, u32[]{:S(2)}) %collective-permute-start.20) | collective-permute-done | bytes 163872 | tf_op jit(solution)/shard_map/ppermute | solution.py:173
  90.6 3.9 %collective-permute-done.24 = f32[1,32,768]{2,1,0:T(8,128)S(1)} collective-permute-done((f32[1,32,768]{2,1,0:T(8,128)S(1)}, f32[1,32,768]{2,1,0:T(8,128)S(1)}, u32[]{:S(2)}, u32[]{:S(2)}) %collective-permute-start.24) | collective-permute-done | bytes 98336 | tf_op jit(solution)/shard_map/ppermute | solution.py:179
  94.5 1.9 %collective-permute-done.23 = f32[1,32,768]{2,1,0:T(8,128)S(1)} collective-permute-done((f32[1,32,768]{2,1,0:T(8,128)S(1)}, f32[1,32,768]{2,1,0:T(8,128)S(1)}, u32[]{:S(2)}, u32[]{:S(2)}) %collective-permute-start.23) | collective-permute-done | bytes 98336 | tf_op jit(solution)/shard_map/ppermute | solution.py:168
  96.5 13.6 %all_to_all.10 = f32[16,8,128]{2,1,0:T(8,128)S(1)} all-to-all(f32[16,8,128]{2,1,0:T(8,128)S(1)} %broadcast_in_dim.4), channel_id=1, replica_groups=mesh['z'=8,'x'=4,'c'=2,'y'=4] {'z','c'}, dimensions={0} | all-to-all | bytes 131072 | tf_op jit(solution)/shard_map/all_to_all | solution.py:188
  110.2 13.5 %all_to_all.11 = f32[16,8,128]{2,1,0:T(8,128)S(1)} all-to-all(f32[16,8,128]{2,1,0:T(8,128)S(1)} %broadcast_in_dim.5), channel_id=1, replica_groups=mesh['z'=8,'x'=4,'c'=2,'y'=4] {'x','y'}, dimensions={0} | all-to-all | bytes 131072 | tf_op jit(solution)/shard_map/all_to_all | solution.py:188
  126.1 9.2 %psum.7 = f32[2,32]{1,0:T(2,128)S(1)} all-reduce(f32[2,32]{1,0:T(2,128)S(1)} %pad_maximum_fusion), channel_id=1, replica_groups=mesh['z'=8,'x'=4,'c'=2,'y'=4] {'y'}, use_global_device_ids=true, to_apply=%region_5.0 | all-reduce | flops 64 | bytes 512 | tf_op jit(solution)/shard_map/psum | solution.py:265
  (79 shorter events, 13.5 us)
Async XLA Ops:
  4.8 3.0 %collective-permute-start = (f32[4,32,1280]{2,1,0:T(8,128)S(1)}, f32[4,32,1280]{2,1,0:T(8,128)S(1)}, u32[]{:S(2)}, u32[]{:S(2)}) collective-permute-start(f32[4,32,1280]{2,1,0:T(8,128)S(1)} %get-tuple-element.37), channel_id=1, source_target_pairs={{0,4},{4,0},{1,5},{5,1},{2,6},{6,2},{3,7},{7,3},{8,12},{12,8},{9,1... | collective-permute-start | bytes 1966088 | tf_op jit(solution)/shard_map/ppermute | solution.py:163
  7.2 15.2 %collective-permute-start.2 = (f32[8,32,1280]{2,1,0:T(8,128)S(1)}, f32[8,32,1280]{2,1,0:T(8,128)S(1)}, u32[]{:S(2)}, u32[]{:S(2)}) collective-permute-start(f32[8,32,1280]{2,1,0:T(8,128)S(1)} %get-tuple-element.43), channel_id=1, source_target_pairs={{0,4},{4,0},{1,5},{5,1},{2,6},{6,2},{3,7},{7,3},{8,12},{12,8},{9,1... | collective-permute-start | bytes 3932168 | tf_op jit(solution)/shard_map/ppermute | solution.py:163
  7.9 14.5 %collective-permute-start.3 = (f32[4,32,1280]{2,1,0:T(8,128)S(1)}, f32[4,32,1280]{2,1,0:T(8,128)S(1)}, u32[]{:S(2)}, u32[]{:S(2)}) collective-permute-start(f32[4,32,1280]{2,1,0:T(8,128)S(1)} %add.122), channel_id=1, source_target_pairs={{0,32},{4,228},{32,64},{36,4},{64,96},{68,36},{96,128},{100,68},{1... | collective-permute-start | bytes 1966088 | tf_op jit(solution)/shard_map/ppermute | solution.py:168
  16.2 6.4 %collective-permute-start.1 = (f32[8,32,768]{2,1,0:T(8,128)S(1)}, f32[8,32,768]{2,1,0:T(8,128)S(1)}, u32[]{:S(2)}, u32[]{:S(2)}) collective-permute-start(f32[8,32,768]{2,1,0:T(8,128)S(1)} %get-tuple-element.42), channel_id=1, source_target_pairs={{0,4},{4,0},{1,5},{5,1},{2,6},{6,2},{3,7},{7,3},{8,12},{12,8},{9,1... | collective-permute-start | bytes 2359304 | tf_op jit(solution)/shard_map/ppermute | solution.py:163
  22.7 18.9 %collective-permute-start.7 = (f32[24,32,768]{2,1,0:T(8,128)S(1)}, f32[24,32,768]{2,1,0:T(8,128)S(1)}, u32[]{:S(2)}, u32[]{:S(2)}) collective-permute-start(f32[24,32,768]{2,1,0:T(8,128)S(1)} %get-tuple-element.52), channel_id=1, source_target_pairs={{0,4},{4,0},{1,5},{5,1},{2,6},{6,2},{3,7},{7,3},{8,12},{12,8},{9,1... | collective-permute-start | bytes 7077896 | tf_op jit(solution)/shard_map/ppermute | solution.py:163
  22.8 7.1 %collective-permute-start.5 = (f32[8,32,1280]{2,1,0:T(8,128)S(1)}, f32[8,32,1280]{2,1,0:T(8,128)S(1)}, u32[]{:S(2)}, u32[]{:S(2)}) collective-permute-start(f32[8,32,1280]{2,1,0:T(8,128)S(1)} %get-tuple-element.49), channel_id=1, source_target_pairs={{0,4},{4,0},{1,5},{5,1},{2,6},{6,2},{3,7},{7,3},{8,12},{12,8},{9,1... | collective-permute-start | bytes 3932168 | tf_op jit(solution)/shard_map/ppermute | solution.py:163
  23.3 18.8 %collective-permute-start.6 = (f32[8,32,1280]{2,1,0:T(8,128)S(1)}, f32[8,32,1280]{2,1,0:T(8,128)S(1)}, u32[]{:S(2)}, u32[]{:S(2)}) collective-permute-start(f32[8,32,1280]{2,1,0:T(8,128)S(1)} %pad_add_fusion), channel_id=1, source_target_pairs={{0,32},{4,228},{32,64},{36,4},{64,96},{68,36},{96,128},{100,68},{1... | collective-permute-start | bytes 3932168 | tf_op jit(solution)/shard_map/ppermute | solution.py:168
  26.4 17.8 %collective-permute-start.4 = (f32[12,32,1280]{2,1,0:T(8,128)S(1)}, f32[12,32,1280]{2,1,0:T(8,128)S(1)}, u32[]{:S(2)}, u32[]{:S(2)}) collective-permute-start(f32[12,32,1280]{2,1,0:T(8,128)S(1)} %get-tuple-element.48), channel_id=1, source_target_pairs={{0,4},{4,0},{1,5},{5,1},{2,6},{6,2},{3,7},{7,3},{8,12},{12,8},{9,1... | collective-permute-start | bytes 5898248 | tf_op jit(solution)/shard_map/ppermute | solution.py:163
  28.4 13.2 %collective-permute-start.8 = (f32[8,32,768]{2,1,0:T(8,128)S(1)}, f32[8,32,768]{2,1,0:T(8,128)S(1)}, u32[]{:S(2)}, u32[]{:S(2)}) collective-permute-start(f32[8,32,768]{2,1,0:T(8,128)S(1)} %add.125), channel_id=1, source_target_pairs={{0,8},{4,28},{8,16},{12,4},{16,24},{20,12},{24,0},{28,20},{1,9},{5... | collective-permute-start | bytes 2359304 | tf_op jit(solution)/shard_map/ppermute | solution.py:168
  42.2 11.9 %collective-permute-start.9 = (f32[8,32,640]{2,1,0:T(8,128)S(1)}, f32[8,32,640]{2,1,0:T(8,128)S(1)}, u32[]{:S(2)}, u32[]{:S(2)}) collective-permute-start(f32[8,32,640]{2,1,0:T(8,128)S(1)} %get-tuple-element.67), channel_id=1, source_target_pairs={{0,32},{4,228},{32,64},{36,4},{64,96},{68,36},{96,128},{100,68},{1... | collective-permute-start | bytes 1966088 | tf_op jit(solution)/shard_map/ppermute | solution.py:168
  42.4 18.7 %collective-permute-start.12 = (f32[8,32,640]{2,1,0:T(8,128)S(1)}, f32[8,32,640]{2,1,0:T(8,128)S(1)}, u32[]{:S(2)}, u32[]{:S(2)}) collective-permute-start(f32[8,32,640]{2,1,0:T(8,128)S(1)} %slice_add_fusion.3), channel_id=1, source_target_pairs={{0,32},{4,228},{32,64},{36,4},{64,96},{68,36},{96,128},{100,68},{1... | collective-permute-start | bytes 1966088 | tf_op jit(solution)/shard_map/ppermute | solution.py:168
  44.6 16.7 %collective-permute-start.15 = (f32[8,32,768]{2,1,0:T(8,128)S(1)}, f32[8,32,768]{2,1,0:T(8,128)S(1)}, u32[]{:S(2)}, u32[]{:S(2)}) collective-permute-start(f32[8,32,768]{2,1,0:T(8,128)S(1)} %get-tuple-element.65), channel_id=1, source_target_pairs={{0,12},{4,24},{8,20},{12,0},{16,28},{20,8},{24,4},{28,16},{1,13},{... | collective-permute-start | bytes 2359304 | tf_op jit(solution)/shard_map/ppermute | solution.py:179
  44.8 20.4 %collective-permute-start.14 = (f32[8,32,768]{2,1,0:T(8,128)S(1)}, f32[8,32,768]{2,1,0:T(8,128)S(1)}, u32[]{:S(2)}, u32[]{:S(2)}) collective-permute-start(f32[8,32,768]{2,1,0:T(8,128)S(1)} %get-tuple-element.66), channel_id=1, source_target_pairs={{0,8},{4,28},{8,16},{12,4},{16,24},{20,12},{24,0},{28,20},{1,9},{5... | collective-permute-start | bytes 2359304 | tf_op jit(solution)/shard_map/ppermute | solution.py:168
  54.2 14.0 %collective-permute-start.10 = (f32[8,32,640]{2,1,0:T(8,128)S(1)}, f32[8,32,640]{2,1,0:T(8,128)S(1)}, u32[]{:S(2)}, u32[]{:S(2)}) collective-permute-start(f32[8,32,640]{2,1,0:T(8,128)S(1)} %slice_add_fusion.6), channel_id=1, source_target_pairs={{0,32},{4,228},{32,64},{36,4},{64,96},{68,36},{96,128},{100,68},{1... | collective-permute-start | bytes 1966088 | tf_op jit(solution)/shard_map/ppermute | solution.py:168
  61.2 15.0 %collective-permute-start.13 = (f32[8,32,640]{2,1,0:T(8,128)S(1)}, f32[8,32,640]{2,1,0:T(8,128)S(1)}, u32[]{:S(2)}, u32[]{:S(2)}) collective-permute-start(f32[8,32,640]{2,1,0:T(8,128)S(1)} %slice_add_fusion.4), channel_id=1, source_target_pairs={{0,32},{4,228},{32,64},{36,4},{64,96},{68,36},{96,128},{100,68},{1... | collective-permute-start | bytes 1966088 | tf_op jit(solution)/shard_map/ppermute | solution.py:168
  65.4 10.9 %collective-permute-start.16 = (f32[1,32,768]{2,1,0:T(8,128)S(1)}, f32[1,32,768]{2,1,0:T(8,128)S(1)}, u32[]{:S(2)}, u32[]{:S(2)}) collective-permute-start(f32[1,32,768]{2,1,0:T(8,128)S(1)} %slice.122), channel_id=1, source_target_pairs={{0,32},{4,228},{32,64},{36,4},{64,96},{68,36},{96,128},{100,68},{1... | collective-permute-start | bytes 294920 | tf_op jit(solution)/shard_map/ppermute | solution.py:168
  68.2 8.3 %collective-permute-start.11 = (f32[4,32,640]{2,1,0:T(8,128)S(1)}, f32[4,32,640]{2,1,0:T(8,128)S(1)}, u32[]{:S(2)}, u32[]{:S(2)}) collective-permute-start(f32[4,32,640]{2,1,0:T(8,128)S(1)} %slice.116), channel_id=1, source_target_pairs={{0,4},{4,0},{1,5},{5,1},{2,6},{6,2},{3,7},{7,3},{8,12},{12,8},{9,1... | collective-permute-start | bytes 983048 | tf_op jit(solution)/shard_map/ppermute | solution.py:163
  76.4 7.0 %collective-permute-start.21 = (f32[2,32,768]{2,1,0:T(8,128)S(1)}, f32[2,32,768]{2,1,0:T(8,128)S(1)}, u32[]{:S(2)}, u32[]{:S(2)}) collective-permute-start(f32[2,32,768]{2,1,0:T(8,128)S(1)} %slice_add_fusion.11), channel_id=1, source_target_pairs={{0,32},{4,228},{32,64},{36,4},{64,96},{68,36},{96,128},{100,68},{1... | collective-permute-start | bytes 589832 | tf_op jit(solution)/shard_map/ppermute | solution.py:168
  78.2 8.6 %collective-permute-start.19 = (f32[32,1280]{1,0:T(8,128)S(1)}, f32[32,1280]{1,0:T(8,128)S(1)}, u32[]{:S(2)}, u32[]{:S(2)}) collective-permute-start(f32[32,1280]{1,0:T(8,128)S(1)} %get-tuple-element.69), channel_id=1, source_target_pairs={{0,16},{8,24},{16,0},{24,8},{1,17},{9,25},{17,1},{25,9},{2,18},{10... | collective-permute-start | bytes 491528 | tf_op jit(solution)/shard_map/ppermute | solution.py:173
  81.3 8.4 %collective-permute-start.20 = (f32[32,1280]{1,0:T(8,128)S(1)}, f32[32,1280]{1,0:T(8,128)S(1)}, u32[]{:S(2)}, u32[]{:S(2)}) collective-permute-start(f32[32,1280]{1,0:T(8,128)S(1)} %get-tuple-element.70), channel_id=1, source_target_pairs={{0,24},{8,0},{16,8},{24,16},{1,25},{9,1},{17,9},{25,17},{2,26},{10... | collective-permute-start | bytes 491528 | tf_op jit(solution)/shard_map/ppermute | solution.py:173
  82.4 7.4 %collective-permute-start.18 = (f32[32,1280]{1,0:T(8,128)S(1)}, f32[32,1280]{1,0:T(8,128)S(1)}, u32[]{:S(2)}, u32[]{:S(2)}) collective-permute-start(f32[32,1280]{1,0:T(8,128)S(1)} %get-tuple-element.71), channel_id=1, source_target_pairs={{0,8},{8,16},{16,24},{24,0},{1,9},{9,17},{17,25},{25,1},{2,10},{10... | collective-permute-start | bytes 491528 | tf_op jit(solution)/shard_map/ppermute | solution.py:173
  83.4 7.0 %collective-permute-start.22 = (f32[2,32,768]{2,1,0:T(8,128)S(1)}, f32[2,32,768]{2,1,0:T(8,128)S(1)}, u32[]{:S(2)}, u32[]{:S(2)}) collective-permute-start(f32[2,32,768]{2,1,0:T(8,128)S(1)} %slice_add_fusion.9), channel_id=1, source_target_pairs={{0,32},{4,228},{32,64},{36,4},{64,96},{68,36},{96,128},{100,68},{1... | collective-permute-start | bytes 589832 | tf_op jit(solution)/shard_map/ppermute | solution.py:168
  90.4 4.1 %collective-permute-start.24 = (f32[1,32,768]{2,1,0:T(8,128)S(1)}, f32[1,32,768]{2,1,0:T(8,128)S(1)}, u32[]{:S(2)}, u32[]{:S(2)}) collective-permute-start(f32[1,32,768]{2,1,0:T(8,128)S(1)} %get-tuple-element.73), channel_id=1, source_target_pairs={{0,36},{4,224},{32,68},{36,0},{64,100},{68,32},{96,132},{100,64},{... | collective-permute-start | bytes 294920 | tf_op jit(solution)/shard_map/ppermute | solution.py:179
  90.5 5.9 %collective-permute-start.23 = (f32[1,32,768]{2,1,0:T(8,128)S(1)}, f32[1,32,768]{2,1,0:T(8,128)S(1)}, u32[]{:S(2)}, u32[]{:S(2)}) collective-permute-start(f32[1,32,768]{2,1,0:T(8,128)S(1)} %get-tuple-element.74), channel_id=1, source_target_pairs={{0,32},{4,228},{32,64},{36,4},{64,96},{68,36},{96,128},{100,68},{1... | collective-permute-start | bytes 294920 | tf_op jit(solution)/shard_map/ppermute | solution.py:168
  (5 other events, 144.9 us)
